TPU v7x, 256 devices: a whole 4x4x8 slice. The times are simulated.
256 devices in a mesh: seq: 32 (over y, x, core), expert: 8 (over z).
Axes of the slice: x: 4, y: 4, z: 8, core: 2. Of those that a mesh axis runs over, the one named last changes fastest.
Arguments:
- layer_input: bfloat16 [2048, 2, 4096], P(('seq', 'expert')), may hold values from -6 to 6
- x_branch: bfloat16 [2048, 2, 4096], P('seq', None, 'expert'), may hold values from -24 to 24
- gate_branch: bfloat16 [2048, 2, 4096], P('seq', None, 'expert'), may hold values from -6 to 6
- conv_weight: bfloat16 [4, 4096], P(None, 'expert'), may hold values from -3 to 3
- conv_bias: bfloat16 [4096], P('expert'), may hold values from -3 to 3
- x_proj: bfloat16 [4096, 288], P('expert'), may hold values from -0.09375 to 0.09375
- dt_proj: bfloat16 [256, 4096], P(None, 'expert'), may hold values from -0.375 to 0.375
- dt_bias: float32 [4096], P('expert'), may hold values from -5.5 to -2
- a_log: float32 [4096, 16], P('expert'), may hold values from -7 to 2.77
- d_skip: float32 [4096], P('expert'), may hold values from 0.5 to 1.5
- carry_state: float32 [2, 4096, 16], P(None, 'expert'), may hold values from -3 to 3
- carry_tail: bfloat16 [3, 2, 4096], P(None, None, 'expert'), may hold values from -6 to 6
- out_proj: bfloat16 [4096, 4096], P('expert'), may hold values from -0.09375 to 0.09375
- steering: bfloat16 [4096], replicated, may hold values from -6 to 6
- refusal: bfloat16 [4, 4096], replicated, may hold values from -6 to 6
- norm_gain: bfloat16 [4096], replicated, may hold values from 0.5 to 1.5
- router: bfloat16 [4096, 8], replicated, may hold values from -0.09375 to 0.09375
- specialist_switch_matrix: bfloat16 [8, 4096, 8192], P('expert', None, 'seq'), may hold values from -0.09375 to 0.09375
- w_up: bfloat16 [8, 4096, 8192], P('expert', None, 'seq'), may hold values from -0.09375 to 0.09375
- w_down: bfloat16 [8, 8192, 4096], P('expert', 'seq'), may hold values from -0.0625 to 0.0625
- expert_ids: int32 [2048, 2, 2], P('seq'), may hold values from 0 to 7, all different within a row; in each aligned block of 128 rows (0 to 127, 128 to 255, ..., all dimensions but the last counted through in order) at most 40 rows name the same one
Outputs:
- layer_out: float32 [2048, 2, 4096], P(('seq', 'expert'))
Inputs may be any that keep to these rules, and one draw needn't show every extreme that they name: `expert_ids`: in every aligned block of 128 rows in position-major order (the tokens of one seq index), no expert is named by more than 40 tokens, and in some block an expert is named by exactly 40; the two experts of a token differ.
All inputs are finite; a program needn't handle non-finite values.
Results may differ from a plain program's by a relative error of at most 0.0044.
Values may be sent and summed in bfloat16 or wider, within the bound.
No kernel may reach another device: no remote copies, remote signals or barrier semaphores. Data moves between devices by JAX's collectives and lax.ppermute only.
A program may use at most 128 MiB of HBM per device.

v0:
```python
import functools

import jax
import jax.numpy as jnp
from jax import lax
from jax.experimental import pallas as pl
from jax.experimental.pallas import tpu as pltpu
from jax.sharding import PartitionSpec as P

EPS = 1e-06
LOG2E = 1.4426950408889634
F32 = jnp.float32
BF16 = jnp.bfloat16
WIDE = pltpu.CompilerParams(vmem_limit_bytes=40 * 1024 * 1024)


def silu(v):
    return v * jax.nn.sigmoid(v)


def dot(a, b):
    return jnp.dot(a, b, preferred_element_type=F32)


def exchanged(blocks, axis, groups=None):
    return lax.all_to_all(blocks, axis, 0, 0, tiled=True, axis_index_groups=groups)


def conv_kernel(lead_ref, x_ref, got_ref, carry_ref, w_ref, b_ref, xp_ref, act_ref, part_ref, pad_ref):
    rows = x_ref.shape[0]
    taps = w_ref.shape[0]
    halo = got_ref.shape[0]
    step = halo // (taps - 1)
    first = lead_ref[0] == 0
    pad_ref[:halo, :] = jnp.where(first, carry_ref[...].astype(F32), got_ref[...].astype(F32))
    pad_ref[halo : halo + rows, :] = x_ref[...].astype(F32)
    total = b_ref[...].astype(F32)
    w = w_ref[...].astype(F32)
    for k in range(taps):
        total = total + w[k : k + 1, :] * pad_ref[k * step : k * step + rows, :]
    act = silu(total)
    act_ref[...] = act
    part_ref[...] = dot(act.astype(BF16), xp_ref[...])


def advance(state, rate, step, drive, b):
    return jnp.exp2(step * rate) * state + drive * b


def local_kernel(prompts, proj_ref, dtp_ref, dtb_ref, act_ref, bc_ref, alog_ref, step_ref, out_ref):
    rows, channels = act_ref.shape
    states = alog_ref.shape[0]
    rank = dtp_ref.shape[0]
    low = proj_ref[:, :rank].astype(BF16)
    step_ref[...] = jax.nn.softplus(dot(low, dtp_ref[...]) + dtb_ref[...])
    rate = -jnp.exp(alog_ref[...]) * LOG2E

    def body(i, carried):
        carried = list(carried)
        at = pl.multiple_of(i * 8, 8)
        step = step_ref[pl.ds(at, 8), :]
        drive = step * act_ref[pl.ds(at, 8), :]
        for r in range(8):
            p = r % prompts
            b = jnp.tile(bc_ref[at + r, :states, :], (1, channels // 128))
            carried[p] = advance(carried[p], rate, step[r : r + 1, :], drive[r : r + 1, :], b)
        return tuple(carried)

    zero = jnp.zeros((states, channels), F32)
    ends = lax.fori_loop(0, rows // 8, body, (zero,) * prompts)
    for p in range(prompts):
        out_ref[p * states : (p + 1) * states, :] = ends[p].astype(BF16)
    step = step_ref[...].reshape(rows // 8, 8, channels).sum(axis=0)
    sums = [sum(step[r : r + 1, :] for r in range(p, 8, prompts)) for p in range(prompts)]
    high = [s.astype(BF16).astype(F32) for s in sums]
    low_part = [(s - h) for s, h in zip(sums, high)]
    rest = jnp.zeros((8 - 2 * prompts, channels), F32)
    out_ref[prompts * states :, :] = jnp.concatenate(high + low_part + [rest], axis=0).astype(BF16)


def scan_kernel(
    prompts, ids_ref, all_ref, carry_ref, step_ref, act_ref, bc_ref, alog_ref, skip_ref, gate_ref, own_ref,
    outp_ref, mixed_ref, y_ref, w_ref, sem,
):
    rows, channels = act_ref.shape
    states = alog_ref.shape[0]
    copy = pltpu.make_async_copy(outp_ref, w_ref, sem)
    copy.start()
    rate = -jnp.exp(alog_ref[...]) * LOG2E

    def earlier(j, carried):
        block = all_ref[j].astype(F32)
        at = prompts * states
        out = []
        for p in range(prompts):
            total = block[at + p : at + p + 1, :] + block[at + prompts + p : at + prompts + p + 1, :]
            out.append(jnp.exp2(total * rate) * carried[p] + block[p * states : (p + 1) * states, :])
        return tuple(out)

    entering = lax.fori_loop(0, ids_ref[0], earlier, tuple(carry_ref[p] for p in range(prompts)))

    def body(i, carried):
        carried = list(carried)
        at = pl.multiple_of(i * 8, 8)
        step = step_ref[pl.ds(at, 8), :]
        drive = step * act_ref[pl.ds(at, 8), :]
        outs = []
        for r in range(8):
            p = r % prompts
            bc = bc_ref[at + r]
            b = jnp.tile(bc[:states], (1, channels // 128))
            c = jnp.tile(bc[states:], (1, channels // 128))
            carried[p] = advance(carried[p], rate, step[r : r + 1, :], drive[r : r + 1, :], b)
            outs.append(jnp.sum(carried[p] * c, axis=0, keepdims=True))
        y_ref[pl.ds(at, 8), :] = jnp.concatenate(outs, axis=0)
        return tuple(carried)

    lax.fori_loop(0, rows // 8, body, entering)
    y = y_ref[...] + skip_ref[...] * act_ref[...]
    gated = (y * silu(gate_ref[...].astype(F32))).astype(BF16)
    copy.wait()
    blocks, _, width = mixed_ref.shape
    own_rows = own_ref.shape[0]
    row_group = lax.broadcasted_iota(jnp.int32, (rows, width), 0) // own_rows
    mine = row_group == ids_ref[1]
    for j in range(blocks):
        part = dot(gated, w_ref[:, j * width : (j + 1) * width])
        own = jnp.tile(own_ref[:, j * width : (j + 1) * width].astype(F32), (rows // own_rows, 1))
        mixed_ref[j] = (part + jnp.where(mine, own, 0.0)).astype(BF16)


def clean_kernel(steer_ref, refusal_ref, out_ref):
    vector = steer_ref[...].astype(F32)
    units = []
    for k in range(refusal_ref.shape[0]):
        r = refusal_ref[k].astype(F32)
        for q in units:
            r = r - jnp.sum(q * r) * q
        r = r * lax.rsqrt(jnp.sum(r * r) + EPS)
        units.append(r)
    for q in units:
        vector = vector - jnp.sum(q * vector) * q
    out_ref[...] = vector


def dispatch_kernel(mixed_ref, clean_ref, gain_ref, lanes_ref, res_ref, send_ref, slots_ref):
    experts, capacity, rows = slots_ref.shape
    width = res_ref.shape[1]
    residual = clean_ref[...]
    for j in range(mixed_ref.shape[0]):
        residual = residual + mixed_ref[j].astype(F32)
    res_ref[...] = residual
    scaled = (residual * gain_ref[...].astype(F32)).astype(BF16)
    square = jnp.sum(residual * residual, axis=1, keepdims=True)
    high = square.astype(BF16).astype(F32)
    middle = (square - high).astype(BF16).astype(F32)
    low = square - high - middle
    lane = lax.broadcasted_iota(jnp.int32, (rows, 128), 1)
    extra = jnp.where(lane == 0, high, jnp.where(lane == 1, middle, jnp.where(lane == 2, low, 0.0)))
    payload = jnp.concatenate([scaled, extra.astype(BF16)], axis=1)
    label = lax.broadcasted_iota(jnp.int32, (experts, rows), 0)
    member = (lanes_ref[0:1, :] == label) | (lanes_ref[1:2, :] == label)
    upper = lax.broadcasted_iota(jnp.int32, (rows, rows), 0) <= lax.broadcasted_iota(jnp.int32, (rows, rows), 1)
    order = dot(member.astype(F32).astype(BF16), upper.astype(F32).astype(BF16))
    place = jnp.where(member, order - 1.0, -1.0)
    slot = lax.broadcasted_iota(jnp.int32, (capacity, rows), 0).astype(F32)
    for e in range(experts):
        chosen = (place[e : e + 1, :] == slot).astype(F32).astype(BF16)
        slots_ref[e] = chosen
        send_ref[e] = dot(chosen, payload).astype(BF16)


def normed_kernel(features, got_ref, out_ref):
    width = out_ref.shape[1] // got_ref.shape[0]
    total = jnp.zeros((out_ref.shape[0], 128), F32)
    for j in range(got_ref.shape[0]):
        total = total + got_ref[j, :, width:].astype(F32)
    scale = lax.rsqrt(jnp.sum(total, axis=1, keepdims=True) / features + EPS)
    for j in range(got_ref.shape[0]):
        out_ref[:, j * width : (j + 1) * width] = (got_ref[j, :, :width].astype(F32) * scale).astype(BF16)


def share_kernel(owner_ref, x_ref, router_ref, slots_ref, rows_ref, out_ref):
    logits = lax.dot_general(x_ref[...], router_ref[...], (((1,), (1,)), ((), ())), preferred_element_type=F32)
    experts = router_ref.shape[0]
    rows = rows_ref.shape[0]
    label = lax.broadcasted_iota(jnp.int32, (rows, experts), 1)
    member = (rows_ref[:, 0:1] == label) | (rows_ref[:, 1:2] == label)
    both = dot(slots_ref[owner_ref[0]], member.astype(F32).astype(BF16))
    own = (lax.broadcasted_iota(jnp.int32, both.shape, 1) == owner_ref[0]).astype(F32) * both
    gap = jnp.sum(logits * (2.0 * own - both), axis=1, keepdims=True)
    out_ref[...] = jnp.broadcast_to(jax.nn.sigmoid(gap), out_ref.shape)


def weigh_kernel(got_ref, share_ref, out_ref):
    total = got_ref[0].astype(F32)
    for i in range(1, got_ref.shape[0]):
        total = total + got_ref[i].astype(F32)
    out_ref[0] = (total * share_ref[:, :1]).astype(BF16)


def combine_kernel(res_ref, got_ref, slots_ref, out_ref):
    total = res_ref[...]
    for e in range(got_ref.shape[0]):
        total = total + lax.dot_general(
            slots_ref[e], got_ref[e], (((0,), (0,)), ((), ())), preferred_element_type=F32
        )
    out_ref[...] = total


def shape(dims, dtype=F32):
    return jax.ShapeDtypeStruct(dims, dtype)


SCALAR = pl.BlockSpec(memory_space=pltpu.SMEM)
VM = pl.BlockSpec(memory_space=pltpu.VMEM)


def call(kernel, outs, specs, scratch=(), name=None):
    return pl.pallas_call(
        kernel, out_shape=outs, in_specs=specs, scratch_shapes=list(scratch), compiler_params=WIDE, name=name
    )


def shards(
    layer_input, x_branch, gate_branch, conv_weight, conv_bias, x_proj, dt_proj, dt_bias, a_log, d_skip, carry_state,
    carry_tail, out_proj, steering, refusal, norm_gain, router, specialist_switch_matrix, w_up, w_down, expert_ids,
):
    taps = conv_weight.shape[0]
    length, prompts, channels = x_branch.shape
    rows = length * prompts
    states = a_log.shape[1]
    rank = dt_proj.shape[0]
    d_model = out_proj.shape[1]
    experts = router.shape[1]
    top_count = expert_ids.shape[-1]
    capacity = rows * top_count * 5 // (4 * experts)
    n_seq = lax.axis_size("seq")
    groups = lax.axis_size("expert")
    width = d_model // groups
    own_rows = rows // groups
    place = lax.axis_index("seq").astype(jnp.int32)
    owner = lax.axis_index("expert").astype(jnp.int32)

    swap = [(i, i ^ 1) for i in range(n_seq)]
    gate_w, up_w, down_w = specialist_switch_matrix[0], w_up[0], w_down[0]
    gate_o, up_o, down_o = (lax.ppermute(w, "seq", swap) for w in (gate_w, up_w, down_w))

    halo = (taps - 1) * prompts
    x_rows = x_branch.reshape(rows, channels)
    received = lax.ppermute(x_rows[rows - halo :], "seq", [(i, i + 1) for i in range(n_seq - 1)])
    activated, part = call(
        conv_kernel,
        (shape((rows, channels)), shape((rows, x_proj.shape[1]))),
        [SCALAR] + [VM] * 6,
        [pltpu.VMEM((rows + 8, channels), F32)],
        name="conv",
    )(place[None], x_rows, received, carry_tail.reshape(halo, channels), conv_weight, conv_bias[None], x_proj)
    summed = exchanged(part, "expert").reshape(groups, own_rows, part.shape[1]).sum(axis=0)
    projected = exchanged(jnp.tile(summed, (groups, 1)), "expert")
    bc = jnp.broadcast_to(projected[:, rank:, None], (rows, 2 * states, 128))
    a_log_t = a_log.T
    step, ends = call(
        functools.partial(local_kernel, prompts),
        (shape((rows, channels)), shape((prompts * states + 8, channels), BF16)),
        [VM] * 6,
        name="local",
    )(projected, dt_proj, dt_bias[None], activated, bc, a_log_t)
    every = exchanged(jnp.broadcast_to(ends[None], (n_seq,) + ends.shape), "seq")
    mixed = call(
        functools.partial(scan_kernel, prompts),
        shape((groups, rows, width), BF16),
        [SCALAR] + [VM] * 9 + [pl.BlockSpec(memory_space=pl.ANY)],
        [pltpu.VMEM((rows, channels), F32), pltpu.VMEM((channels, d_model), BF16), pltpu.SemaphoreType.DMA],
        name="scan",
    )(
        jnp.stack([place, owner]), every, carry_state.transpose(0, 2, 1), step, activated, bc, a_log_t, d_skip[None],
        gate_branch.reshape(rows, channels), layer_input.reshape(own_rows, d_model), out_proj,
    )
    mixed = exchanged(mixed, "expert")

    clean = call(clean_kernel, shape((d_model // 128, 128)), [VM] * 2, name="clean")(
        steering.reshape(-1, 128), refusal.reshape(refusal.shape[0], -1, 128)
    )
    start = owner * width
    ids = expert_ids.reshape(rows, top_count)
    residual, send, slots = call(
        dispatch_kernel,
        (
            shape((rows, width)),
            shape((experts, capacity, width + 128), BF16),
            shape((experts, capacity, rows), BF16),
        ),
        [VM] * 4,
        name="dispatch",
    )(
        mixed,
        lax.dynamic_slice_in_dim(clean.reshape(1, d_model), start, width, 1),
        lax.dynamic_slice_in_dim(norm_gain[None], start, width, 1),
        ids.T,
    )
    got = exchanged(send, "expert")
    normed = call(
        functools.partial(normed_kernel, float(d_model)), shape((capacity, d_model), BF16), [VM], name="normed"
    )(got)

    same_core = [[i for i in range(n_seq) if i % 2 == c] for c in range(2)]
    pieces = lax.all_gather(normed, "seq", axis=0, tiled=True, axis_index_groups=same_core)
    share = call(share_kernel, shape((capacity, 128)), [SCALAR] + [VM] * 4, name="share")(
        owner[None], normed, router.T, slots, ids
    )
    gate = dot(pieces, jnp.concatenate([gate_w, gate_o], axis=1))
    upward = dot(pieces, jnp.concatenate([up_w, up_o], axis=1))
    hidden = (jax.nn.silu(gate) * upward).astype(BF16)
    partial = dot(hidden, jnp.concatenate([down_w, down_o], axis=0)).astype(BF16)
    partial = exchanged(partial, "seq", same_core).reshape(n_seq // 2, capacity, d_model)
    weighted = pl.pallas_call(
        weigh_kernel,
        grid=(groups,),
        out_shape=shape((groups, capacity, width), BF16),
        in_specs=[
            pl.BlockSpec((n_seq // 2, capacity, width), lambda j: (0, 0, j)),
            pl.BlockSpec((capacity, 128), lambda j: (0, 0)),
        ],
        out_specs=pl.BlockSpec((1, capacity, width), lambda j: (j, 0, 0)),
        compiler_params=WIDE,
        name="weigh",
    )(partial, share)
    back = exchanged(weighted, "expert")
    total = call(combine_kernel, shape((rows, width)), [VM] * 3, name="combine")(residual, back, slots)
    out = exchanged(total, "expert").reshape(groups, own_rows, width)
    return out.transpose(1, 0, 2).reshape(own_rows // prompts, prompts, d_model)


def solution(mesh):
    return jax.shard_map(
        shards,
        mesh=mesh,
        in_specs=(
            P(("seq", "expert"), None, None),
            P("seq", None, "expert"),
            P("seq", None, "expert"),
            P(None, "expert"),
            P("expert"),
            P("expert", None),
            P(None, "expert"),
            P("expert"),
            P("expert", None),
            P("expert"),
            P(None, "expert", None),
            P(None, None, "expert"),
            P("expert", None),
            P(),
            P(),
            P(),
            P(),
            P("expert", None, "seq"),
            P("expert", None, "seq"),
            P("expert", "seq", None),
            P("seq", None, None),
        ),
        out_specs=P(("seq", "expert"), None, None),
        check_vma=False,
    )
```

profile of v0, /device:TPU:2, one launch (start us, length us, event | category | flops | bytes accessed | tf_op | source)
XLA Modules:
  0.0 343.2 jit_solution(1573840354258027077)
XLA Ops:
  7.2 1.9 collective-permute-start
  9.2 1.0 reshape.50.x_ref
  11.5 1.2 copy.22.xp_ref
  13.8 20.0 %all_to_all.55 = f32[8,16,288]{2,1,0:T(8,128)S(1)} all-to-all(f32[8,16,288]{2,1,0:T(8,128)S(1)} %bitcast.31), channel_id=1, replica_groups=mesh['seq'=32,'expert'=8] {'expert'}, dimensions={0} | all-to-all | bytes 294912 | tf_op jit(solution)/shard_map/all_to_all | solution.py:26
  33.8 13.4 %all_to_all.56 = f32[8,16,288]{2,1,0:T(8,128)S(1)} all-to-all(f32[8,16,288]{2,1,0:T(8,128)S(1)} %tile.2), channel_id=1, replica_groups=mesh['seq'=32,'expert'=8] {'expert'}, dimensions={0} | all-to-all | bytes 294912 | tf_op jit(solution)/shard_map/all_to_all | solution.py:26
  47.9 1.2 local.1
  49.9 1.2 broadcast_in_dim.13
  51.0 7.8 %all-to-all-start.2 = ((bf16[32,40,512]{2,1,0:T(8,128)(2,1)}), bf16[32,40,512]{2,1,0:T(8,128)(2,1)S(1)}, u32[]{:S(2)}, u32[]{:S(2)}) async-start(bf16[32,40,512]{2,1,0:T(8,128)(2,1)} %broadcast_in_dim.13), calls=%async_computation.2 | async-start | bytes 2621440 | tf_op jit(solution)/shard_map/all_to_all | solution.py:26
  58.8 1.0 reshape.53.own_ref
  59.8 1.6 reshape.52.gate_ref
  61.5 16.3 %all-to-all-done.2.all_ref = bf16[32,40,512]{2,1,0:T(8,128)(2,1)S(1)} async-done(((bf16[32,40,512]{2,1,0:T(8,128)(2,1)}), bf16[32,40,512]{2,1,0:T(8,128)(2,1)S(1)}, u32[]{:S(2)}, u32[]{:S(2)}) %all-to-all-start.2) | async-done | bytes 1310752 | tf_op jit(solution)/shard_map/all_to_all | solution.py:26
  77.8 2.2 copy-done
  79.9 0.9 copy-done.3
  80.9 0.9 copy-done.4
  81.8 0.9 copy-done.7
  84.3 3.3 scan.1
  87.7 1.0 copy-done.1
  88.7 3.7 %all-to-all-start.3 = ((bf16[8,128,512]{2,1,0:T(8,128)(2,1)}), bf16[8,128,512]{2,1,0:T(8,128)(2,1)S(1)}, u32[]{:S(2)}, u32[]{:S(2)}) async-start(bf16[8,128,512]{2,1,0:T(8,128)(2,1)} %copy-done.1), calls=%async_computation.3 | async-start | bytes 2097152 | tf_op jit(solution)/shard_map/all_to_all | solution.py:26
  93.4 1.5 clean.1
  94.9 26.7 %all-to-all-done.3.mixed_ref = bf16[8,128,512]{2,1,0:T(8,128)(2,1)S(1)} async-done(((bf16[8,128,512]{2,1,0:T(8,128)(2,1)}), bf16[8,128,512]{2,1,0:T(8,128)(2,1)S(1)}, u32[]{:S(2)}, u32[]{:S(2)}) %all-to-all-start.3) | async-done | bytes 1048608 | tf_op jit(solution)/shard_map/all_to_all | solution.py:26
  122.2 17.9 %all_to_all.57.got_ref = bf16[8,40,640]{2,1,0:T(8,128)(2,1)S(1)} all-to-all(bf16[8,40,640]{2,1,0:T(8,128)(2,1)S(1)} %get-tuple-element.17), channel_id=1, replica_groups=mesh['seq'=32,'expert'=8] {'expert'}, dimensions={0} | all-to-all | bytes 819200 | tf_op jit(solution)/shard_map/all_to_all | solution.py:26
  141.7 3.9 %collective-permute-done.2 = bf16[4096,256]{1,0:T(8,128)(2,1)} collective-permute-done((bf16[4096,256]{1,0:T(8,128)(2,1)}, bf16[4096,256]{1,0:T(8,128)(2,1)}, u32[]{:S(2)}, u32[]{:S(2)}) %collective-permute-start.2) | collective-permute-done | bytes 2097184 | tf_op jit(solution)/shard_map/ppermute | solution.py:247
  145.6 51.3 %all-gather.2.cloned.1.call-done = bf16[640,4096]{1,0:T(8,128)(2,1)} async-done(((bf16[40,4096]{1,0:T(8,128)(2,1)}), bf16[640,4096]{1,0:T(8,128)(2,1)}) %all-gather.2.cloned.1.call-update) | async-done | bytes 5242896 | tf_op jit(solution)/shard_map/all_gather | solution.py:308
  196.9 7.7 %fusion.4 = f32[640,512]{1,0:T(8,128)} fusion(bf16[640,4096]{1,0:T(8,128)(2,1)} %all-gather.2.cloned.1.call-done, bf16[4096,256]{1,0:T(8,128)(2,1)} %collective-permute-done.2, bf16[4096,256]{1,0:T(8,128)(2,1)} %bitcast.45), kind=kOutput, calls=%fused_computation.5 | convolution fusion | flops 2692743168 | bytes 10747904 | tf_op jit(solution)/shard_map/dot_general | solution.py:22
  204.6 12.8 %convolution_convert_fusion = bf16[640,4096]{1,0:T(8,128)(2,1)} fusion(bf16[256,4096]{1,0:T(8,128)(2,1)} %collective-permute-done.3, bf16[256,4096]{1,0:T(8,128)(2,1)S(1)} %bitcast.47, f32[640,512]{1,0:T(8,128)} %fusion.4, bf16[640,4096]{1,0:T(8,128)(2,1)} %all-gather.2.cloned.1.call-done, bf16[4096,256]{1,0:T(8,128)(2,1)} %collective-permute-done.1, ...), kind=kOutput, calls=%fused_computation | convolution fusion | flops 5390073856 | bytes 20185088 | tf_op jit(solution)/shard_map/dot_general | solution.py:22
  217.4 5.8 %all-to-all-start.5 = ((bf16[16,40,4096]{2,1,0:T(8,128)(2,1)}), bf16[16,40,4096]{2,1,0:T(8,128)(2,1)}, u32[]{:S(2)}, u32[]{:S(2)}) async-start(bf16[16,40,4096]{2,1,0:T(8,128)(2,1)} %bitcast.41), calls=%async_computation.5 | async-start | bytes 10485760 | tf_op jit(solution)/shard_map/all_to_all | solution.py:26
  223.3 1.3 share.1.share_ref
  224.6 73.3 %all-to-all-done.5.got_ref = bf16[16,40,4096]{2,1,0:T(8,128)(2,1)} async-done(((bf16[16,40,4096]{2,1,0:T(8,128)(2,1)}), bf16[16,40,4096]{2,1,0:T(8,128)(2,1)}, u32[]{:S(2)}, u32[]{:S(2)}) %all-to-all-start.5) | async-done | bytes 5242912 | tf_op jit(solution)/shard_map/all_to_all | solution.py:26
  297.9 5.1 %weigh.1 = bf16[8,40,512]{2,1,0:T(8,128)(2,1)S(1)} custom-call(bf16[16,40,4096]{2,1,0:T(8,128)(2,1)} %all-to-all-done.5.got_ref, f32[40,128]{1,0:T(8,128)S(1)} %share.1.share_ref), custom_call_target="tpu_custom_call" | custom-call | tf_op jit(solution)/shard_map/weigh/pallas_call | solution.py:317
  303.0 18.9 %all_to_all.58.got_ref = bf16[8,40,512]{2,1,0:T(8,128)(2,1)S(1)} all-to-all(bf16[8,40,512]{2,1,0:T(8,128)(2,1)S(1)} %weigh.1), channel_id=1, replica_groups=mesh['seq'=32,'expert'=8] {'expert'}, dimensions={0} | all-to-all | bytes 655360 | tf_op jit(solution)/shard_map/all_to_all | solution.py:26
  322.4 12.9 %all_to_all.59 = f32[8,16,512]{2,1,0:T(8,128)S(1)} all-to-all(f32[8,16,512]{2,1,0:T(8,128)S(1)} %bitcast.28), channel_id=1, replica_groups=mesh['seq'=32,'expert'=8] {'expert'}, dimensions={0} | all-to-all | bytes 524288 | tf_op jit(solution)/shard_map/all_to_all | solution.py:26
  335.5 0.9 reshape.58
  (61 shorter events, 10.0 us)
Async XLA Ops:
  7.2 5.5 %collective-permute-start = (bf16[6,512]{1,0:T(8,128)(2,1)S(1)}, bf16[6,512]{1,0:T(8,128)(2,1)S(1)}, u32[]{:S(2)}, u32[]{:S(2)}) collective-permute-start(bf16[6,512]{1,0:T(8,128)(2,1)S(1)} %slice.10), channel_id=1, source_target_pairs={{0,8},{8,16},{16,24},{24,32},{32,40},{40,48},{48,56},{56,64},{64,7... | collective-permute-start | bytes 18440 | tf_op jit(solution)/shard_map/ppermute | solution.py:251
  11.5 36.4 %copy-start.14 = (f32[512]{0:T(512)S(1)}, f32[512]{0:T(512)}, u32[]{:S(2)}) copy-start(f32[512]{0:T(512)} %param.28) | copy-start | bytes 6148
  12.7 35.2 %copy-start.5 = (bf16[256,512]{1,0:T(8,128)(2,1)S(1)}, bf16[256,512]{1,0:T(8,128)(2,1)}, u32[]{:S(2)}) copy-start(bf16[256,512]{1,0:T(8,128)(2,1)} %dtp_ref.1) | copy-start | bytes 786436
  12.7 35.2 %copy-start.8 = (f32[512,16]{0,1:T(8,128)S(1)}, f32[512,16]{0,1:T(8,128)}, u32[]{:S(2)}) copy-start(f32[512,16]{0,1:T(8,128)} %param.29) | copy-start | bytes 98308
  12.8 0.7 copy-start.13
  13.8 35.3 %copy-start.2 = (f32[128,512]{1,0:T(8,128)}, f32[128,512]{1,0:T(8,128)S(1)}, u32[]{:S(2)}) copy-start(f32[128,512]{1,0:T(8,128)S(1)} %get-tuple-element.13.act_ref) | copy-start | bytes 786436
  49.2 0.7 copy-start.6
  49.9 27.9 %copy-start.15 = (f32[512]{0:T(512)S(1)}, f32[512]{0:T(512)}, u32[]{:S(2)}) copy-start(f32[512]{0:T(512)} %param.30) | copy-start | bytes 6148
  51.0 26.7 %all-to-all-start.2 = ((bf16[32,40,512]{2,1,0:T(8,128)(2,1)}), bf16[32,40,512]{2,1,0:T(8,128)(2,1)S(1)}, u32[]{:S(2)}, u32[]{:S(2)}) async-start(bf16[32,40,512]{2,1,0:T(8,128)(2,1)} %broadcast_in_dim.13), calls=%async_computation.2 | async-start | bytes 2621440 | tf_op jit(solution)/shard_map/all_to_all | solution.py:26
  77.8 2.2 copy-start
  79.9 0.9 copy-start.3
  80.9 0.9 copy-start.4
  81.8 0.9 copy-start.7
  82.7 0.8 copy-start.9
  83.5 0.8 copy-start.10
  87.7 1.0 copy-start.1
  88.7 4.5 %copy-start.16 = (bf16[4,4096]{1,0:T(4,128)(2,1)S(1)}, bf16[4,4096]{1,0:T(4,128)(2,1)}, u32[]{:S(2)}) copy-start(bf16[4,4096]{1,0:T(4,128)(2,1)} %param.35) | copy-start | bytes 98308
  88.7 4.5 %copy-start.17 = (s32[64,2,2]{0,2,1:T(2,128)S(1)}, s32[64,2,2]{0,2,1:T(2,128)}, u32[]{:S(2)}) copy-start(s32[64,2,2]{0,2,1:T(2,128)} %param.41) | copy-start | bytes 3076
  88.7 4.7 %copy-start.12 = (bf16[4096]{0:T(1024)(128)(2,1)S(1)}, bf16[4096]{0:T(1024)(128)(2,1)}, u32[]{:S(2)}) copy-start(bf16[4096]{0:T(1024)(128)(2,1)} %param.34) | copy-start | bytes 24580
  88.7 33.0 %all-to-all-start.3 = ((bf16[8,128,512]{2,1,0:T(8,128)(2,1)}), bf16[8,128,512]{2,1,0:T(8,128)(2,1)S(1)}, u32[]{:S(2)}, u32[]{:S(2)}) async-start(bf16[8,128,512]{2,1,0:T(8,128)(2,1)} %copy-done.1), calls=%async_computation.3 | async-start | bytes 2097152 | tf_op jit(solution)/shard_map/all_to_all | solution.py:26
  92.4 104.6 %all-gather.2.cloned.1.call-start = ((), (), s32[]{:S(2)}) async-start(), calls=%async_computation.8 | async-start | bytes 5570560 | tf_op jit(solution)/shard_map/all_gather | solution.py:308
  141.0 4.6 %collective-permute-start.2 = (bf16[4096,256]{1,0:T(8,128)(2,1)}, bf16[4096,256]{1,0:T(8,128)(2,1)}, u32[]{:S(2)}, u32[]{:S(2)}) collective-permute-start(bf16[4096,256]{1,0:T(8,128)(2,1)} %bitcast.44), channel_id=1, source_target_pairs={{0,8},{8,0},{16,24},{24,16},{32,40},{40,32},{48,56},{56,48},{64,72... | collective-permute-start | bytes 6291464 | tf_op jit(solution)/shard_map/ppermute | solution.py:247
  141.1 63.5 %collective-permute-start.1 = (bf16[4096,256]{1,0:T(8,128)(2,1)}, bf16[4096,256]{1,0:T(8,128)(2,1)}, u32[]{:S(2)}, u32[]{:S(2)}) collective-permute-start(bf16[4096,256]{1,0:T(8,128)(2,1)} %bitcast.48), channel_id=1, source_target_pairs={{0,8},{8,0},{16,24},{24,16},{32,40},{40,32},{48,56},{56,48},{64,72... | collective-permute-start | bytes 6291464 | tf_op jit(solution)/shard_map/ppermute | solution.py:247
  141.6 63.0 %copy-start.18 = (bf16[1,256,4096]{2,1,0:T(8,128)(2,1)S(1)}, bf16[1,256,4096]{2,1,0:T(8,128)(2,1)}, u32[]{:S(2)}) copy-start(bf16[1,256,4096]{2,1,0:T(8,128)(2,1)} %param.40) | copy-start | bytes 6291460
  141.6 63.0 %collective-permute-start.3 = (bf16[256,4096]{1,0:T(8,128)(2,1)}, bf16[256,4096]{1,0:T(8,128)(2,1)}, u32[]{:S(2)}, u32[]{:S(2)}) collective-permute-start(bf16[256,4096]{1,0:T(8,128)(2,1)} %bitcast.46), channel_id=1, source_target_pairs={{0,8},{8,0},{16,24},{24,16},{32,40},{40,32},{48,56},{56,48},{64,72... | collective-permute-start | bytes 6291464 | tf_op jit(solution)/shard_map/ppermute | solution.py:247
  217.4 5.9 %copy-start.11 = (bf16[4096,8]{0,1:T(8,128)(2,1)S(1)}, bf16[4096,8]{0,1:T(8,128)(2,1)}, u32[]{:S(2)}) copy-start(bf16[4096,8]{0,1:T(8,128)(2,1)} %param.37) | copy-start | bytes 196612
  217.4 80.5 %all-to-all-start.5 = ((bf16[16,40,4096]{2,1,0:T(8,128)(2,1)}), bf16[16,40,4096]{2,1,0:T(8,128)(2,1)}, u32[]{:S(2)}, u32[]{:S(2)}) async-start(bf16[16,40,4096]{2,1,0:T(8,128)(2,1)} %bitcast.41), calls=%async_computation.5 | async-start | bytes 10485760 | tf_op jit(solution)/shard_map/all_to_all | solution.py:26
Sparse Core Ops, SparseCore 0:
  141.2 55.7 all-gather.1
where the time goes:
time: 347 us; the launch traced here: 343 us
  waiting for transfers between devices  171 us (49%)
  blocking collectives  83.1 us (24%)
  matrix products  20.5 us (6%)
  starting transfers between devices  20 us (6%)
  local copies, waits for them, and re-layouts  19.7 us (6%)
  Pallas kernels  14.7 us (4%)
  between operations  13.7 us (4%)
    all_to_all x3, waiting for transfers between devices, exchanged(): lax.all_to_all(blocks, axis, 0, 0, tiled=True, axis_index_groups=groups)  116 us
    all_to_all x5, blocking collectives, exchanged(): lax.all_to_all(blocks, axis, 0, 0, tiled=True, axis_index_groups=groups)  83.1 us
    all_gather x1, waiting for transfers between devices, shards(): lax.all_gather(normed, 'seq', axis=0, tiled=True, axis_index_groups=same_...  51.3 us
    dot_general x2, matrix products, dot(): return jnp.dot(a, b, preferred_element_type=F32)  20.5 us
    all_to_all x3, starting transfers between devices, exchanged(): lax.all_to_all(blocks, axis, 0, 0, tiled=True, axis_index_groups=groups)  17.3 us
    unnamed x41, local copies, waits for them, and re-layouts  10.3 us
  transfers between devices with their start and end apart: 8, of which 5 were waited for; matrix products, arithmetic and copies ran while one was open for 4% of the time, Pallas kernels for 1%

commit v1 on v0

--- a/solution.py
+++ b/solution.py
@@ -20,6 +20,10 @@
 
 def dot(a, b):
     return jnp.dot(a, b, preferred_element_type=F32)
+
+
+def fence(*values):
+    return lax.optimization_barrier(values)
 
 
 def exchanged(blocks, axis, groups=None):
@@ -40,7 +44,7 @@
         total = total + w[k : k + 1, :] * pad_ref[k * step : k * step + rows, :]
     act = silu(total)
     act_ref[...] = act
-    part_ref[...] = dot(act.astype(BF16), xp_ref[...])
+    part_ref[...] = lax.dot_general(act.astype(BF16), xp_ref[...], (((1,), (1,)), ((), ())), preferred_element_type=F32)
 
 
 def advance(state, rate, step, drive, b):
@@ -192,6 +196,37 @@
     out_ref[...] = jnp.broadcast_to(jax.nn.sigmoid(gap), out_ref.shape)
 
 
+def fetched(sources, held, sem):
+    copies = [pltpu.make_async_copy(a, b, sem.at[i]) for i, (a, b) in enumerate(zip(sources, held))]
+    for copy in copies:
+        copy.start()
+    return copies
+
+
+def hidden_kernel(half_ref, x_ref, g0_ref, u0_ref, g1_ref, u1_ref, out_ref, g0, u0, g1, u1, sem):
+    copies = fetched((g0_ref, u0_ref, g1_ref, u1_ref), (g0, u0, g1, u1), sem)
+    x = x_ref[...]
+    width = g0.shape[1]
+    for k, (g, u) in enumerate(((g0, u0), (g1, u1))):
+        copies[2 * k].wait()
+        gate = dot(x, g[...])
+        copies[2 * k + 1].wait()
+        out_ref[:, k * width : (k + 1) * width] = (silu(gate) * dot(x, u[...])).astype(BF16)
+
+
+def down_kernel(own_ref, far_ref, d0_ref, d1_ref, d2_ref, d3_ref, out_ref, d0, d1, d2, d3, sem):
+    copies = fetched((d0_ref, d1_ref, d2_ref, d3_ref), (d0, d1, d2, d3), sem)
+    width = d0.shape[0]
+    hidden = [ref[:, k * width : (k + 1) * width] for ref in (own_ref, far_ref) for k in range(2)]
+    for copy in copies:
+        copy.wait()
+    for j in range(0, out_ref.shape[1], 512):
+        total = dot(hidden[0], d0[:, j : j + 512])
+        for h, d in zip(hidden[1:], (d1, d2, d3)):
+            total = total + dot(h, d[:, j : j + 512])
+        out_ref[:, j : j + 512] = total.astype(BF16)
+
+
 def weigh_kernel(got_ref, share_ref, out_ref):
     total = got_ref[0].astype(F32)
     for i in range(1, got_ref.shape[0]):
@@ -242,48 +277,64 @@
     place = lax.axis_index("seq").astype(jnp.int32)
     owner = lax.axis_index("expert").astype(jnp.int32)
 
-    swap = [(i, i ^ 1) for i in range(n_seq)]
+    near, across = ([(i, i ^ d) for i in range(n_seq)] for d in (1, 2))
     gate_w, up_w, down_w = specialist_switch_matrix[0], w_up[0], w_down[0]
-    gate_o, up_o, down_o = (lax.ppermute(w, "seq", swap) for w in (gate_w, up_w, down_w))
+    others = tuple(lax.ppermute(w, "seq", near) for w in (gate_w, up_w, down_w))
+    down_far = lax.ppermute(down_w, "seq", across)
 
     halo = (taps - 1) * prompts
     x_rows = x_branch.reshape(rows, channels)
     received = lax.ppermute(x_rows[rows - halo :], "seq", [(i, i + 1) for i in range(n_seq - 1)])
+    here = (
+        a_log.T, carry_state.transpose(0, 2, 1), gate_branch.reshape(rows, channels),
+        layer_input.reshape(own_rows, d_model), jnp.stack([place, owner]),
+    )
+
     activated, part = call(
         conv_kernel,
         (shape((rows, channels)), shape((rows, x_proj.shape[1]))),
         [SCALAR] + [VM] * 6,
         [pltpu.VMEM((rows + 8, channels), F32)],
         name="conv",
-    )(place[None], x_rows, received, carry_tail.reshape(halo, channels), conv_weight, conv_bias[None], x_proj)
+    )(place[None], x_rows, received, carry_tail.reshape(halo, channels), conv_weight, conv_bias[None], x_proj.T)
+    part, activated, *here = fence(part, activated, *here)
     summed = exchanged(part, "expert").reshape(groups, own_rows, part.shape[1]).sum(axis=0)
+    summed, activated, *here = fence(summed, activated, *here)
     projected = exchanged(jnp.tile(summed, (groups, 1)), "expert")
+    projected, activated, *rest = fence(projected, activated, *here, *others, down_far)
+    (a_log_t, carry_t, gate_rows, own, spot), (gate_o, up_o, down_o, down_far) = rest[:-4], rest[-4:]
+    down_corner = lax.ppermute(down_far, "seq", near)
     bc = jnp.broadcast_to(projected[:, rank:, None], (rows, 2 * states, 128))
-    a_log_t = a_log.T
     step, ends = call(
         functools.partial(local_kernel, prompts),
         (shape((rows, channels)), shape((prompts * states + 8, channels), BF16)),
         [VM] * 6,
         name="local",
     )(projected, dt_proj, dt_bias[None], activated, bc, a_log_t)
-    every = exchanged(jnp.broadcast_to(ends[None], (n_seq,) + ends.shape), "seq")
+    ends, step, bc = fence(jnp.broadcast_to(ends[None], (n_seq,) + ends.shape), step, bc)
+    every = exchanged(ends, "seq")
+    every, step, bc, activated, a_log_t, carry_t, gate_rows, own = fence(
+        every, step, bc, activated, a_log_t, carry_t, gate_rows, own
+    )
     mixed = call(
         functools.partial(scan_kernel, prompts),
         shape((groups, rows, width), BF16),
         [SCALAR] + [VM] * 9 + [pl.BlockSpec(memory_space=pl.ANY)],
         [pltpu.VMEM((rows, channels), F32), pltpu.VMEM((channels, d_model), BF16), pltpu.SemaphoreType.DMA],
         name="scan",
-    )(
-        jnp.stack([place, owner]), every, carry_state.transpose(0, 2, 1), step, activated, bc, a_log_t, d_skip[None],
-        gate_branch.reshape(rows, channels), layer_input.reshape(own_rows, d_model), out_proj,
+    )(spot, every, carry_t, step, activated, bc, a_log_t, d_skip[None], gate_rows, own, out_proj)
+    mixed, steering, refusal, norm_gain, expert_ids, down_corner = fence(
+        mixed, steering, refusal, norm_gain, expert_ids, down_corner
     )
     mixed = exchanged(mixed, "expert")
-
     clean = call(clean_kernel, shape((d_model // 128, 128)), [VM] * 2, name="clean")(
         steering.reshape(-1, 128), refusal.reshape(refusal.shape[0], -1, 128)
     )
     start = owner * width
+    clean = lax.dynamic_slice_in_dim(clean.reshape(1, d_model), start, width, 1)
+    gain = lax.dynamic_slice_in_dim(norm_gain[None], start, width, 1)
     ids = expert_ids.reshape(rows, top_count)
+
     residual, send, slots = call(
         dispatch_kernel,
         (
@@ -293,33 +344,61 @@
         ),
         [VM] * 4,
         name="dispatch",
-    )(
-        mixed,
-        lax.dynamic_slice_in_dim(clean.reshape(1, d_model), start, width, 1),
-        lax.dynamic_slice_in_dim(norm_gain[None], start, width, 1),
-        ids.T,
-    )
+    )(mixed, clean, gain, ids.T)
     got = exchanged(send, "expert")
     normed = call(
         functools.partial(normed_kernel, float(d_model)), shape((capacity, d_model), BF16), [VM], name="normed"
     )(got)
 
-    same_core = [[i for i in range(n_seq) if i % 2 == c] for c in range(2)]
-    pieces = lax.all_gather(normed, "seq", axis=0, tiled=True, axis_index_groups=same_core)
+    kinds = [[i for i in range(n_seq) if i % 4 == k] for k in range(4)]
+    pieces = lax.all_gather(normed, "seq", axis=0, tiled=True, axis_index_groups=[kinds[0] + kinds[2], kinds[1] + kinds[3]])
     share = call(share_kernel, shape((capacity, 128)), [SCALAR] + [VM] * 4, name="share")(
         owner[None], normed, router.T, slots, ids
     )
-    gate = dot(pieces, jnp.concatenate([gate_w, gate_o], axis=1))
-    upward = dot(pieces, jnp.concatenate([up_w, up_o], axis=1))
-    hidden = (jax.nn.silu(gate) * upward).astype(BF16)
-    partial = dot(hidden, jnp.concatenate([down_w, down_o], axis=0)).astype(BF16)
-    partial = exchanged(partial, "seq", same_core).reshape(n_seq // 2, capacity, d_model)
+    half = pieces.shape[0] // 2
+    big = pltpu.CompilerParams(vmem_limit_bytes=58 * 1024 * 1024)
+    hbm = pl.BlockSpec(memory_space=pltpu.HBM)
+    up_sources = (gate_w, up_w, gate_o, up_o)
+    inner = 2 * up_w.shape[1]
+
+    def hidden_of(which):
+        return pl.pallas_call(
+            hidden_kernel,
+            grid_spec=pltpu.PrefetchScalarGridSpec(
+                num_scalar_prefetch=1,
+                grid=(1,),
+                in_specs=[pl.BlockSpec((half, d_model), lambda i, which: (which[0], 0))] + [hbm] * 4,
+                out_specs=pl.BlockSpec((half, inner), lambda i, which: (0, 0)),
+                scratch_shapes=[pltpu.VMEM(w.shape, BF16) for w in up_sources] + [pltpu.SemaphoreType.DMA((4,))],
+            ),
+            out_shape=shape((half, inner), BF16),
+            compiler_params=big,
+            name="hidden",
+        )(which[None], pieces, *up_sources)
+
+    mine = (place // 2) % 2
+    given = lax.ppermute(hidden_of(1 - mine), "seq", across)
+    kept = hidden_of(mine)
+    down_sources = (down_w, down_o, down_far, down_corner)
+    partial = pl.pallas_call(
+        down_kernel,
+        grid=(1,),
+        out_shape=shape((half, d_model), BF16),
+        in_specs=[pl.BlockSpec((half, inner), lambda i: (0, 0))] * 2 + [hbm] * 4,
+        out_specs=pl.BlockSpec((half, d_model), lambda i: (0, 0)),
+        scratch_shapes=[pltpu.VMEM(w.shape, BF16) for w in down_sources] + [pltpu.SemaphoreType.DMA((4,))],
+        compiler_params=big,
+        name="down",
+    )(kept, given, *down_sources)
+    partial, share, residual, slots = fence(partial, share, residual, slots)
+    partial = exchanged(partial, "seq", kinds).reshape(n_seq // 4, capacity, d_model)
+    partial, share, residual, slots = fence(partial, share, residual, slots)
     weighted = pl.pallas_call(
         weigh_kernel,
         grid=(groups,),
         out_shape=shape((groups, capacity, width), BF16),
         in_specs=[
-            pl.BlockSpec((n_seq // 2, capacity, width), lambda j: (0, 0, j)),
+            pl.BlockSpec((n_seq // 4, capacity, width), lambda j: (0, 0, j)),
             pl.BlockSpec((capacity, 128), lambda j: (0, 0)),
         ],
         out_specs=pl.BlockSpec((1, capacity, width), lambda j: (j, 0, 0)),

time: 347 us -> 412 us (1.19)
  blocking collectives: 83.1 us -> 140 us
  Pallas kernels: 14.7 us -> 40.7 us
  matrix products: 20.5 us -> 0 us
  waiting for transfers between devices: 171 us -> 185 us
  local copies, waits for them, and re-layouts: 19.7 us -> 10.2 us
    all_to_all x3 -> x1, waiting for transfers between devices: 116 us -> 27 us  [exchanged(): lax.all_to_all(blocks, axis, 0, 0, tiled=True, axis_index_groups=groups)]
    all_gather x1, waiting for transfers between devices: 51.3 us -> 120 us  [shards(): lax.all_gather(normed, 'seq', axis=0, tiled=True, axis_index_groups=[kind...]
    all_to_all x5 -> x7, blocking collectives: 83.1 us -> 140 us  [exchanged(): lax.all_to_all(blocks, axis, 0, 0, tiled=True, axis_index_groups=groups)]
    ppermute x1, waiting for transfers between devices: 0.01 us -> 38 us  [shards(): lax.ppermute(x_rows[rows - halo:], 'seq', [(i, i + 1) for i in range(n_se...]
    pallas_call x0 -> x3, Pallas kernels: none -> 29.2 us  [the longest x2 20.2 us: hidden_of(): pl.pallas_call(hidden_kernel, grid_spec=pltpu.PrefetchScalarGridSpec(num_...]
    dot_general x2 -> x0, matrix products: 20.5 us -> none  [dot(): return jnp.dot(a, b, preferred_element_type=F32)]
    ppermute x3 -> x6, starting transfers between devices: 0.69 us -> 15.9 us  [the longest x1 13 us: shards(): given = lax.ppermute(hidden_of(1 - mine), 'seq', across)]
    all_to_all x3 -> x1, starting transfers between devices: 17.3 us -> 3.57 us  [exchanged(): lax.all_to_all(blocks, axis, 0, 0, tiled=True, axis_index_groups=groups)]
  transfers between devices with their start and end apart: 8 -> 9, of which waited for: 5 -> 3; matrix products, arithmetic and copies ran while one was open for 4% -> 2% of each run, Pallas kernels for 1% -> 5%
where the time goes in v1:
time: 412 us; the launch traced here: 411 us
  waiting for transfers between devices  185 us (45%)
  blocking collectives  140 us (34%)
  Pallas kernels  40.7 us (10%)
  starting transfers between devices  21.9 us (5%)
  between operations  13.7 us (3%)
  local copies, waits for them, and re-layouts  10.2 us (2%)
    all_to_all x7, blocking collectives, exchanged(): lax.all_to_all(blocks, axis, 0, 0, tiled=True, axis_index_groups=groups)  140 us
    all_gather x1, waiting for transfers between devices, shards(): lax.all_gather(normed, 'seq', axis=0, tiled=True, axis_index_groups=[kind...  120 us
    ppermute x1, waiting for transfers between devices, shards(): lax.ppermute(x_rows[rows - halo:], 'seq', [(i, i + 1) for i in range(n_se...  38 us
    all_to_all x1, waiting for transfers between devices, exchanged(): lax.all_to_all(blocks, axis, 0, 0, tiled=True, axis_index_groups=groups)  27 us
    pallas_call x2, Pallas kernels, hidden_of(): pl.pallas_call(hidden_kernel, grid_spec=pltpu.PrefetchScalarGridSpec(num_...  20.2 us
    ppermute x1, starting transfers between devices, shards(): given = lax.ppermute(hidden_of(1 - mine), 'seq', across)  13 us
    pallas_call x1, Pallas kernels, shards(): pl.pallas_call(down_kernel, grid=(1,), out_shape=shape((half, d_model), B...  8.95 us
  transfers between devices with their start and end apart: 9, of which 3 were waited for; matrix products, arithmetic and copies ran while one was open for 2% of the time, Pallas kernels for 5%

profile of v1, /device:TPU:2, one launch (start us, length us, event | category | flops | bytes accessed | tf_op | source)
XLA Modules:
  0.0 411.4 jit_solution(11047683181428464345)
XLA Ops:
  7.0 2.3 collective-permute-start.4
  9.3 0.7 slice.9
  10.0 2.4 collective-permute-start
  12.5 1.0 reshape.50.x_ref
  14.2 0.7 reshape.51.carry_ref
  14.9 1.0 reshape.53.own_ref
  15.9 1.0 reshape.52.gate_ref
  16.9 38.0 %collective-permute-done.got_ref = bf16[6,512]{1,0:T(8,128)(2,1)S(1)} collective-permute-done((bf16[6,512]{1,0:T(8,128)(2,1)S(1)}, bf16[6,512]{1,0:T(8,128)(2,1)S(1)}, u32[]{:S(2)}, u32[]{:S(2)}) %collective-permute-start) | collective-permute-done | bytes 6176 | tf_op jit(solution)/shard_map/ppermute | solution.py:287
  54.9 1.0 copy-done.1
  56.9 17.2 %all_to_all.56 = f32[8,16,288]{2,1,0:T(8,128)S(1)} all-to-all(f32[8,16,288]{2,1,0:T(8,128)S(1)} %bitcast.33), channel_id=1, replica_groups=mesh['seq'=32,'expert'=8] {'expert'}, dimensions={0} | all-to-all | bytes 294912 | tf_op jit(solution)/shard_map/all_to_all | solution.py:30
  74.1 12.2 %all_to_all.57 = f32[8,16,288]{2,1,0:T(8,128)S(1)} all-to-all(f32[8,16,288]{2,1,0:T(8,128)S(1)} %tile.2), channel_id=1, replica_groups=mesh['seq'=32,'expert'=8] {'expert'}, dimensions={0} | all-to-all | bytes 294912 | tf_op jit(solution)/shard_map/all_to_all | solution.py:30
  87.1 1.2 local.1
  88.4 26.2 %all_to_all.58.all_ref = bf16[32,40,512]{2,1,0:T(8,128)(2,1)S(1)} all-to-all(bf16[32,40,512]{2,1,0:T(8,128)(2,1)S(1)} %broadcast_in_dim.37), channel_id=1, replica_groups=mesh['seq'=32,'expert'=8] {'seq'}, dimensions={0} | all-to-all | bytes 2621440 | tf_op jit(solution)/shard_map/all_to_all | solution.py:30
  114.6 4.4 %scan.1 = bf16[8,128,512]{2,1,0:T(8,128)(2,1)} custom-call(s32[2]{0:T(128)S(1)} %pad_add_fusion.ids_ref, bf16[32,40,512]{2,1,0:T(8,128)(2,1)S(1)} %all_to_all.58.all_ref, f32[2,16,512]{2,1,0:T(8,128)S(1)} %bitcast.37, f32[128,512]{1,0:T(8,128)S(1)} %get-tuple-element.92.step_ref, f32[128,512]{1,0:T(8,128)S(1)} %get-tuple-element.93.act_ref, ...), custom_call_target="tpu_custom_call" | custom-call | tf_op jit(solution)/shard_map/scan/pallas_call | solution.py:319
  119.0 3.6 all-to-all-start.3
  122.6 0.8 dynamic-slice.3
  123.6 1.5 clean.1
  125.2 27.0 %all-to-all-done.3.mixed_ref = bf16[8,128,512]{2,1,0:T(8,128)(2,1)S(1)} async-done(((bf16[8,128,512]{2,1,0:T(8,128)(2,1)}), bf16[8,128,512]{2,1,0:T(8,128)(2,1)S(1)}, u32[]{:S(2)}, u32[]{:S(2)}) %all-to-all-start.3) | async-done | bytes 1048608 | tf_op jit(solution)/shard_map/all_to_all | solution.py:30
  152.8 17.9 %all_to_all.59.got_ref = bf16[8,40,640]{2,1,0:T(8,128)(2,1)S(1)} all-to-all(bf16[8,40,640]{2,1,0:T(8,128)(2,1)S(1)} %get-tuple-element.104), channel_id=1, replica_groups=mesh['seq'=32,'expert'=8] {'expert'}, dimensions={0} | all-to-all | bytes 819200 | tf_op jit(solution)/shard_map/all_to_all | solution.py:30
  170.7 0.9 normed.1.x_ref
  171.6 120.2 %all-gather.2.cloned.1.call-done.x_ref = bf16[640,4096]{1,0:T(8,128)(2,1)} async-done(((bf16[40,4096]{1,0:T(8,128)(2,1)}), bf16[640,4096]{1,0:T(8,128)(2,1)}) %all-gather.2.cloned.1.call-update) | async-done | bytes 5242896 | tf_op jit(solution)/shard_map/all_gather | solution.py:354
  291.8 10.1 %hidden.3 = bf16[320,512]{1,0:T(8,128)(2,1)} custom-call(s32[1]{0:T(128)} %bitcast.17.half_ref, bf16[640,4096]{1,0:T(8,128)(2,1)} %all-gather.2.cloned.1.call-done.x_ref, bf16[4096,256]{1,0:T(8,128)(2,1)} %bitcast.45, bf16[4096,256]{1,0:T(8,128)(2,1)} %bitcast.48, bf16[4096,256]{1,0:T(8,128)(2,1)} %copy-done.10, bf16[4096,256]{1,0:T(8,128)(2,1)} %collective-permute-done.2.u1_ref), custom_call_target="tpu_custom_call" | custom-call | tf_op jit(solution)/shard_map/hidden/pallas_call | solution.py:365
  302.0 13.0 %collective-permute-start.6 = (bf16[320,512]{1,0:T(8,128)(2,1)}, bf16[320,512]{1,0:T(8,128)(2,1)S(1)}, u32[]{:S(2)}, u32[]{:S(2)}) collective-permute-start(bf16[320,512]{1,0:T(8,128)(2,1)} %hidden.3), channel_id=1, source_target_pairs={{0,16},{8,24},{16,0},{24,8},{32,48},{40,56},{48,32},{56,40},{64,80... | collective-permute-start | bytes 983048 | tf_op jit(solution)/shard_map/ppermute | solution.py:380
  315.0 1.3 share.1.share_ref
  316.3 10.1 %hidden.2.own_ref = bf16[320,512]{1,0:T(8,128)(2,1)} custom-call(s32[1]{0:T(128)} %bitcast.half_ref, bf16[640,4096]{1,0:T(8,128)(2,1)} %all-gather.2.cloned.1.call-done.x_ref, bf16[4096,256]{1,0:T(8,128)(2,1)} %bitcast.46, bf16[4096,256]{1,0:T(8,128)(2,1)} %bitcast.49, bf16[4096,256]{1,0:T(8,128)(2,1)} %copy-done.10, ...), custom_call_target="tpu_custom_call" | custom-call | tf_op jit(solution)/shard_map/hidden/pallas_call | solution.py:365
  326.5 0.7 copy-done.11
  327.2 8.9 %down.1 = bf16[320,4096]{1,0:T(8,128)(2,1)} custom-call(bf16[320,512]{1,0:T(8,128)(2,1)} %hidden.2.own_ref, bf16[320,512]{1,0:T(8,128)(2,1)} %copy-done.11, bf16[256,4096]{1,0:T(8,128)(2,1)} %bitcast.52, bf16[256,4096]{1,0:T(8,128)(2,1)} %collective-permute-done.3.d1_ref, bf16[256,4096]{1,0:T(8,128)(2,1)} %collective-permute-done.4.d2_ref, ...), custom_call_target="tpu_custom_call" | custom-call | tf_op jit(solution)/shard_map/down/pallas_call | solution.py:383
  336.2 35.2 %all_to_all.60.got_ref = bf16[8,40,4096]{2,1,0:T(8,128)(2,1)S(1)} all-to-all(bf16[8,40,4096]{2,1,0:T(8,128)(2,1)} %bitcast.43), channel_id=1, replica_groups={{0,32,64,96,128,160,192,224},{8,40,72,104,136,168,200,232},{16,48,80,11..., dimensions={0} | all-to-all | bytes 5242880 | tf_op jit(solution)/shard_map/all_to_all | solution.py:30
  371.4 0.8 weigh.1
  372.2 18.0 %all_to_all.61.got_ref = bf16[8,40,512]{2,1,0:T(8,128)(2,1)S(1)} all-to-all(bf16[8,40,512]{2,1,0:T(8,128)(2,1)S(1)} %weigh.1), channel_id=1, replica_groups=mesh['seq'=32,'expert'=8] {'expert'}, dimensions={0} | all-to-all | bytes 655360 | tf_op jit(solution)/shard_map/all_to_all | solution.py:30
  390.6 12.9 %all_to_all.62 = f32[8,16,512]{2,1,0:T(8,128)S(1)} all-to-all(f32[8,16,512]{2,1,0:T(8,128)S(1)} %bitcast.29), channel_id=1, replica_groups=mesh['seq'=32,'expert'=8] {'expert'}, dimensions={0} | all-to-all | bytes 524288 | tf_op jit(solution)/shard_map/all_to_all | solution.py:30
  403.7 0.9 reshape.58
  (55 shorter events, 4.7 us)
Async XLA Ops:
  6.5 79.7 %collective-permute-start.1 = (bf16[4096,256]{1,0:T(8,128)(2,1)}, bf16[4096,256]{1,0:T(8,128)(2,1)S(1)}, u32[]{:S(2)}, u32[]{:S(2)}) collective-permute-start(bf16[4096,256]{1,0:T(8,128)(2,1)} %bitcast.44), channel_id=1, source_target_pairs={{0,8},{8,0},{16,24},{24,16},{32,40},{40,32},{48,56},{56,48},{64,72... | collective-permute-start | bytes 6291464 | tf_op jit(solution)/shard_map/ppermute | solution.py:282
  6.5 79.7 %collective-permute-start.2 = (bf16[4096,256]{1,0:T(8,128)(2,1)}, bf16[4096,256]{1,0:T(8,128)(2,1)}, u32[]{:S(2)}, u32[]{:S(2)}) collective-permute-start(bf16[4096,256]{1,0:T(8,128)(2,1)} %bitcast.47), channel_id=1, source_target_pairs={{0,8},{8,0},{16,24},{24,16},{32,40},{40,32},{48,56},{56,48},{64,72... | collective-permute-start | bytes 6291464 | tf_op jit(solution)/shard_map/ppermute | solution.py:282
  7.0 79.2 %collective-permute-start.4 = (bf16[256,4096]{1,0:T(8,128)(2,1)}, bf16[256,4096]{1,0:T(8,128)(2,1)}, u32[]{:S(2)}, u32[]{:S(2)}) collective-permute-start(bf16[256,4096]{1,0:T(8,128)(2,1)} %bitcast.50), channel_id=1, source_target_pairs={{0,16},{8,24},{16,0},{24,8},{32,48},{40,56},{48,32},{56,40},{64,80... | collective-permute-start | bytes 6291464 | tf_op jit(solution)/shard_map/ppermute | solution.py:283
  9.3 77.0 %collective-permute-start.3 = (bf16[256,4096]{1,0:T(8,128)(2,1)}, bf16[256,4096]{1,0:T(8,128)(2,1)}, u32[]{:S(2)}, u32[]{:S(2)}) collective-permute-start(bf16[256,4096]{1,0:T(8,128)(2,1)} %bitcast.51), channel_id=1, source_target_pairs={{0,8},{8,0},{16,24},{24,16},{32,40},{40,32},{48,56},{56,48},{64,72... | collective-permute-start | bytes 6291464 | tf_op jit(solution)/shard_map/ppermute | solution.py:282
  10.0 44.8 %collective-permute-start = (bf16[6,512]{1,0:T(8,128)(2,1)S(1)}, bf16[6,512]{1,0:T(8,128)(2,1)S(1)}, u32[]{:S(2)}, u32[]{:S(2)}) collective-permute-start(bf16[6,512]{1,0:T(8,128)(2,1)S(1)} %slice.10), channel_id=1, source_target_pairs={{0,8},{8,16},{16,24},{24,32},{32,40},{40,48},{48,56},{56,64},{64,7... | collective-permute-start | bytes 18440 | tf_op jit(solution)/shard_map/ppermute | solution.py:287
  14.9 72.1 %copy-start.3 = (f32[512,16]{0,1:T(8,128)S(1)}, f32[512,16]{0,1:T(8,128)}, u32[]{:S(2)}) copy-start(f32[512,16]{0,1:T(8,128)} %param.29) | copy-start | bytes 98308
  14.9 72.2 %copy-start.8 = (f32[512]{0:T(512)S(1)}, f32[512]{0:T(512)}, u32[]{:S(2)}) copy-start(f32[512]{0:T(512)} %param.28) | copy-start | bytes 6148
  15.9 71.2 %copy-start.2 = (bf16[256,512]{1,0:T(8,128)(2,1)S(1)}, bf16[256,512]{1,0:T(8,128)(2,1)}, u32[]{:S(2)}) copy-start(bf16[256,512]{1,0:T(8,128)(2,1)} %dtp_ref.1) | copy-start | bytes 786436
  54.9 1.0 copy-start.1
  55.8 0.7 copy-start.7
  86.3 2.0 copy-start.10
  86.3 32.7 %collective-permute-start.5 = (bf16[256,4096]{1,0:T(8,128)(2,1)}, bf16[256,4096]{1,0:T(8,128)(2,1)}, u32[]{:S(2)}, u32[]{:S(2)}) collective-permute-start(bf16[256,4096]{1,0:T(8,128)(2,1)} %collective-permute-done.4.d2_ref), channel_id=1, source_target_pairs={{0,8},{8,0},{16,24},{24,16},{32,40},{40,32},{48,56},{56,48},{64,72... | collective-permute-start | bytes 6291464 | tf_op jit(solution)/shard_map/ppermute | solution.py:306
  87.1 27.5 %copy-start = (bf16[512,4096]{1,0:T(8,128)(2,1)S(1)}, bf16[512,4096]{1,0:T(8,128)(2,1)}, u32[]{:S(2)}) copy-start(bf16[512,4096]{1,0:T(8,128)(2,1)} %outp_ref.1) | copy-start | bytes 12582916
  88.3 26.3 %copy-start.4 = (f32[2,512,16]{1,2,0:T(8,128)S(1)}, f32[2,512,16]{1,2,0:T(8,128)}, u32[]{:S(2)}) copy-start(f32[2,512,16]{1,2,0:T(8,128)} %param.31) | copy-start | bytes 196612
  88.3 26.3 %copy-start.9 = (f32[512]{0:T(512)S(1)}, f32[512]{0:T(512)}, u32[]{:S(2)}) copy-start(f32[512]{0:T(512)} %param.30) | copy-start | bytes 6148
  119.0 4.4 %copy-start.12 = (bf16[4,4096]{1,0:T(4,128)(2,1)S(1)}, bf16[4,4096]{1,0:T(4,128)(2,1)}, u32[]{:S(2)}) copy-start(bf16[4,4096]{1,0:T(4,128)(2,1)} %param.35) | copy-start | bytes 98308
  119.0 4.4 %copy-start.13 = (s32[64,2,2]{0,2,1:T(2,128)S(1)}, s32[64,2,2]{0,2,1:T(2,128)}, u32[]{:S(2)}) copy-start(s32[64,2,2]{0,2,1:T(2,128)} %param.41) | copy-start | bytes 3076
  119.0 4.6 %copy-start.6 = (bf16[4096]{0:T(1024)(128)(2,1)S(1)}, bf16[4096]{0:T(1024)(128)(2,1)}, u32[]{:S(2)}) copy-start(bf16[4096]{0:T(1024)(128)(2,1)} %param.34) | copy-start | bytes 24580
  119.0 33.2 %all-to-all-start.3 = ((bf16[8,128,512]{2,1,0:T(8,128)(2,1)}), bf16[8,128,512]{2,1,0:T(8,128)(2,1)S(1)}, u32[]{:S(2)}, u32[]{:S(2)}) async-start(bf16[8,128,512]{2,1,0:T(8,128)(2,1)} %scan.1), calls=%async_computation.3 | async-start | bytes 2097152 | tf_op jit(solution)/shard_map/all_to_all | solution.py:30
  122.6 169.3 %all-gather.2.cloned.1.call-start = ((), (), s32[]{:S(2)}) async-start(), calls=%async_computation.8 | async-start | bytes 5570560 | tf_op jit(solution)/shard_map/all_gather | solution.py:354
  291.8 23.2 %copy-start.5 = (bf16[4096,8]{0,1:T(8,128)(2,1)S(1)}, bf16[4096,8]{0,1:T(8,128)(2,1)}, u32[]{:S(2)}) copy-start(bf16[4096,8]{0,1:T(8,128)(2,1)} %param.37) | copy-start | bytes 196612
  302.0 24.5 %collective-permute-start.6 = (bf16[320,512]{1,0:T(8,128)(2,1)}, bf16[320,512]{1,0:T(8,128)(2,1)S(1)}, u32[]{:S(2)}, u32[]{:S(2)}) collective-permute-start(bf16[320,512]{1,0:T(8,128)(2,1)} %hidden.3), channel_id=1, source_target_pairs={{0,16},{8,24},{16,0},{24,8},{32,48},{40,56},{48,32},{56,40},{64,80... | collective-permute-start | bytes 983048 | tf_op jit(solution)/shard_map/ppermute | solution.py:380
  326.5 0.7 copy-start.11
Sparse Core Ops, SparseCore 0:
  171.7 120.0 all-gather.1

commit v2 on v0

--- a/solution.py
+++ b/solution.py
@@ -20,6 +20,10 @@
 
 def dot(a, b):
     return jnp.dot(a, b, preferred_element_type=F32)
+
+
+def fence(*values):
+    return lax.optimization_barrier(values)
 
 
 def exchanged(blocks, axis, groups=None):
@@ -40,7 +44,7 @@
         total = total + w[k : k + 1, :] * pad_ref[k * step : k * step + rows, :]
     act = silu(total)
     act_ref[...] = act
-    part_ref[...] = dot(act.astype(BF16), xp_ref[...])
+    part_ref[...] = lax.dot_general(act.astype(BF16), xp_ref[...], (((1,), (1,)), ((), ())), preferred_element_type=F32)
 
 
 def advance(state, rate, step, drive, b):
@@ -192,6 +196,39 @@
     out_ref[...] = jnp.broadcast_to(jax.nn.sigmoid(gap), out_ref.shape)
 
 
+def fetched(sources, held, sem):
+    copies = [pltpu.make_async_copy(a, b, sem.at[i]) for i, (a, b) in enumerate(zip(sources, held))]
+    for copy in copies:
+        copy.start()
+    return copies
+
+
+def expert_kernel(x_ref, g0_ref, u0_ref, g1_ref, u1_ref, d0_ref, d1_ref, out_ref, x_held, g0, u0, g1, u1, d0, d1, sem):
+    tiles, tile, _ = x_held.shape
+    sources = [x_ref.at[pl.ds(0, tile)], g0_ref, u0_ref, g1_ref, u1_ref, d0_ref, d1_ref]
+    targets = [x_held.at[0], g0, u0, g1, u1, d0, d1]
+    sources += [x_ref.at[pl.ds(i * tile, tile)] for i in range(1, tiles)]
+    targets += [x_held.at[i] for i in range(1, tiles)]
+    copies = fetched(sources, targets, sem)
+    for i in range(tiles):
+        copies[7 + i - 1 if i else 0].wait()
+        x = x_held[i]
+        hidden = []
+        for k, (g, u) in enumerate(((g0, u0), (g1, u1))):
+            if i == 0:
+                copies[1 + 2 * k].wait()
+            gate = dot(x, g[...])
+            if i == 0:
+                copies[2 + 2 * k].wait()
+            hidden.append((silu(gate) * dot(x, u[...])).astype(BF16))
+        if i == 0:
+            copies[5].wait()
+            copies[6].wait()
+        for j in range(0, out_ref.shape[1], 512):
+            total = dot(hidden[0], d0[:, j : j + 512]) + dot(hidden[1], d1[:, j : j + 512])
+            out_ref[i * tile : (i + 1) * tile, j : j + 512] = total.astype(BF16)
+
+
 def weigh_kernel(got_ref, share_ref, out_ref):
     total = got_ref[0].astype(F32)
     for i in range(1, got_ref.shape[0]):
@@ -199,13 +236,13 @@
     out_ref[0] = (total * share_ref[:, :1]).astype(BF16)
 
 
-def combine_kernel(res_ref, got_ref, slots_ref, out_ref):
-    total = res_ref[...]
+def combine_kernel(got_ref, slots_ref, out_ref):
+    total = jnp.zeros(out_ref.shape, F32)
     for e in range(got_ref.shape[0]):
         total = total + lax.dot_general(
             slots_ref[e], got_ref[e], (((0,), (0,)), ((), ())), preferred_element_type=F32
         )
-    out_ref[...] = total
+    out_ref[...] = total.astype(BF16)
 
 
 def shape(dims, dtype=F32):
@@ -242,48 +279,60 @@
     place = lax.axis_index("seq").astype(jnp.int32)
     owner = lax.axis_index("expert").astype(jnp.int32)
 
-    swap = [(i, i ^ 1) for i in range(n_seq)]
-    gate_w, up_w, down_w = specialist_switch_matrix[0], w_up[0], w_down[0]
-    gate_o, up_o, down_o = (lax.ppermute(w, "seq", swap) for w in (gate_w, up_w, down_w))
+    near = [(i, i ^ 1) for i in range(n_seq)]
+    weights = (specialist_switch_matrix[0], w_up[0], w_down[0])
+    others = tuple(lax.ppermute(w, "seq", near) for w in weights)
 
     halo = (taps - 1) * prompts
     x_rows = x_branch.reshape(rows, channels)
     received = lax.ppermute(x_rows[rows - halo :], "seq", [(i, i + 1) for i in range(n_seq - 1)])
+    here = (
+        a_log.T, carry_state.transpose(0, 2, 1), gate_branch.reshape(rows, channels),
+        layer_input.reshape(own_rows, d_model), jnp.stack([place, owner]),
+    )
+
     activated, part = call(
         conv_kernel,
         (shape((rows, channels)), shape((rows, x_proj.shape[1]))),
         [SCALAR] + [VM] * 6,
         [pltpu.VMEM((rows + 8, channels), F32)],
         name="conv",
-    )(place[None], x_rows, received, carry_tail.reshape(halo, channels), conv_weight, conv_bias[None], x_proj)
+    )(place[None], x_rows, received, carry_tail.reshape(halo, channels), conv_weight, conv_bias[None], x_proj.T)
+    part, activated, *here = fence(part, activated, *here)
     summed = exchanged(part, "expert").reshape(groups, own_rows, part.shape[1]).sum(axis=0)
+    summed, activated, *here = fence(summed, activated, *here)
     projected = exchanged(jnp.tile(summed, (groups, 1)), "expert")
+    projected, activated, *rest = fence(projected, activated, *here, *others)
+    (a_log_t, carry_t, gate_rows, own, spot), others = rest[:-3], rest[-3:]
     bc = jnp.broadcast_to(projected[:, rank:, None], (rows, 2 * states, 128))
-    a_log_t = a_log.T
     step, ends = call(
         functools.partial(local_kernel, prompts),
         (shape((rows, channels)), shape((prompts * states + 8, channels), BF16)),
         [VM] * 6,
         name="local",
     )(projected, dt_proj, dt_bias[None], activated, bc, a_log_t)
-    every = exchanged(jnp.broadcast_to(ends[None], (n_seq,) + ends.shape), "seq")
+    ends, step, bc = fence(jnp.broadcast_to(ends[None], (n_seq,) + ends.shape), step, bc)
+    every = exchanged(ends, "seq")
+    every, step, bc, activated, a_log_t, carry_t, gate_rows, own = fence(
+        every, step, bc, activated, a_log_t, carry_t, gate_rows, own
+    )
     mixed = call(
         functools.partial(scan_kernel, prompts),
         shape((groups, rows, width), BF16),
         [SCALAR] + [VM] * 9 + [pl.BlockSpec(memory_space=pl.ANY)],
         [pltpu.VMEM((rows, channels), F32), pltpu.VMEM((channels, d_model), BF16), pltpu.SemaphoreType.DMA],
         name="scan",
-    )(
-        jnp.stack([place, owner]), every, carry_state.transpose(0, 2, 1), step, activated, bc, a_log_t, d_skip[None],
-        gate_branch.reshape(rows, channels), layer_input.reshape(own_rows, d_model), out_proj,
-    )
+    )(spot, every, carry_t, step, activated, bc, a_log_t, d_skip[None], gate_rows, own, out_proj)
+    mixed, steering, refusal, norm_gain, expert_ids = fence(mixed, steering, refusal, norm_gain, expert_ids)
     mixed = exchanged(mixed, "expert")
-
     clean = call(clean_kernel, shape((d_model // 128, 128)), [VM] * 2, name="clean")(
         steering.reshape(-1, 128), refusal.reshape(refusal.shape[0], -1, 128)
     )
     start = owner * width
+    clean = lax.dynamic_slice_in_dim(clean.reshape(1, d_model), start, width, 1)
+    gain = lax.dynamic_slice_in_dim(norm_gain[None], start, width, 1)
     ids = expert_ids.reshape(rows, top_count)
+
     residual, send, slots = call(
         dispatch_kernel,
         (
@@ -293,12 +342,7 @@
         ),
         [VM] * 4,
         name="dispatch",
-    )(
-        mixed,
-        lax.dynamic_slice_in_dim(clean.reshape(1, d_model), start, width, 1),
-        lax.dynamic_slice_in_dim(norm_gain[None], start, width, 1),
-        ids.T,
-    )
+    )(mixed, clean, gain, ids.T)
     got = exchanged(send, "expert")
     normed = call(
         functools.partial(normed_kernel, float(d_model)), shape((capacity, d_model), BF16), [VM], name="normed"
@@ -309,11 +353,26 @@
     share = call(share_kernel, shape((capacity, 128)), [SCALAR] + [VM] * 4, name="share")(
         owner[None], normed, router.T, slots, ids
     )
-    gate = dot(pieces, jnp.concatenate([gate_w, gate_o], axis=1))
-    upward = dot(pieces, jnp.concatenate([up_w, up_o], axis=1))
-    hidden = (jax.nn.silu(gate) * upward).astype(BF16)
-    partial = dot(hidden, jnp.concatenate([down_w, down_o], axis=0)).astype(BF16)
+    residual, share = fence(residual, share)
+    own_residual = exchanged(residual, "expert").reshape(groups, own_rows, width)
+    hbm = pl.BlockSpec(memory_space=pltpu.HBM)
+    pieces, own_residual, share = fence(pieces, own_residual, share)
+    held = (weights[0], weights[1], others[0], others[1], weights[2], others[2])
+    tiles = 2
+    partial = pl.pallas_call(
+        expert_kernel,
+        out_shape=pltpu.VMEM(pieces.shape, BF16),
+        in_specs=[hbm] * (1 + len(held)),
+        out_specs=VM,
+        scratch_shapes=[pltpu.VMEM((tiles, pieces.shape[0] // tiles, d_model), BF16)]
+        + [pltpu.VMEM(w.shape, BF16) for w in held]
+        + [pltpu.SemaphoreType.DMA((tiles + len(held),))],
+        compiler_params=pltpu.CompilerParams(vmem_limit_bytes=54 * 1024 * 1024),
+        name="expert",
+    )(pieces, *held)
+    partial, share, slots, own_residual = fence(partial, share, slots, own_residual)
     partial = exchanged(partial, "seq", same_core).reshape(n_seq // 2, capacity, d_model)
+    partial, share, slots, own_residual = fence(partial, share, slots, own_residual)
     weighted = pl.pallas_call(
         weigh_kernel,
         grid=(groups,),
@@ -327,8 +386,9 @@
         name="weigh",
     )(partial, share)
     back = exchanged(weighted, "expert")
-    total = call(combine_kernel, shape((rows, width)), [VM] * 3, name="combine")(residual, back, slots)
+    total = call(combine_kernel, shape((rows, width), BF16), [VM] * 2, name="combine")(back, slots)
     out = exchanged(total, "expert").reshape(groups, own_rows, width)
+    out = own_residual + out.astype(F32)
     return out.transpose(1, 0, 2).reshape(own_rows // prompts, prompts, d_model)
 
 

time: 347 us -> 312 us (0.90)
  blocking collectives: 83.1 us -> 188 us
  waiting for transfers between devices: 171 us -> 66.7 us
  matrix products: 20.5 us -> 0 us
  starting transfers between devices: 20 us -> 6.66 us
  Pallas kernels: 14.7 us -> 26.2 us
  local copies, waits for them, and re-layouts: 19.7 us -> 9.48 us
    all_to_all x5 -> x8, blocking collectives: 83.1 us -> 188 us  [exchanged(): lax.all_to_all(blocks, axis, 0, 0, tiled=True, axis_index_groups=groups)]
    all_to_all x3 -> x1, waiting for transfers between devices: 116 us -> 27 us  [exchanged(): lax.all_to_all(blocks, axis, 0, 0, tiled=True, axis_index_groups=groups)]
    dot_general x2 -> x0, matrix products: 20.5 us -> none  [dot(): return jnp.dot(a, b, preferred_element_type=F32)]
    pallas_call x1 -> x2, Pallas kernels: 0.46 us -> 14.7 us  [the longest x1 14.3 us: shards(): pl.pallas_call(expert_kernel, out_shape=pltpu.VMEM(pieces.shape, BF16), i...]
    all_to_all x3 -> x1, starting transfers between devices: 17.3 us -> 3.7 us  [exchanged(): lax.all_to_all(blocks, axis, 0, 0, tiled=True, axis_index_groups=groups)]
    all_gather x1, waiting for transfers between devices: 51.3 us -> 39.7 us  [shards(): lax.all_gather(normed, 'seq', axis=0, tiled=True, axis_index_groups=same_...]
    unnamed x41 -> x27, local copies, waits for them, and re-layouts: 10.3 us -> 1.71 us
    ppermute x3, waiting for transfers between devices: 3.89 us -> 0.01 us  [shards(): others = tuple((lax.ppermute(w, 'seq', near) for w in weights))]
  transfers between devices with their start and end apart: 8 -> 6, of which waited for: 5 -> 2; matrix products, arithmetic and copies ran while one was open for 4% -> 2% of each run, Pallas kernels for 1% -> 1%
where the time goes in v2:
time: 312 us; the launch traced here: 311 us
  blocking collectives  188 us (60%)
  waiting for transfers between devices  66.7 us (21%)
  Pallas kernels  26.2 us (8%)
  between operations  13.7 us (4%)
  local copies, waits for them, and re-layouts  9.48 us (3%)
  starting transfers between devices  6.66 us (2%)
    all_to_all x8, blocking collectives, exchanged(): lax.all_to_all(blocks, axis, 0, 0, tiled=True, axis_index_groups=groups)  188 us
    all_gather x1, waiting for transfers between devices, shards(): lax.all_gather(normed, 'seq', axis=0, tiled=True, axis_index_groups=same_...  39.7 us
    all_to_all x1, waiting for transfers between devices, exchanged(): lax.all_to_all(blocks, axis, 0, 0, tiled=True, axis_index_groups=groups)  27 us
    pallas_call x1, Pallas kernels, shards(): pl.pallas_call(expert_kernel, out_shape=pltpu.VMEM(pieces.shape, BF16), i...  14.3 us
  transfers between devices with their start and end apart: 6, of which 2 were waited for; matrix products, arithmetic and copies ran while one was open for 2% of the time, Pallas kernels for 1%

profile of v2, /device:TPU:2, one launch (start us, length us, event | category | flops | bytes accessed | tf_op | source)
XLA Modules:
  0.0 311.4 jit_solution(6855932508741984172)
XLA Ops:
  6.5 0.5 collective-permute-start.2
  7.0 0.7 slice.9
  7.8 2.4 collective-permute-start
  10.3 1.0 reshape.54.x_ref
  11.2 0.7 broadcast_in_dim.13.b_ref
  11.9 0.7 reshape.55.carry_ref
  12.6 1.0 reshape.57.own_ref
  13.6 1.0 reshape.56.gate_ref
  14.6 1.0 copy-done.1
  15.6 0.7 copy-done.7
  16.6 20.0 %all_to_all.65 = f32[8,16,288]{2,1,0:T(8,128)S(1)} all-to-all(f32[8,16,288]{2,1,0:T(8,128)S(1)} %bitcast.35), channel_id=1, replica_groups=mesh['seq'=32,'expert'=8] {'expert'}, dimensions={0} | all-to-all | bytes 294912 | tf_op jit(solution)/shard_map/all_to_all | solution.py:30
  36.7 13.4 %all_to_all.66 = f32[8,16,288]{2,1,0:T(8,128)S(1)} all-to-all(f32[8,16,288]{2,1,0:T(8,128)S(1)} %tile.2), channel_id=1, replica_groups=mesh['seq'=32,'expert'=8] {'expert'}, dimensions={0} | all-to-all | bytes 294912 | tf_op jit(solution)/shard_map/all_to_all | solution.py:30
  50.1 0.6 broadcast_in_dim.29.bc_ref
  50.8 1.2 local.1
  52.1 26.0 %all_to_all.67.all_ref = bf16[32,40,512]{2,1,0:T(8,128)(2,1)S(1)} all-to-all(bf16[32,40,512]{2,1,0:T(8,128)(2,1)S(1)} %broadcast_in_dim.30), channel_id=1, replica_groups=mesh['seq'=32,'expert'=8] {'seq'}, dimensions={0} | all-to-all | bytes 2621440 | tf_op jit(solution)/shard_map/all_to_all | solution.py:30
  78.2 4.4 %scan.1 = bf16[8,128,512]{2,1,0:T(8,128)(2,1)} custom-call(s32[2]{0:T(128)S(1)} %pad_add_fusion.ids_ref, bf16[32,40,512]{2,1,0:T(8,128)(2,1)S(1)} %all_to_all.67.all_ref, f32[2,16,512]{2,1,0:T(8,128)S(1)} %bitcast.39, f32[128,512]{1,0:T(8,128)S(1)} %get-tuple-element.95.step_ref, f32[128,512]{1,0:T(8,128)S(1)} %get-tuple-element.96.act_ref, ...), custom_call_target="tpu_custom_call" | custom-call | tf_op jit(solution)/shard_map/scan/pallas_call | solution.py:319
  82.6 3.7 %all-to-all-start.3 = ((bf16[8,128,512]{2,1,0:T(8,128)(2,1)}), bf16[8,128,512]{2,1,0:T(8,128)(2,1)S(1)}, u32[]{:S(2)}, u32[]{:S(2)}) async-start(bf16[8,128,512]{2,1,0:T(8,128)(2,1)} %scan.1), calls=%async_computation.3 | async-start | bytes 2097152 | tf_op jit(solution)/shard_map/all_to_all | solution.py:30
  86.3 0.8 dynamic-slice.3
  87.3 1.5 clean.1
  88.9 27.0 %all-to-all-done.3.mixed_ref = bf16[8,128,512]{2,1,0:T(8,128)(2,1)S(1)} async-done(((bf16[8,128,512]{2,1,0:T(8,128)(2,1)}), bf16[8,128,512]{2,1,0:T(8,128)(2,1)S(1)}, u32[]{:S(2)}, u32[]{:S(2)}) %all-to-all-start.3) | async-done | bytes 1048608 | tf_op jit(solution)/shard_map/all_to_all | solution.py:30
  115.9 0.6 dispatch.1
  116.5 17.9 %all_to_all.68.got_ref = bf16[8,40,640]{2,1,0:T(8,128)(2,1)S(1)} all-to-all(bf16[8,40,640]{2,1,0:T(8,128)(2,1)S(1)} %get-tuple-element.106), channel_id=1, replica_groups=mesh['seq'=32,'expert'=8] {'expert'}, dimensions={0} | all-to-all | bytes 819200 | tf_op jit(solution)/shard_map/all_to_all | solution.py:30
  134.4 0.9 normed.1.x_ref
  135.3 1.3 share.1.share_ref
  136.6 14.7 %all_to_all.69 = f32[8,16,512]{2,1,0:T(8,128)S(1)} all-to-all(f32[8,16,512]{2,1,0:T(8,128)S(1)} %bitcast.34), channel_id=1, replica_groups=mesh['seq'=32,'expert'=8] {'expert'}, dimensions={0} | all-to-all | bytes 524288 | tf_op jit(solution)/shard_map/all_to_all | solution.py:30
  151.3 39.7 %all-gather.2.cloned.1.call-done.x_ref = bf16[640,4096]{1,0:T(8,128)(2,1)} async-done(((bf16[40,4096]{1,0:T(8,128)(2,1)}), bf16[640,4096]{1,0:T(8,128)(2,1)}) %all-gather.2.cloned.1.call-update) | async-done | bytes 5242896 | tf_op jit(solution)/shard_map/all_gather | solution.py:352
  191.0 14.3 %expert.1 = bf16[640,4096]{1,0:T(8,128)(2,1)S(1)} custom-call(bf16[640,4096]{1,0:T(8,128)(2,1)} %all-gather.2.cloned.1.call-done.x_ref, bf16[4096,256]{1,0:T(8,128)(2,1)} %bitcast.46, bf16[4096,256]{1,0:T(8,128)(2,1)} %bitcast.48, bf16[4096,256]{1,0:T(8,128)(2,1)} %copy-done.10, bf16[4096,256]{1,0:T(8,128)(2,1)} %collective-permute-done.2.u1_ref, ...), custom_call_target="tpu_custom_call" | custom-call | tf_op jit(solution)/shard_map/expert/pallas_call | solution.py:362
  205.3 66.2 %all_to_all.70.got_ref = bf16[16,40,4096]{2,1,0:T(8,128)(2,1)S(1)} all-to-all(bf16[16,40,4096]{2,1,0:T(8,128)(2,1)S(1)} %bitcast.27), channel_id=1, replica_groups={{0,16,32,48,64,80,96,112,128,144,160,176,192,208,224,240},{8,24,40,56,7..., dimensions={0} | all-to-all | bytes 10485760 | tf_op jit(solution)/shard_map/all_to_all | solution.py:30
  271.5 1.2 weigh.1
  272.7 18.7 %all_to_all.71.got_ref = bf16[8,40,512]{2,1,0:T(8,128)(2,1)S(1)} all-to-all(bf16[8,40,512]{2,1,0:T(8,128)(2,1)S(1)} %weigh.1), channel_id=1, replica_groups=mesh['seq'=32,'expert'=8] {'expert'}, dimensions={0} | all-to-all | bytes 655360 | tf_op jit(solution)/shard_map/all_to_all | solution.py:30
  291.9 11.5 %all_to_all.72 = bf16[8,16,512]{2,1,0:T(8,128)(2,1)S(1)} all-to-all(bf16[8,16,512]{2,1,0:T(8,128)(2,1)S(1)} %bitcast.32), channel_id=1, replica_groups=mesh['seq'=32,'expert'=8] {'expert'}, dimensions={0} | all-to-all | bytes 262144 | tf_op jit(solution)/shard_map/all_to_all | solution.py:30
  303.6 0.9 reshape.62
  (47 shorter events, 1.5 us)
Async XLA Ops:
  6.5 43.6 %collective-permute-start.1 = (bf16[4096,256]{1,0:T(8,128)(2,1)}, bf16[4096,256]{1,0:T(8,128)(2,1)S(1)}, u32[]{:S(2)}, u32[]{:S(2)}) collective-permute-start(bf16[4096,256]{1,0:T(8,128)(2,1)} %bitcast.45), channel_id=1, source_target_pairs={{0,8},{8,0},{16,24},{24,16},{32,40},{40,32},{48,56},{56,48},{64,72... | collective-permute-start | bytes 6291464 | tf_op jit(solution)/shard_map/ppermute | solution.py:284
  6.5 43.6 %collective-permute-start.2 = (bf16[4096,256]{1,0:T(8,128)(2,1)}, bf16[4096,256]{1,0:T(8,128)(2,1)}, u32[]{:S(2)}, u32[]{:S(2)}) collective-permute-start(bf16[4096,256]{1,0:T(8,128)(2,1)} %bitcast.47), channel_id=1, source_target_pairs={{0,8},{8,0},{16,24},{24,16},{32,40},{40,32},{48,56},{56,48},{64,72... | collective-permute-start | bytes 6291464 | tf_op jit(solution)/shard_map/ppermute | solution.py:284
  7.0 43.1 %collective-permute-start.3 = (bf16[256,4096]{1,0:T(8,128)(2,1)}, bf16[256,4096]{1,0:T(8,128)(2,1)}, u32[]{:S(2)}, u32[]{:S(2)}) collective-permute-start(bf16[256,4096]{1,0:T(8,128)(2,1)} %bitcast.49), channel_id=1, source_target_pairs={{0,8},{8,0},{16,24},{24,16},{32,40},{40,32},{48,56},{56,48},{64,72... | collective-permute-start | bytes 6291464 | tf_op jit(solution)/shard_map/ppermute | solution.py:284
  7.8 6.8 %collective-permute-start = (bf16[6,512]{1,0:T(8,128)(2,1)S(1)}, bf16[6,512]{1,0:T(8,128)(2,1)S(1)}, u32[]{:S(2)}, u32[]{:S(2)}) collective-permute-start(bf16[6,512]{1,0:T(8,128)(2,1)S(1)} %slice.10), channel_id=1, source_target_pairs={{0,8},{8,16},{16,24},{24,32},{32,40},{40,48},{48,56},{56,64},{64,7... | collective-permute-start | bytes 18440 | tf_op jit(solution)/shard_map/ppermute | solution.py:288
  12.6 38.1 %copy-start.3 = (f32[512,16]{0,1:T(8,128)S(1)}, f32[512,16]{0,1:T(8,128)}, u32[]{:S(2)}) copy-start(f32[512,16]{0,1:T(8,128)} %param.29) | copy-start | bytes 98308
  12.6 38.1 %copy-start.8 = (f32[512]{0:T(512)S(1)}, f32[512]{0:T(512)}, u32[]{:S(2)}) copy-start(f32[512]{0:T(512)} %param.28) | copy-start | bytes 6148
  13.6 37.2 %copy-start.2 = (bf16[256,512]{1,0:T(8,128)(2,1)S(1)}, bf16[256,512]{1,0:T(8,128)(2,1)}, u32[]{:S(2)}) copy-start(bf16[256,512]{1,0:T(8,128)(2,1)} %dtp_ref.1) | copy-start | bytes 786436
  14.6 1.0 copy-start.1
  15.6 0.7 copy-start.7
  50.1 1.9 copy-start.10
  50.8 27.4 %copy-start = (bf16[512,4096]{1,0:T(8,128)(2,1)S(1)}, bf16[512,4096]{1,0:T(8,128)(2,1)}, u32[]{:S(2)}) copy-start(bf16[512,4096]{1,0:T(8,128)(2,1)} %outp_ref.1) | copy-start | bytes 12582916
  52.0 26.1 %copy-start.4 = (f32[2,512,16]{1,2,0:T(8,128)S(1)}, f32[2,512,16]{1,2,0:T(8,128)}, u32[]{:S(2)}) copy-start(f32[2,512,16]{1,2,0:T(8,128)} %param.31) | copy-start | bytes 196612
  52.0 26.1 %copy-start.9 = (f32[512]{0:T(512)S(1)}, f32[512]{0:T(512)}, u32[]{:S(2)}) copy-start(f32[512]{0:T(512)} %param.30) | copy-start | bytes 6148
  82.5 4.6 %copy-start.11 = (bf16[4,4096]{1,0:T(4,128)(2,1)S(1)}, bf16[4,4096]{1,0:T(4,128)(2,1)}, u32[]{:S(2)}) copy-start(bf16[4,4096]{1,0:T(4,128)(2,1)} %param.35) | copy-start | bytes 98308
  82.5 4.6 %copy-start.12 = (s32[64,2,2]{0,2,1:T(2,128)S(1)}, s32[64,2,2]{0,2,1:T(2,128)}, u32[]{:S(2)}) copy-start(s32[64,2,2]{0,2,1:T(2,128)} %param.41) | copy-start | bytes 3076
  82.6 4.8 %copy-start.6 = (bf16[4096]{0:T(1024)(128)(2,1)S(1)}, bf16[4096]{0:T(1024)(128)(2,1)}, u32[]{:S(2)}) copy-start(bf16[4096]{0:T(1024)(128)(2,1)} %param.34) | copy-start | bytes 24580
  82.6 33.3 %all-to-all-start.3 = ((bf16[8,128,512]{2,1,0:T(8,128)(2,1)}), bf16[8,128,512]{2,1,0:T(8,128)(2,1)S(1)}, u32[]{:S(2)}, u32[]{:S(2)}) async-start(bf16[8,128,512]{2,1,0:T(8,128)(2,1)} %scan.1), calls=%async_computation.3 | async-start | bytes 2097152 | tf_op jit(solution)/shard_map/all_to_all | solution.py:30
  86.3 49.0 %copy-start.5 = (bf16[4096,8]{0,1:T(8,128)(2,1)S(1)}, bf16[4096,8]{0,1:T(8,128)(2,1)}, u32[]{:S(2)}) copy-start(bf16[4096,8]{0,1:T(8,128)(2,1)} %param.37) | copy-start | bytes 196612
  86.3 104.7 %all-gather.2.cloned.1.call-start = ((), (), s32[]{:S(2)}) async-start(), calls=%async_computation.9 | async-start | bytes 5570560 | tf_op jit(solution)/shard_map/all_gather | solution.py:352
Sparse Core Ops, SparseCore 0:
  135.4 55.5 all-gather.1

commit v3 on v2

--- a/solution.py
+++ b/solution.py
@@ -203,30 +203,52 @@
     return copies
 
 
-def expert_kernel(x_ref, g0_ref, u0_ref, g1_ref, u1_ref, d0_ref, d1_ref, out_ref, x_held, g0, u0, g1, u1, d0, d1, sem):
-    tiles, tile, _ = x_held.shape
-    sources = [x_ref.at[pl.ds(0, tile)], g0_ref, u0_ref, g1_ref, u1_ref, d0_ref, d1_ref]
-    targets = [x_held.at[0], g0, u0, g1, u1, d0, d1]
-    sources += [x_ref.at[pl.ds(i * tile, tile)] for i in range(1, tiles)]
-    targets += [x_held.at[i] for i in range(1, tiles)]
+def gathered_half(x_ref, held_ref, sem, parity):
+    pairs, _, capacity, _ = x_ref.shape
+    copies = [pltpu.make_async_copy(x_ref.at[i, parity], held_ref.at[i], sem.at[i]) for i in range(pairs)]
+    for copy in copies:
+        copy.start()
+    return copies
+
+
+def first_kernel(parity_ref, x_ref, g0_ref, u0_ref, g1_ref, u1_ref, out_ref, own_ref, g0, u0, g1, u1, x_held, sems, sem):
+    theirs = gathered_half(x_ref, x_held, sems.at[0], 1 - parity_ref[0])
+    copies = fetched((g0_ref, u0_ref, g1_ref, u1_ref), (g0, u0, g1, u1), sem)
+    ours = gathered_half(x_ref, own_ref, sems.at[1], parity_ref[0])
+    for copy in theirs:
+        copy.wait()
+    x = x_held[...].reshape(out_ref.shape[0], -1)
+    width = g0.shape[1]
+    for k, (g, u) in enumerate(((g0, u0), (g1, u1))):
+        copies[2 * k].wait()
+        gate = dot(x, g[...])
+        copies[2 * k + 1].wait()
+        out_ref[:, k * width : (k + 1) * width] = (silu(gate) * dot(x, u[...])).astype(BF16)
+    for copy in ours:
+        copy.wait()
+
+
+def second_kernel(x_ref, g0, u0, g1, u1, *refs):
+    sources, out_ref, held, sem = refs[:6], refs[6], refs[7:11], refs[11]
+    part = sources[2].shape[0]
+    targets = held[:2] + tuple(d.at[pl.ds(k * part, part)] for d in held[2:] for k in range(2))
     copies = fetched(sources, targets, sem)
-    for i in range(tiles):
-        copies[7 + i - 1 if i else 0].wait()
-        x = x_held[i]
-        hidden = []
-        for k, (g, u) in enumerate(((g0, u0), (g1, u1))):
-            if i == 0:
-                copies[1 + 2 * k].wait()
-            gate = dot(x, g[...])
-            if i == 0:
-                copies[2 + 2 * k].wait()
-            hidden.append((silu(gate) * dot(x, u[...])).astype(BF16))
-        if i == 0:
-            copies[5].wait()
-            copies[6].wait()
-        for j in range(0, out_ref.shape[1], 512):
-            total = dot(hidden[0], d0[:, j : j + 512]) + dot(hidden[1], d1[:, j : j + 512])
-            out_ref[i * tile : (i + 1) * tile, j : j + 512] = total.astype(BF16)
+    x = x_ref[...].reshape(out_ref.shape[0], -1)
+    width = g0.shape[1]
+    for k, (g, u) in enumerate(((g0, u0), (g1, u1))):
+        out_ref[:, k * width : (k + 1) * width] = (silu(dot(x, g[...])) * dot(x, u[...])).astype(BF16)
+    for copy in copies:
+        copy.wait()
+
+
+def down_kernel(own_ref, far_ref, d0, d1, d2, d3, out_ref):
+    width = d0.shape[0]
+    hidden = [ref[:, k * width : (k + 1) * width] for ref in (own_ref, far_ref) for k in range(2)]
+    for j in range(0, out_ref.shape[1], 512):
+        total = dot(hidden[0], d0[:, j : j + 512])
+        for h, d in zip(hidden[1:], (d1, d2, d3)):
+            total = total + dot(h, d[:, j : j + 512])
+        out_ref[:, j : j + 512] = total.astype(BF16)
 
 
 def weigh_kernel(got_ref, share_ref, out_ref):
@@ -279,7 +301,7 @@
     place = lax.axis_index("seq").astype(jnp.int32)
     owner = lax.axis_index("expert").astype(jnp.int32)
 
-    near = [(i, i ^ 1) for i in range(n_seq)]
+    near, across = ([(i, i ^ d) for i in range(n_seq)] for d in (1, 2))
     weights = (specialist_switch_matrix[0], w_up[0], w_down[0])
     others = tuple(lax.ppermute(w, "seq", near) for w in weights)
 
@@ -313,9 +335,11 @@
     )(projected, dt_proj, dt_bias[None], activated, bc, a_log_t)
     ends, step, bc = fence(jnp.broadcast_to(ends[None], (n_seq,) + ends.shape), step, bc)
     every = exchanged(ends, "seq")
-    every, step, bc, activated, a_log_t, carry_t, gate_rows, own = fence(
-        every, step, bc, activated, a_log_t, carry_t, gate_rows, own
-    )
+    every, step, bc, activated, a_log_t, carry_t, gate_rows, own, down_w = fence(
+        every, step, bc, activated, a_log_t, carry_t, gate_rows, own, weights[2]
+    )
+    part = down_w.shape[0] // 2
+    far_a, far_b = (lax.ppermute(down_w[k * part : (k + 1) * part], "seq", across) for k in range(2))
     mixed = call(
         functools.partial(scan_kernel, prompts),
         shape((groups, rows, width), BF16),
@@ -349,36 +373,64 @@
     )(got)
 
     same_core = [[i for i in range(n_seq) if i % 2 == c] for c in range(2)]
+    normed, far_a = fence(normed, far_a)
+    corner_a = lax.ppermute(far_a, "seq", near)
     pieces = lax.all_gather(normed, "seq", axis=0, tiled=True, axis_index_groups=same_core)
     share = call(share_kernel, shape((capacity, 128)), [SCALAR] + [VM] * 4, name="share")(
         owner[None], normed, router.T, slots, ids
     )
     residual, share = fence(residual, share)
     own_residual = exchanged(residual, "expert").reshape(groups, own_rows, width)
+    own_residual, share, far_b = fence(own_residual, share, far_b)
+    corner_b = lax.ppermute(far_b, "seq", near)
     hbm = pl.BlockSpec(memory_space=pltpu.HBM)
-    pieces, own_residual, share = fence(pieces, own_residual, share)
-    held = (weights[0], weights[1], others[0], others[1], weights[2], others[2])
-    tiles = 2
+    pieces, own_residual, share, corner_a, corner_b = fence(pieces, own_residual, share, corner_a, corner_b)
+    pairs = n_seq // 4
+    pieces = pieces.reshape(pairs, 2, capacity, d_model)
+    ups = (weights[0], weights[1], others[0], others[1])
+    downs = (down_w, others[2], far_a, far_b, corner_a, corner_b)
+    half = pairs * capacity
+    inner = 2 * ups[0].shape[1]
+    dma = pltpu.SemaphoreType.DMA
+    theirs, x_own, *ups = pl.pallas_call(
+        first_kernel,
+        out_shape=(shape((half, inner), BF16), pltpu.VMEM((pairs, capacity, d_model), BF16))
+        + tuple(pltpu.VMEM(w.shape, BF16) for w in ups),
+        in_specs=[SCALAR] + [hbm] * 5,
+        out_specs=(VM,) * 6,
+        scratch_shapes=[pltpu.VMEM((pairs, capacity, d_model), BF16), dma((2, pairs)), dma((4,))],
+        compiler_params=pltpu.CompilerParams(vmem_limit_bytes=16 * 1024 * 1024),
+        name="first",
+    )(((place // 2) % 2)[None], *(pltpu.with_memory_space_constraint(v, pltpu.HBM) for v in (pieces, *ups)))
+    given = lax.ppermute(theirs, "seq", across)
+    kept, *downs = pl.pallas_call(
+        second_kernel,
+        out_shape=(shape((half, inner), BF16),) + (pltpu.VMEM(down_w.shape, BF16),) * 4,
+        in_specs=[VM] * 5 + [hbm] * 6,
+        out_specs=(VM,) * 5,
+        scratch_shapes=[dma((6,))],
+        compiler_params=pltpu.CompilerParams(vmem_limit_bytes=16 * 1024 * 1024),
+        cost_estimate=pl.CostEstimate(flops=4 * half * inner * d_model, bytes_accessed=1 << 24, transcendentals=0),
+        name="second",
+    )(x_own, *ups, *(pltpu.with_memory_space_constraint(v, pltpu.HBM) for v in downs))
     partial = pl.pallas_call(
-        expert_kernel,
-        out_shape=pltpu.VMEM(pieces.shape, BF16),
-        in_specs=[hbm] * (1 + len(held)),
+        down_kernel,
+        out_shape=pltpu.VMEM((half, d_model), BF16),
+        in_specs=[VM] * 6,
         out_specs=VM,
-        scratch_shapes=[pltpu.VMEM((tiles, pieces.shape[0] // tiles, d_model), BF16)]
-        + [pltpu.VMEM(w.shape, BF16) for w in held]
-        + [pltpu.SemaphoreType.DMA((tiles + len(held),))],
-        compiler_params=pltpu.CompilerParams(vmem_limit_bytes=54 * 1024 * 1024),
-        name="expert",
-    )(pieces, *held)
+        compiler_params=pltpu.CompilerParams(vmem_limit_bytes=16 * 1024 * 1024),
+        name="down",
+    )(kept, given, *downs)
+    kinds = [[i for i in range(n_seq) if i % 4 == k] for k in range(4)]
     partial, share, slots, own_residual = fence(partial, share, slots, own_residual)
-    partial = exchanged(partial, "seq", same_core).reshape(n_seq // 2, capacity, d_model)
+    partial = exchanged(partial, "seq", kinds).reshape(pairs, capacity, d_model)
     partial, share, slots, own_residual = fence(partial, share, slots, own_residual)
     weighted = pl.pallas_call(
         weigh_kernel,
         grid=(groups,),
         out_shape=shape((groups, capacity, width), BF16),
         in_specs=[
-            pl.BlockSpec((n_seq // 2, capacity, width), lambda j: (0, 0, j)),
+            pl.BlockSpec((pairs, capacity, width), lambda j: (0, 0, j)),
             pl.BlockSpec((capacity, 128), lambda j: (0, 0)),
         ],
         out_specs=pl.BlockSpec((1, capacity, width), lambda j: (j, 0, 0)),

time: 312 us -> 292 us (0.936)
  blocking collectives: 188 us -> 143 us
  waiting for transfers between devices: 66.7 us -> 80.3 us
  starting transfers between devices: 6.66 us -> 14.2 us
    all_to_all x8 -> x7, blocking collectives: 188 us -> 143 us  [exchanged(): lax.all_to_all(blocks, axis, 0, 0, tiled=True, axis_index_groups=groups)]
    ppermute x0 -> x5, waiting for transfers between devices: none -> 30.5 us  [the longest x2 23.7 us: shards(): lax.ppermute(down_w[k * part:(k + 1) * part], 'seq', across)]
    all_gather x1, waiting for transfers between devices: 39.7 us -> 24 us  [shards(): lax.all_gather(normed, 'seq', axis=0, tiled=True, axis_index_groups=same_...]
    all_to_all x1 -> x2, starting transfers between devices: 3.7 us -> 7.76 us  [exchanged(): lax.all_to_all(blocks, axis, 0, 0, tiled=True, axis_index_groups=groups)]
    ppermute x0 -> x5, starting transfers between devices: none -> 3.52 us  [the longest x2 2.78 us: shards(): lax.ppermute(down_w[k * part:(k + 1) * part], 'seq', across)]
    all_to_all x1 -> x2, waiting for transfers between devices: 27 us -> 24 us  [exchanged(): lax.all_to_all(blocks, axis, 0, 0, tiled=True, axis_index_groups=groups)]
    pallas_call x1 -> x3, Pallas kernels: 14.3 us -> 16.7 us  [the longest x1 8.98 us: shards(): pl.pallas_call(first_kernel, out_shape=(shape((half, inner), BF16), pltpu...]
  transfers between devices with their start and end apart: 6 -> 12, of which waited for: 2 -> 6; matrix products, arithmetic and copies ran while one was open for 2% -> 3% of each run, Pallas kernels for 1% -> 3%
where the time goes in v3:
time: 292 us; the launch traced here: 291 us
  blocking collectives  143 us (49%)
  waiting for transfers between devices  80.3 us (28%)
  Pallas kernels  28.5 us (10%)
  starting transfers between devices  14.2 us (5%)
  between operations  13.8 us (5%)
  local copies, waits for them, and re-layouts  11 us (4%)
    all_to_all x7, blocking collectives, exchanged(): lax.all_to_all(blocks, axis, 0, 0, tiled=True, axis_index_groups=groups)  143 us
    all_to_all x2, waiting for transfers between devices, exchanged(): lax.all_to_all(blocks, axis, 0, 0, tiled=True, axis_index_groups=groups)  24 us
    all_gather x1, waiting for transfers between devices, shards(): lax.all_gather(normed, 'seq', axis=0, tiled=True, axis_index_groups=same_...  24 us
    ppermute x2, waiting for transfers between devices, shards(): lax.ppermute(down_w[k * part:(k + 1) * part], 'seq', across)  23.7 us
    pallas_call x1, Pallas kernels, shards(): pl.pallas_call(first_kernel, out_shape=(shape((half, inner), BF16), pltpu...  8.98 us
    all_to_all x2, starting transfers between devices, exchanged(): lax.all_to_all(blocks, axis, 0, 0, tiled=True, axis_index_groups=groups)  7.76 us
  transfers between devices with their start and end apart: 12, of which 6 were waited for; matrix products, arithmetic and copies ran while one was open for 3% of the time, Pallas kernels for 3%

profile of v3, /device:TPU:2, one launch (start us, length us, event | category | flops | bytes accessed | tf_op | source)
XLA Modules:
  0.0 291.4 jit_solution(2563742796109886890)
XLA Ops:
  7.8 2.4 collective-permute-start
  10.3 1.0 reshape.57.x_ref
  12.6 1.0 reshape.60.own_ref
  13.6 1.0 reshape.59.gate_ref
  14.6 1.7 collective-permute-done.got_ref
  16.3 1.0 copy-done.1
  18.3 19.3 %all_to_all.65 = f32[8,16,288]{2,1,0:T(8,128)S(1)} all-to-all(f32[8,16,288]{2,1,0:T(8,128)S(1)} %bitcast.36), channel_id=1, replica_groups=mesh['seq'=32,'expert'=8] {'expert'}, dimensions={0} | all-to-all | bytes 294912 | tf_op jit(solution)/shard_map/all_to_all | solution.py:30
  37.7 12.3 %all_to_all.66 = f32[8,16,288]{2,1,0:T(8,128)S(1)} all-to-all(f32[8,16,288]{2,1,0:T(8,128)S(1)} %tile.2), channel_id=1, replica_groups=mesh['seq'=32,'expert'=8] {'expert'}, dimensions={0} | all-to-all | bytes 294912 | tf_op jit(solution)/shard_map/all_to_all | solution.py:30
  50.7 1.2 local.1
  52.1 26.3 %all_to_all.67.all_ref = bf16[32,40,512]{2,1,0:T(8,128)(2,1)S(1)} all-to-all(bf16[32,40,512]{2,1,0:T(8,128)(2,1)S(1)} %broadcast_in_dim.34), channel_id=1, replica_groups=mesh['seq'=32,'expert'=8] {'seq'}, dimensions={0} | all-to-all | bytes 2621440 | tf_op jit(solution)/shard_map/all_to_all | solution.py:30
  78.4 4.3 %scan.1 = bf16[8,128,512]{2,1,0:T(8,128)(2,1)} custom-call(s32[2]{0:T(128)S(1)} %pad_add_fusion.ids_ref, bf16[32,40,512]{2,1,0:T(8,128)(2,1)S(1)} %all_to_all.67.all_ref, f32[2,16,512]{2,1,0:T(8,128)S(1)} %bitcast.40, f32[128,512]{1,0:T(8,128)S(1)} %get-tuple-element.114.step_ref, f32[128,512]{1,0:T(8,128)S(1)} %get-tuple-element.115.act_ref, ...), custom_call_target="tpu_custom_call" | custom-call | tf_op jit(solution)/shard_map/scan/pallas_call | solution.py:343
  82.8 3.7 %all-to-all-start.3 = ((bf16[8,128,512]{2,1,0:T(8,128)(2,1)}), bf16[8,128,512]{2,1,0:T(8,128)(2,1)S(1)}, u32[]{:S(2)}, u32[]{:S(2)}) async-start(bf16[8,128,512]{2,1,0:T(8,128)(2,1)} %scan.1), calls=%async_computation.3 | async-start | bytes 2097152 | tf_op jit(solution)/shard_map/all_to_all | solution.py:30
  86.6 1.5 fusion
  88.1 1.4 collective-permute-start.4
  90.5 1.5 clean.1
  92.0 24.0 %all-to-all-done.3.mixed_ref = bf16[8,128,512]{2,1,0:T(8,128)(2,1)S(1)} async-done(((bf16[8,128,512]{2,1,0:T(8,128)(2,1)}), bf16[8,128,512]{2,1,0:T(8,128)(2,1)S(1)}, u32[]{:S(2)}, u32[]{:S(2)}) %all-to-all-start.3) | async-done | bytes 1048608 | tf_op jit(solution)/shard_map/all_to_all | solution.py:30
  116.9 17.9 %all_to_all.68.got_ref = bf16[8,40,640]{2,1,0:T(8,128)(2,1)S(1)} all-to-all(bf16[8,40,640]{2,1,0:T(8,128)(2,1)S(1)} %get-tuple-element.125), channel_id=1, replica_groups=mesh['seq'=32,'expert'=8] {'expert'}, dimensions={0} | all-to-all | bytes 819200 | tf_op jit(solution)/shard_map/all_to_all | solution.py:30
  135.8 1.4 collective-permute-start.5
  137.1 1.3 share.1.share_ref
  138.4 4.1 %all-to-all-start.5 = ((f32[8,16,512]{2,1,0:T(8,128)}), f32[8,16,512]{2,1,0:T(8,128)}, u32[]{:S(2)}, u32[]{:S(2)}) async-start(f32[8,16,512]{2,1,0:T(8,128)} %bitcast.18), calls=%async_computation.5 | async-start | bytes 524288 | tf_op jit(solution)/shard_map/all_to_all | solution.py:30
  142.6 23.7 %collective-permute-done.5.refs_3_ = bf16[128,4096]{1,0:T(8,128)(2,1)S(1)} collective-permute-done((bf16[128,4096]{1,0:T(8,128)(2,1)}, bf16[128,4096]{1,0:T(8,128)(2,1)S(1)}, u32[]{:S(2)}, u32[]{:S(2)}) %collective-permute-start.5) | collective-permute-done | bytes 1048608 | tf_op jit(solution)/shard_map/ppermute | solution.py:342
  166.4 2.7 collective-permute-done.7.refs_5_
  169.1 24.0 %all-gather.2.cloned.1.call-done = bf16[640,4096]{1,0:T(8,128)(2,1)} async-done(((bf16[40,4096]{1,0:T(8,128)(2,1)}), bf16[640,4096]{1,0:T(8,128)(2,1)}) %all-gather.2.cloned.1.call-update) | async-done | bytes 5242896 | tf_op jit(solution)/shard_map/all_gather | solution.py:378
  193.1 9.0 %first.1 = (bf16[320,512]{1,0:T(8,128)(2,1)S(1)}, bf16[8,40,4096]{2,1,0:T(8,128)(2,1)S(1)}, bf16[4096,256]{1,0:T(8,128)(2,1)S(1)}, bf16[4096,256]{1,0:T(8,128)(2...) custom-call(s32[1]{0:T(128)} %bitcast.parity_ref, bf16[8,2,40,4096]{3,2,1,0:T(8,128)(2,1)} %bitcast.49, ...), custom_call_target="tpu_custom_call" | custom-call | tf_op jit(solution)/shard_map/first/pallas_call | solution.py:395
  202.8 4.9 %second.1 = (bf16[320,512]{1,0:T(8,128)(2,1)S(1)}, bf16[256,4096]{1,0:T(8,128)(2,1)S(1)}, bf16[256,4096]{1,0:T(8,128)(2,1)S(1)}, bf16[256,4096]{1,0:T(8,128)(2,1)S(1)}, bf16[256,4096]{1,0:T(8,128)(2,1)S(1)}) custom-call(bf16[8,40,4096]{2,1,0:T(8,128)(2,1)S(1)} %get-tuple-element.139.x_ref, bf16[4096,256]{1,0:T(8,128)(2,1)S(1)} %get-tuple-element.140.g0, ...), custom_call_target="tpu_custom_call" | custom-call | flops 2684354560 | bytes 16777216 | tf_op jit(solution)/shard_map/second/pallas_call | solution.py:406
  207.6 4.0 %collective-permute-done.8.far_ref = bf16[320,512]{1,0:T(8,128)(2,1)S(1)} collective-permute-done((bf16[320,512]{1,0:T(8,128)(2,1)S(1)}, bf16[320,512]{1,0:T(8,128)(2,1)S(1)}, u32[]{:S(2)}, u32[]{:S(2)}) %collective-permute-start.8) | collective-permute-done | bytes 327712 | tf_op jit(solution)/shard_map/ppermute | solution.py:405
  211.7 2.9 down.1
  214.5 37.2 %all_to_all.69.got_ref = bf16[8,40,4096]{2,1,0:T(8,128)(2,1)S(1)} all-to-all(bf16[8,40,4096]{2,1,0:T(8,128)(2,1)S(1)} %bitcast.29), channel_id=1, replica_groups={{0,32,64,96,128,160,192,224},{8,40,72,104,136,168,200,232},{16,48,80,11..., dimensions={0} | all-to-all | bytes 5242880 | tf_op jit(solution)/shard_map/all_to_all | solution.py:30
  252.6 18.0 %all_to_all.70.got_ref = bf16[8,40,512]{2,1,0:T(8,128)(2,1)S(1)} all-to-all(bf16[8,40,512]{2,1,0:T(8,128)(2,1)S(1)} %weigh.1), channel_id=1, replica_groups=mesh['seq'=32,'expert'=8] {'expert'}, dimensions={0} | all-to-all | bytes 655360 | tf_op jit(solution)/shard_map/all_to_all | solution.py:30
  271.1 11.5 %all_to_all.71 = bf16[8,16,512]{2,1,0:T(8,128)(2,1)S(1)} all-to-all(bf16[8,16,512]{2,1,0:T(8,128)(2,1)S(1)} %bitcast.34), channel_id=1, replica_groups=mesh['seq'=32,'expert'=8] {'expert'}, dimensions={0} | all-to-all | bytes 262144 | tf_op jit(solution)/shard_map/all_to_all | solution.py:30
  282.5 1.0 add_bitcast_fusion
  283.7 0.9 reshape.66
  (69 shorter events, 9.5 us)
Async XLA Ops:
  6.5 43.5 %collective-permute-start.1 = (bf16[4096,256]{1,0:T(8,128)(2,1)}, bf16[4096,256]{1,0:T(8,128)(2,1)}, u32[]{:S(2)}, u32[]{:S(2)}) collective-permute-start(bf16[4096,256]{1,0:T(8,128)(2,1)} %bitcast.50), channel_id=1, source_target_pairs={{0,8},{8,0},{16,24},{24,16},{32,40},{40,32},{48,56},{56,48},{64,72... | collective-permute-start | bytes 6291464 | tf_op jit(solution)/shard_map/ppermute | solution.py:306
  6.5 43.5 %collective-permute-start.2 = (bf16[4096,256]{1,0:T(8,128)(2,1)}, bf16[4096,256]{1,0:T(8,128)(2,1)}, u32[]{:S(2)}, u32[]{:S(2)}) collective-permute-start(bf16[4096,256]{1,0:T(8,128)(2,1)} %bitcast.52), channel_id=1, source_target_pairs={{0,8},{8,0},{16,24},{24,16},{32,40},{40,32},{48,56},{56,48},{64,72... | collective-permute-start | bytes 6291464 | tf_op jit(solution)/shard_map/ppermute | solution.py:306
  7.0 43.0 %collective-permute-start.3 = (bf16[256,4096]{1,0:T(8,128)(2,1)}, bf16[256,4096]{1,0:T(8,128)(2,1)S(1)}, u32[]{:S(2)}, u32[]{:S(2)}) collective-permute-start(bf16[256,4096]{1,0:T(8,128)(2,1)} %bitcast.46), channel_id=1, source_target_pairs={{0,8},{8,0},{16,24},{24,16},{32,40},{40,32},{48,56},{56,48},{64,72... | collective-permute-start | bytes 6291464 | tf_op jit(solution)/shard_map/ppermute | solution.py:306
  7.8 8.6 %collective-permute-start = (bf16[6,512]{1,0:T(8,128)(2,1)S(1)}, bf16[6,512]{1,0:T(8,128)(2,1)S(1)}, u32[]{:S(2)}, u32[]{:S(2)}) collective-permute-start(bf16[6,512]{1,0:T(8,128)(2,1)S(1)} %slice.16), channel_id=1, source_target_pairs={{0,8},{8,16},{16,24},{24,32},{32,40},{40,48},{48,56},{56,64},{64,7... | collective-permute-start | bytes 18440 | tf_op jit(solution)/shard_map/ppermute | solution.py:310
  12.6 38.0 %copy-start.3 = (f32[512,16]{0,1:T(8,128)S(1)}, f32[512,16]{0,1:T(8,128)}, u32[]{:S(2)}) copy-start(f32[512,16]{0,1:T(8,128)} %param.29) | copy-start | bytes 98308
  12.6 38.0 %copy-start.8 = (f32[512]{0:T(512)S(1)}, f32[512]{0:T(512)}, u32[]{:S(2)}) copy-start(f32[512]{0:T(512)} %param.28) | copy-start | bytes 6148
  13.6 37.1 %copy-start.2 = (bf16[256,512]{1,0:T(8,128)(2,1)S(1)}, bf16[256,512]{1,0:T(8,128)(2,1)}, u32[]{:S(2)}) copy-start(bf16[256,512]{1,0:T(8,128)(2,1)} %dtp_ref.1) | copy-start | bytes 786436
  16.3 1.0 copy-start.1
  17.3 0.7 copy-start.7
  50.0 1.9 copy-start.11
  50.7 27.7 %copy-start = (bf16[512,4096]{1,0:T(8,128)(2,1)S(1)}, bf16[512,4096]{1,0:T(8,128)(2,1)}, u32[]{:S(2)}) copy-start(bf16[512,4096]{1,0:T(8,128)(2,1)} %outp_ref.1) | copy-start | bytes 12582916
  51.9 26.5 %copy-start.4 = (f32[2,512,16]{1,2,0:T(8,128)S(1)}, f32[2,512,16]{1,2,0:T(8,128)}, u32[]{:S(2)}) copy-start(f32[2,512,16]{1,2,0:T(8,128)} %param.31) | copy-start | bytes 196612
  51.9 26.5 %copy-start.9 = (f32[512]{0:T(512)S(1)}, f32[512]{0:T(512)}, u32[]{:S(2)}) copy-start(f32[512]{0:T(512)} %param.30) | copy-start | bytes 6148
  82.7 3.8 %copy-start.10 = (bf16[1,256,4096]{2,1,0:T(8,128)(2,1)S(1)}, bf16[1,256,4096]{2,1,0:T(8,128)(2,1)}, u32[]{:S(2)}) copy-start(bf16[1,256,4096]{2,1,0:T(8,128)(2,1)} %param.40) | copy-start | bytes 6291460
  82.8 33.3 %all-to-all-start.3 = ((bf16[8,128,512]{2,1,0:T(8,128)(2,1)}), bf16[8,128,512]{2,1,0:T(8,128)(2,1)S(1)}, u32[]{:S(2)}, u32[]{:S(2)}) async-start(bf16[8,128,512]{2,1,0:T(8,128)(2,1)} %scan.1), calls=%async_computation.3 | async-start | bytes 2097152 | tf_op jit(solution)/shard_map/all_to_all | solution.py:30
  86.5 3.8 %copy-start.15 = (bf16[4,4096]{1,0:T(4,128)(2,1)S(1)}, bf16[4,4096]{1,0:T(4,128)(2,1)}, u32[]{:S(2)}) copy-start(bf16[4,4096]{1,0:T(4,128)(2,1)} %param.35) | copy-start | bytes 98308
  86.5 3.8 %copy-start.16 = (s32[64,2,2]{0,2,1:T(2,128)S(1)}, s32[64,2,2]{0,2,1:T(2,128)}, u32[]{:S(2)}) copy-start(s32[64,2,2]{0,2,1:T(2,128)} %param.41) | copy-start | bytes 3076
  86.5 4.0 %copy-start.6 = (bf16[4096]{0:T(1024)(128)(2,1)S(1)}, bf16[4096]{0:T(1024)(128)(2,1)}, u32[]{:S(2)}) copy-start(bf16[4096]{0:T(1024)(128)(2,1)} %param.34) | copy-start | bytes 24580
  86.5 106.6 %all-gather.2.cloned.1.call-start = ((), (), s32[]{:S(2)}) async-start(), calls=%async_computation.9 | async-start | bytes 5570560 | tf_op jit(solution)/shard_map/all_gather | solution.py:378
  88.1 49.0 %copy-start.5 = (bf16[4096,8]{0,1:T(8,128)(2,1)S(1)}, bf16[4096,8]{0,1:T(8,128)(2,1)}, u32[]{:S(2)}) copy-start(bf16[4096,8]{0,1:T(8,128)(2,1)} %param.37) | copy-start | bytes 196612
  88.1 47.6 %collective-permute-start.4 = (bf16[128,4096]{1,0:T(8,128)(2,1)}, bf16[128,4096]{1,0:T(8,128)(2,1)S(1)}, u32[]{:S(2)}, u32[]{:S(2)}) collective-permute-start(bf16[128,4096]{1,0:T(8,128)(2,1)} %get-tuple-element.164), channel_id=1, source_target_pairs={{0,16},{8,24},{16,0},{24,8},{32,48},{40,56},{48,32},{56,40},{64,80... | collective-permute-start | bytes 3145736 | tf_op jit(solution)/shard_map/ppermute | solution.py:342
  135.7 66.4 %copy-start.12 = (bf16[128,4096]{1,0:T(8,128)(2,1)}, bf16[128,4096]{1,0:T(8,128)(2,1)S(1)}, u32[]{:S(2)}) copy-start(bf16[128,4096]{1,0:T(8,128)(2,1)S(1)} %collective-permute-done.4.refs_2_) | copy-start | bytes 3145732
  135.8 30.6 %collective-permute-start.5 = (bf16[128,4096]{1,0:T(8,128)(2,1)}, bf16[128,4096]{1,0:T(8,128)(2,1)S(1)}, u32[]{:S(2)}, u32[]{:S(2)}) collective-permute-start(bf16[128,4096]{1,0:T(8,128)(2,1)} %get-tuple-element.163), channel_id=1, source_target_pairs={{0,16},{8,24},{16,0},{24,8},{32,48},{40,56},{48,32},{56,40},{64,80... | collective-permute-start | bytes 3145736 | tf_op jit(solution)/shard_map/ppermute | solution.py:342
  138.4 27.9 %all-to-all-start.5 = ((f32[8,16,512]{2,1,0:T(8,128)}), f32[8,16,512]{2,1,0:T(8,128)}, u32[]{:S(2)}, u32[]{:S(2)}) async-start(f32[8,16,512]{2,1,0:T(8,128)} %bitcast.18), calls=%async_computation.5 | async-start | bytes 524288 | tf_op jit(solution)/shard_map/all_to_all | solution.py:30
  142.5 23.9 %collective-permute-start.6 = (bf16[128,4096]{1,0:T(8,128)(2,1)S(1)}, bf16[128,4096]{1,0:T(8,128)(2,1)S(1)}, u32[]{:S(2)}, u32[]{:S(2)}) collective-permute-start(bf16[128,4096]{1,0:T(8,128)(2,1)S(1)} %collective-permute-done.4.refs_2_), channel_id=1, source_target_pairs={{0,8},{8,0},{16,24},{24,16},{32,40},{40,32},{48,56},{56,48},{64,72... | collective-permute-start | bytes 3145736 | tf_op jit(solution)/shard_map/ppermute | solution.py:377
  166.3 35.8 %copy-start.13 = (bf16[128,4096]{1,0:T(8,128)(2,1)}, bf16[128,4096]{1,0:T(8,128)(2,1)S(1)}, u32[]{:S(2)}) copy-start(bf16[128,4096]{1,0:T(8,128)(2,1)S(1)} %collective-permute-done.5.refs_3_) | copy-start | bytes 3145732
  166.4 2.8 collective-permute-start.7
  166.4 26.7 %copy-start.14 = (bf16[128,4096]{1,0:T(8,128)(2,1)}, bf16[128,4096]{1,0:T(8,128)(2,1)S(1)}, u32[]{:S(2)}) copy-start(bf16[128,4096]{1,0:T(8,128)(2,1)S(1)} %collective-permute-done.6.refs_4_) | copy-start | bytes 3145732
  202.1 9.5 %collective-permute-start.8 = (bf16[320,512]{1,0:T(8,128)(2,1)S(1)}, bf16[320,512]{1,0:T(8,128)(2,1)S(1)}, u32[]{:S(2)}, u32[]{:S(2)}) collective-permute-start(bf16[320,512]{1,0:T(8,128)(2,1)S(1)} %get-tuple-element.148), channel_id=1, source_target_pairs={{0,16},{8,24},{16,0},{24,8},{32,48},{40,56},{48,32},{56,40},{64,80... | collective-permute-start | bytes 983048 | tf_op jit(solution)/shard_map/ppermute | solution.py:405
Sparse Core Ops, SparseCore 0:
  135.9 57.1 all-gather.1

commit v4 on v3

--- a/solution.py
+++ b/solution.py
@@ -30,7 +30,12 @@
     return lax.all_to_all(blocks, axis, 0, 0, tiled=True, axis_index_groups=groups)
 
 
-def conv_kernel(lead_ref, x_ref, got_ref, carry_ref, w_ref, b_ref, xp_ref, act_ref, part_ref, pad_ref):
+def conv_kernel(
+    lead_ref, x_ref, got_ref, carry_ref, taps_ref, b_ref, proj_ref, act_ref, part_ref, pad_ref, w_ref, xp_ref, sem
+):
+    copies = [pltpu.make_async_copy(a, b, sem.at[i]) for i, (a, b) in enumerate(((taps_ref, w_ref), (proj_ref, xp_ref)))]
+    for copy in copies:
+        copy.start()
     rows = x_ref.shape[0]
     taps = w_ref.shape[0]
     halo = got_ref.shape[0]
@@ -39,12 +44,28 @@
     pad_ref[:halo, :] = jnp.where(first, carry_ref[...].astype(F32), got_ref[...].astype(F32))
     pad_ref[halo : halo + rows, :] = x_ref[...].astype(F32)
     total = b_ref[...].astype(F32)
+    copies[0].wait()
     w = w_ref[...].astype(F32)
     for k in range(taps):
         total = total + w[k : k + 1, :] * pad_ref[k * step : k * step + rows, :]
     act = silu(total)
     act_ref[...] = act
+    copies[1].wait()
     part_ref[...] = lax.dot_general(act.astype(BF16), xp_ref[...], (((1,), (1,)), ((), ())), preferred_element_type=F32)
+
+
+def sum_kernel(rank, got_ref, out_ref):
+    total = got_ref[0]
+    for j in range(1, got_ref.shape[0]):
+        total = total + got_ref[j]
+    rest = total[:, rank:]
+    high = rest.astype(BF16).astype(F32)
+    middle = (rest - high).astype(BF16).astype(F32)
+    out = [total[:, :rank], high, middle, rest - high - middle]
+    pad = out_ref.shape[2] - rank - 3 * rest.shape[1]
+    out = jnp.concatenate(out + [jnp.zeros((rest.shape[0], pad), F32)], axis=1).astype(BF16)
+    for j in range(out_ref.shape[0]):
+        out_ref[j] = out
 
 
 def advance(state, rate, step, drive, b):
@@ -55,7 +76,7 @@
     rows, channels = act_ref.shape
     states = alog_ref.shape[0]
     rank = dtp_ref.shape[0]
-    low = proj_ref[:, :rank].astype(BF16)
+    low = proj_ref[:, :rank]
     step_ref[...] = jax.nn.softplus(dot(low, dtp_ref[...]) + dtb_ref[...])
     rate = -jnp.exp(alog_ref[...]) * LOG2E
 
@@ -211,10 +232,9 @@
     return copies
 
 
-def first_kernel(parity_ref, x_ref, g0_ref, u0_ref, g1_ref, u1_ref, out_ref, own_ref, g0, u0, g1, u1, x_held, sems, sem):
-    theirs = gathered_half(x_ref, x_held, sems.at[0], 1 - parity_ref[0])
+def first_kernel(parity_ref, x_ref, g0_ref, u0_ref, g1_ref, u1_ref, out_ref, g0, u0, g1, u1, x_held, sems, sem):
+    theirs = gathered_half(x_ref, x_held, sems, 1 - parity_ref[0])
     copies = fetched((g0_ref, u0_ref, g1_ref, u1_ref), (g0, u0, g1, u1), sem)
-    ours = gathered_half(x_ref, own_ref, sems.at[1], parity_ref[0])
     for copy in theirs:
         copy.wait()
     x = x_held[...].reshape(out_ref.shape[0], -1)
@@ -224,16 +244,17 @@
         gate = dot(x, g[...])
         copies[2 * k + 1].wait()
         out_ref[:, k * width : (k + 1) * width] = (silu(gate) * dot(x, u[...])).astype(BF16)
-    for copy in ours:
-        copy.wait()
-
-
-def second_kernel(x_ref, g0, u0, g1, u1, *refs):
-    sources, out_ref, held, sem = refs[:6], refs[6], refs[7:11], refs[11]
+
+
+def second_kernel(parity_ref, x_ref, g0, u0, g1, u1, *refs):
+    sources, out_ref, held, x_held, sems, sem = refs[:6], refs[6], refs[7:11], refs[11], refs[12], refs[13]
+    ours = gathered_half(x_ref, x_held, sems, parity_ref[0])
     part = sources[2].shape[0]
     targets = held[:2] + tuple(d.at[pl.ds(k * part, part)] for d in held[2:] for k in range(2))
     copies = fetched(sources, targets, sem)
-    x = x_ref[...].reshape(out_ref.shape[0], -1)
+    for copy in ours:
+        copy.wait()
+    x = x_held[...].reshape(out_ref.shape[0], -1)
     width = g0.shape[1]
     for k, (g, u) in enumerate(((g0, u0), (g1, u1))):
         out_ref[:, k * width : (k + 1) * width] = (silu(dot(x, g[...])) * dot(x, u[...])).astype(BF16)
@@ -265,6 +286,12 @@
             slots_ref[e], got_ref[e], (((0,), (0,)), ((), ())), preferred_element_type=F32
         )
     out_ref[...] = total.astype(BF16)
+
+
+def final_kernel(own_ref, got_ref, out_ref):
+    width = got_ref.shape[2]
+    for j in range(got_ref.shape[0]):
+        out_ref[:, j * width : (j + 1) * width] = own_ref[j] + got_ref[j].astype(F32)
 
 
 def shape(dims, dtype=F32):
@@ -316,17 +343,34 @@
     activated, part = call(
         conv_kernel,
         (shape((rows, channels)), shape((rows, x_proj.shape[1]))),
-        [SCALAR] + [VM] * 6,
-        [pltpu.VMEM((rows + 8, channels), F32)],
+        [SCALAR] + [VM] * 3 + [pl.BlockSpec(memory_space=pltpu.HBM), VM, pl.BlockSpec(memory_space=pltpu.HBM)],
+        [
+            pltpu.VMEM((rows + 8, channels), F32),
+            pltpu.VMEM(conv_weight.shape, BF16),
+            pltpu.VMEM(x_proj.shape[::-1], BF16),
+            pltpu.SemaphoreType.DMA((2,)),
+        ],
         name="conv",
-    )(place[None], x_rows, received, carry_tail.reshape(halo, channels), conv_weight, conv_bias[None], x_proj.T)
+    )(
+        place[None], x_rows, received, carry_tail.reshape(halo, channels),
+        pltpu.with_memory_space_constraint(conv_weight, pltpu.HBM), conv_bias[None],
+        pltpu.with_memory_space_constraint(x_proj.T, pltpu.HBM),
+    )
     part, activated, *here = fence(part, activated, *here)
-    summed = exchanged(part, "expert").reshape(groups, own_rows, part.shape[1]).sum(axis=0)
+    summed = exchanged(part, "expert").reshape(groups, own_rows, part.shape[1])
+    summed = call(
+        functools.partial(sum_kernel, rank),
+        shape((groups, own_rows, -(-(rank + 6 * states) // 128) * 128), BF16),
+        [VM],
+        name="sum",
+    )(summed)
     summed, activated, *here = fence(summed, activated, *here)
-    projected = exchanged(jnp.tile(summed, (groups, 1)), "expert")
+    projected = exchanged(summed, "expert").reshape(rows, -1)
     projected, activated, *rest = fence(projected, activated, *here, *others)
     (a_log_t, carry_t, gate_rows, own, spot), others = rest[:-3], rest[-3:]
-    bc = jnp.broadcast_to(projected[:, rank:, None], (rows, 2 * states, 128))
+    terms = [projected[:, rank + 2 * states * k : rank + 2 * states * (k + 1)].astype(F32) for k in range(3)]
+    bc = (terms[0] + terms[1]) + terms[2]
+    bc = jnp.broadcast_to(bc[:, :, None], (rows, 2 * states, 128))
     step, ends = call(
         functools.partial(local_kernel, prompts),
         (shape((rows, channels)), shape((prompts * states + 8, channels), BF16)),
@@ -392,27 +436,29 @@
     half = pairs * capacity
     inner = 2 * ups[0].shape[1]
     dma = pltpu.SemaphoreType.DMA
-    theirs, x_own, *ups = pl.pallas_call(
+    parity = ((place // 2) % 2)[None]
+    pieces = pltpu.with_memory_space_constraint(pieces, pltpu.HBM)
+    held_rows = [pltpu.VMEM((pairs, capacity, d_model), BF16), dma((pairs,))]
+    theirs, *ups = pl.pallas_call(
         first_kernel,
-        out_shape=(shape((half, inner), BF16), pltpu.VMEM((pairs, capacity, d_model), BF16))
-        + tuple(pltpu.VMEM(w.shape, BF16) for w in ups),
+        out_shape=(shape((half, inner), BF16),) + tuple(pltpu.VMEM(w.shape, BF16) for w in ups),
         in_specs=[SCALAR] + [hbm] * 5,
-        out_specs=(VM,) * 6,
-        scratch_shapes=[pltpu.VMEM((pairs, capacity, d_model), BF16), dma((2, pairs)), dma((4,))],
+        out_specs=(VM,) * 5,
+        scratch_shapes=held_rows + [dma((4,))],
         compiler_params=pltpu.CompilerParams(vmem_limit_bytes=16 * 1024 * 1024),
         name="first",
-    )(((place // 2) % 2)[None], *(pltpu.with_memory_space_constraint(v, pltpu.HBM) for v in (pieces, *ups)))
+    )(parity, pieces, *(pltpu.with_memory_space_constraint(v, pltpu.HBM) for v in ups))
     given = lax.ppermute(theirs, "seq", across)
     kept, *downs = pl.pallas_call(
         second_kernel,
         out_shape=(shape((half, inner), BF16),) + (pltpu.VMEM(down_w.shape, BF16),) * 4,
-        in_specs=[VM] * 5 + [hbm] * 6,
+        in_specs=[SCALAR, hbm] + [VM] * 4 + [hbm] * 6,
         out_specs=(VM,) * 5,
-        scratch_shapes=[dma((6,))],
+        scratch_shapes=held_rows + [dma((6,))],
         compiler_params=pltpu.CompilerParams(vmem_limit_bytes=16 * 1024 * 1024),
         cost_estimate=pl.CostEstimate(flops=4 * half * inner * d_model, bytes_accessed=1 << 24, transcendentals=0),
         name="second",
-    )(x_own, *ups, *(pltpu.with_memory_space_constraint(v, pltpu.HBM) for v in downs))
+    )(parity, pieces, *ups, *(pltpu.with_memory_space_constraint(v, pltpu.HBM) for v in downs))
     partial = pl.pallas_call(
         down_kernel,
         out_shape=pltpu.VMEM((half, d_model), BF16),
@@ -440,8 +486,8 @@
     back = exchanged(weighted, "expert")
     total = call(combine_kernel, shape((rows, width), BF16), [VM] * 2, name="combine")(back, slots)
     out = exchanged(total, "expert").reshape(groups, own_rows, width)
-    out = own_residual + out.astype(F32)
-    return out.transpose(1, 0, 2).reshape(own_rows // prompts, prompts, d_model)
+    out = call(final_kernel, shape((own_rows, d_model)), [VM] * 2, name="final")(own_residual, out)
+    return out.reshape(own_rows // prompts, prompts, d_model)
 
 
 def solution(mesh):

time: 292 us -> 290 us (level)
  Pallas kernels: 28.5 us -> 32.4 us
    pallas_call x1 -> x3, Pallas kernels: 8.98 us -> 9.87 us  [the longest x1 9.75 us: shards(): pl.pallas_call(first_kernel, out_shape=(shape((half, inner), BF16),) + tu...]
  transfers between devices with their start and end apart: 12 -> 12, of which waited for: 6 -> 6; matrix products, arithmetic and copies ran while one was open for 3% -> 3% of each run, Pallas kernels for 3% -> 4%
where the time goes in v4:
time: 290 us; the launch traced here: 289 us
  blocking collectives  141 us (49%)
  waiting for transfers between devices  79 us (27%)
  Pallas kernels  32.4 us (11%)
  between operations  13.8 us (5%)
  starting transfers between devices  13.6 us (5%)
  local copies, waits for them, and re-layouts  9.06 us (3%)
    all_to_all x7, blocking collectives, exchanged(): lax.all_to_all(blocks, axis, 0, 0, tiled=True, axis_index_groups=groups)  141 us
    ppermute x2, waiting for transfers between devices, shards(): lax.ppermute(down_w[k * part:(k + 1) * part], 'seq', across)  24.4 us
    all_to_all x2, waiting for transfers between devices, exchanged(): lax.all_to_all(blocks, axis, 0, 0, tiled=True, axis_index_groups=groups)  24.1 us
    all_gather x1, waiting for transfers between devices, shards(): lax.all_gather(normed, 'seq', axis=0, tiled=True, axis_index_groups=same_...  24 us
    pallas_call x1, Pallas kernels, shards(): pl.pallas_call(first_kernel, out_shape=(shape((half, inner), BF16),) + tu...  9.75 us
    all_to_all x2, starting transfers between devices, exchanged(): lax.all_to_all(blocks, axis, 0, 0, tiled=True, axis_index_groups=groups)  7.12 us
    pallas_call x1, Pallas kernels, shards(): pl.pallas_call(second_kernel, out_shape=(shape((half, inner), BF16),) + (...  6.84 us
  transfers between devices with their start and end apart: 12, of which 6 were waited for; matrix products, arithmetic and copies ran while one was open for 3% of the time, Pallas kernels for 4%

profile of v4, /device:TPU:2, one launch (start us, length us, event | category | flops | bytes accessed | tf_op | source)
XLA Modules:
  0.0 289.3 jit_solution(3342581341986057550)
XLA Ops:
  7.8 2.4 collective-permute-start
  10.3 1.0 reshape.53.x_ref
  12.6 1.0 reshape.56.own_ref
  13.6 1.0 reshape.55.gate_ref
  14.6 1.7 collective-permute-done.got_ref
  16.3 1.3 conv.1
  17.6 19.3 %all_to_all.61.got_ref = f32[8,16,288]{2,1,0:T(8,128)S(1)} all-to-all(f32[8,16,288]{2,1,0:T(8,128)S(1)} %bitcast.33), channel_id=1, replica_groups=mesh['seq'=32,'expert'=8] {'expert'}, dimensions={0} | all-to-all | bytes 294912 | tf_op jit(solution)/shard_map/all_to_all | solution.py:30
  37.0 11.1 %all_to_all.62 = bf16[8,16,384]{2,1,0:T(8,128)(2,1)S(1)} all-to-all(bf16[8,16,384]{2,1,0:T(8,128)(2,1)S(1)} %sum.1), channel_id=1, replica_groups=mesh['seq'=32,'expert'=8] {'expert'}, dimensions={0} | all-to-all | bytes 196608 | tf_op jit(solution)/shard_map/all_to_all | solution.py:30
  48.8 1.2 local.1
  50.2 26.3 %all_to_all.63.all_ref = bf16[32,40,512]{2,1,0:T(8,128)(2,1)S(1)} all-to-all(bf16[32,40,512]{2,1,0:T(8,128)(2,1)S(1)} %broadcast_in_dim.34), channel_id=1, replica_groups=mesh['seq'=32,'expert'=8] {'seq'}, dimensions={0} | all-to-all | bytes 2621440 | tf_op jit(solution)/shard_map/all_to_all | solution.py:30
  76.6 4.4 %scan.1 = bf16[8,128,512]{2,1,0:T(8,128)(2,1)} custom-call(s32[2]{0:T(128)S(1)} %pad_add_fusion.ids_ref, bf16[32,40,512]{2,1,0:T(8,128)(2,1)S(1)} %all_to_all.63.all_ref, f32[2,16,512]{2,1,0:T(8,128)S(1)} %bitcast.37, f32[128,512]{1,0:T(8,128)S(1)} %get-tuple-element.113.step_ref, f32[128,512]{1,0:T(8,128)S(1)} %get-tuple-element.114.act_ref, ...), custom_call_target="tpu_custom_call" | custom-call | tf_op jit(solution)/shard_map/scan/pallas_call | solution.py:387
  80.9 3.7 %all-to-all-start.3 = ((bf16[8,128,512]{2,1,0:T(8,128)(2,1)}), bf16[8,128,512]{2,1,0:T(8,128)(2,1)S(1)}, u32[]{:S(2)}, u32[]{:S(2)}) async-start(bf16[8,128,512]{2,1,0:T(8,128)(2,1)} %scan.1), calls=%async_computation.3 | async-start | bytes 2097152 | tf_op jit(solution)/shard_map/all_to_all | solution.py:30
  84.8 1.5 fusion
  86.2 1.4 collective-permute-start.4
  88.6 1.5 clean.1
  90.2 24.1 %all-to-all-done.3.mixed_ref = bf16[8,128,512]{2,1,0:T(8,128)(2,1)S(1)} async-done(((bf16[8,128,512]{2,1,0:T(8,128)(2,1)}), bf16[8,128,512]{2,1,0:T(8,128)(2,1)S(1)}, u32[]{:S(2)}, u32[]{:S(2)}) %all-to-all-start.3) | async-done | bytes 1048608 | tf_op jit(solution)/shard_map/all_to_all | solution.py:30
  114.3 0.9 dispatch.1
  115.1 17.9 %all_to_all.64.got_ref = bf16[8,40,640]{2,1,0:T(8,128)(2,1)S(1)} all-to-all(bf16[8,40,640]{2,1,0:T(8,128)(2,1)S(1)} %get-tuple-element.124), channel_id=1, replica_groups=mesh['seq'=32,'expert'=8] {'expert'}, dimensions={0} | all-to-all | bytes 819200 | tf_op jit(solution)/shard_map/all_to_all | solution.py:30
  133.1 0.9 normed.1.x_ref
  133.9 1.4 collective-permute-start.5
  135.3 1.3 share.1.share_ref
  136.6 3.4 %all-to-all-start.5 = ((f32[8,16,512]{2,1,0:T(8,128)}), f32[8,16,512]{2,1,0:T(8,128)S(1)}, u32[]{:S(2)}, u32[]{:S(2)}) async-start(f32[8,16,512]{2,1,0:T(8,128)} %bitcast.18), calls=%async_computation.5 | async-start | bytes 524288 | tf_op jit(solution)/shard_map/all_to_all | solution.py:30
  140.1 24.4 %collective-permute-done.5.refs_3_ = bf16[128,4096]{1,0:T(8,128)(2,1)S(1)} collective-permute-done((bf16[128,4096]{1,0:T(8,128)(2,1)}, bf16[128,4096]{1,0:T(8,128)(2,1)S(1)}, u32[]{:S(2)}, u32[]{:S(2)}) %collective-permute-start.5) | collective-permute-done | bytes 1048608 | tf_op jit(solution)/shard_map/ppermute | solution.py:386
  164.6 2.7 collective-permute-done.7.refs_5_
  167.3 24.0 %all-gather.2.cloned.1.call-done = bf16[640,4096]{1,0:T(8,128)(2,1)} async-done(((bf16[40,4096]{1,0:T(8,128)(2,1)}), bf16[640,4096]{1,0:T(8,128)(2,1)}) %all-gather.2.cloned.1.call-update) | async-done | bytes 5242896 | tf_op jit(solution)/shard_map/all_gather | solution.py:422
  191.3 9.8 %first.1 = (bf16[320,512]{1,0:T(8,128)(2,1)S(1)}, bf16[4096,256]{1,0:T(8,128)(2,1)S(1)}, bf16[4096,256]{1,0:T(8,128)(2,1)S(1)}, bf16[4096,256]{1,0:T(8,128)(2,1)S(1)}, bf16[4096,256]{1,0:T(8,128)(2,1)S(1)}) custom-call(s32[1]{0:T(128)} %bitcast.parity_ref, bf16[8,2,40,4096]{3,2,1,0:T(8,128)(2,1)} %bitcast.43, bf16[4096,256]{1,0:T(8,128)(2,1)} %bitcast.49, ...), custom_call_target="tpu_custom_call" | custom-call | tf_op jit(solution)/shard_map/first/pallas_call | solution.py:442
  201.7 6.8 %second.1 = (bf16[320,512]{1,0:T(8,128)(2,1)S(1)}, bf16[256,4096]{1,0:T(8,128)(2,1)S(1)}, bf16[256,4096]{1,0:T(8,128)(2,1)S(1)}, bf16[256,4096]{1,0:T(8,128)(2,1)S(1)}, bf16[256,4096]{1,0:T(8,128)(2,1)S(1)}) custom-call(s32[1]{0:T(128)} %bitcast.parity_ref, bf16[8,2,40,4096]{3,2,1,0:T(8,128)(2,1)} %bitcast.44, bf16[4096,256]{1,0:T(8,128)(2,1)S(1)} %get-tuple-element.138.g0, ...), custom_call_target="tpu_custom_call" | custom-call | flops 2684354560 | bytes 16777216 | tf_op jit(solution)/shard_map/second/pallas_call | solution.py:452
  208.6 2.0 collective-permute-done.8.far_ref
  210.6 2.9 %down.1 = bf16[320,4096]{1,0:T(8,128)(2,1)S(1)} custom-call(bf16[320,512]{1,0:T(8,128)(2,1)S(1)} %get-tuple-element.145.own_ref, bf16[320,512]{1,0:T(8,128)(2,1)S(1)} %collective-permute-done.8.far_ref, bf16[256,4096]{1,0:T(8,128)(2,1)S(1)} %get-tuple-element.147.d0, bf16[256,4096]{1,0:T(8,128)(2,1)S(1)} %get-tuple-element.148.d1, ...), custom_call_target="tpu_custom_call" | custom-call | tf_op jit(solution)/shard_map/down/pallas_call | solution.py:462
  213.6 37.2 %all_to_all.65.got_ref = bf16[8,40,4096]{2,1,0:T(8,128)(2,1)S(1)} all-to-all(bf16[8,40,4096]{2,1,0:T(8,128)(2,1)S(1)} %bitcast.27), channel_id=1, replica_groups={{0,32,64,96,128,160,192,224},{8,40,72,104,136,168,200,232},{16,48,80,11..., dimensions={0} | all-to-all | bytes 5242880 | tf_op jit(solution)/shard_map/all_to_all | solution.py:30
  251.6 18.0 %all_to_all.66.got_ref = bf16[8,40,512]{2,1,0:T(8,128)(2,1)S(1)} all-to-all(bf16[8,40,512]{2,1,0:T(8,128)(2,1)S(1)} %weigh.1), channel_id=1, replica_groups=mesh['seq'=32,'expert'=8] {'expert'}, dimensions={0} | all-to-all | bytes 655360 | tf_op jit(solution)/shard_map/all_to_all | solution.py:30
  270.1 11.5 %all_to_all.67.got_ref = bf16[8,16,512]{2,1,0:T(8,128)(2,1)S(1)} all-to-all(bf16[8,16,512]{2,1,0:T(8,128)(2,1)S(1)} %bitcast.32), channel_id=1, replica_groups=mesh['seq'=32,'expert'=8] {'expert'}, dimensions={0} | all-to-all | bytes 262144 | tf_op jit(solution)/shard_map/all_to_all | solution.py:30
  (61 shorter events, 7.5 us)
Async XLA Ops:
  6.5 41.5 %collective-permute-start.1 = (bf16[4096,256]{1,0:T(8,128)(2,1)}, bf16[4096,256]{1,0:T(8,128)(2,1)}, u32[]{:S(2)}, u32[]{:S(2)}) collective-permute-start(bf16[4096,256]{1,0:T(8,128)(2,1)} %bitcast.48), channel_id=1, source_target_pairs={{0,8},{8,0},{16,24},{24,16},{32,40},{40,32},{48,56},{56,48},{64,72... | collective-permute-start | bytes 6291464 | tf_op jit(solution)/shard_map/ppermute | solution.py:333
  6.5 41.5 %collective-permute-start.2 = (bf16[4096,256]{1,0:T(8,128)(2,1)}, bf16[4096,256]{1,0:T(8,128)(2,1)}, u32[]{:S(2)}, u32[]{:S(2)}) collective-permute-start(bf16[4096,256]{1,0:T(8,128)(2,1)} %bitcast.50), channel_id=1, source_target_pairs={{0,8},{8,0},{16,24},{24,16},{32,40},{40,32},{48,56},{56,48},{64,72... | collective-permute-start | bytes 6291464 | tf_op jit(solution)/shard_map/ppermute | solution.py:333
  7.0 41.0 %collective-permute-start.3 = (bf16[256,4096]{1,0:T(8,128)(2,1)}, bf16[256,4096]{1,0:T(8,128)(2,1)S(1)}, u32[]{:S(2)}, u32[]{:S(2)}) collective-permute-start(bf16[256,4096]{1,0:T(8,128)(2,1)} %bitcast.45), channel_id=1, source_target_pairs={{0,8},{8,0},{16,24},{24,16},{32,40},{40,32},{48,56},{56,48},{64,72... | collective-permute-start | bytes 6291464 | tf_op jit(solution)/shard_map/ppermute | solution.py:333
  7.8 8.6 %collective-permute-start = (bf16[6,512]{1,0:T(8,128)(2,1)S(1)}, bf16[6,512]{1,0:T(8,128)(2,1)S(1)}, u32[]{:S(2)}, u32[]{:S(2)}) collective-permute-start(bf16[6,512]{1,0:T(8,128)(2,1)S(1)} %slice.22), channel_id=1, source_target_pairs={{0,8},{8,16},{16,24},{24,32},{32,40},{40,48},{48,56},{56,64},{64,7... | collective-permute-start | bytes 18440 | tf_op jit(solution)/shard_map/ppermute | solution.py:337
  12.6 36.2 %copy-start.1 = (bf16[256,512]{1,0:T(8,128)(2,1)S(1)}, bf16[256,512]{1,0:T(8,128)(2,1)}, u32[]{:S(2)}) copy-start(bf16[256,512]{1,0:T(8,128)(2,1)} %dtp_ref.1) | copy-start | bytes 786436
  12.6 36.2 %copy-start.2 = (f32[512,16]{0,1:T(8,128)S(1)}, f32[512,16]{0,1:T(8,128)}, u32[]{:S(2)}) copy-start(f32[512,16]{0,1:T(8,128)} %param.29) | copy-start | bytes 98308
  12.6 36.2 %copy-start.6 = (f32[512]{0:T(512)S(1)}, f32[512]{0:T(512)}, u32[]{:S(2)}) copy-start(f32[512]{0:T(512)} %param.28) | copy-start | bytes 6148
  48.1 2.0 copy-start.9
  48.8 27.7 %copy-start = (bf16[512,4096]{1,0:T(8,128)(2,1)S(1)}, bf16[512,4096]{1,0:T(8,128)(2,1)}, u32[]{:S(2)}) copy-start(bf16[512,4096]{1,0:T(8,128)(2,1)} %outp_ref.1) | copy-start | bytes 12582916
  50.1 26.5 %copy-start.3 = (f32[2,512,16]{1,2,0:T(8,128)S(1)}, f32[2,512,16]{1,2,0:T(8,128)}, u32[]{:S(2)}) copy-start(f32[2,512,16]{1,2,0:T(8,128)} %param.31) | copy-start | bytes 196612
  50.1 26.5 %copy-start.7 = (f32[512]{0:T(512)S(1)}, f32[512]{0:T(512)}, u32[]{:S(2)}) copy-start(f32[512]{0:T(512)} %param.30) | copy-start | bytes 6148
  80.9 3.8 %copy-start.8 = (bf16[1,256,4096]{2,1,0:T(8,128)(2,1)S(1)}, bf16[1,256,4096]{2,1,0:T(8,128)(2,1)}, u32[]{:S(2)}) copy-start(bf16[1,256,4096]{2,1,0:T(8,128)(2,1)} %param.40) | copy-start | bytes 6291460
  80.9 33.3 %all-to-all-start.3 = ((bf16[8,128,512]{2,1,0:T(8,128)(2,1)}), bf16[8,128,512]{2,1,0:T(8,128)(2,1)S(1)}, u32[]{:S(2)}, u32[]{:S(2)}) async-start(bf16[8,128,512]{2,1,0:T(8,128)(2,1)} %scan.1), calls=%async_computation.3 | async-start | bytes 2097152 | tf_op jit(solution)/shard_map/all_to_all | solution.py:30
  84.7 3.7 %copy-start.12 = (bf16[4,4096]{1,0:T(4,128)(2,1)S(1)}, bf16[4,4096]{1,0:T(4,128)(2,1)}, u32[]{:S(2)}) copy-start(bf16[4,4096]{1,0:T(4,128)(2,1)} %param.35) | copy-start | bytes 98308
  84.7 3.7 %copy-start.13 = (s32[64,2,2]{0,2,1:T(2,128)S(1)}, s32[64,2,2]{0,2,1:T(2,128)}, u32[]{:S(2)}) copy-start(s32[64,2,2]{0,2,1:T(2,128)} %param.41) | copy-start | bytes 3076
  84.7 3.9 %copy-start.5 = (bf16[4096]{0:T(1024)(128)(2,1)S(1)}, bf16[4096]{0:T(1024)(128)(2,1)}, u32[]{:S(2)}) copy-start(bf16[4096]{0:T(1024)(128)(2,1)} %param.34) | copy-start | bytes 24580
  84.7 106.6 %all-gather.2.cloned.1.call-start = ((), (), s32[]{:S(2)}) async-start(), calls=%async_computation.9 | async-start | bytes 5570560 | tf_op jit(solution)/shard_map/all_gather | solution.py:422
  86.2 49.1 %copy-start.4 = (bf16[4096,8]{0,1:T(8,128)(2,1)S(1)}, bf16[4096,8]{0,1:T(8,128)(2,1)}, u32[]{:S(2)}) copy-start(bf16[4096,8]{0,1:T(8,128)(2,1)} %param.37) | copy-start | bytes 196612
  86.2 47.7 %collective-permute-start.4 = (bf16[128,4096]{1,0:T(8,128)(2,1)}, bf16[128,4096]{1,0:T(8,128)(2,1)S(1)}, u32[]{:S(2)}, u32[]{:S(2)}) collective-permute-start(bf16[128,4096]{1,0:T(8,128)(2,1)} %get-tuple-element.162), channel_id=1, source_target_pairs={{0,16},{8,24},{16,0},{24,8},{32,48},{40,56},{48,32},{56,40},{64,80... | collective-permute-start | bytes 3145736 | tf_op jit(solution)/shard_map/ppermute | solution.py:386
  133.9 67.2 %copy-start.10 = (bf16[128,4096]{1,0:T(8,128)(2,1)}, bf16[128,4096]{1,0:T(8,128)(2,1)S(1)}, u32[]{:S(2)}) copy-start(bf16[128,4096]{1,0:T(8,128)(2,1)S(1)} %collective-permute-done.4.refs_2_) | copy-start | bytes 3145732
  133.9 30.6 %collective-permute-start.5 = (bf16[128,4096]{1,0:T(8,128)(2,1)}, bf16[128,4096]{1,0:T(8,128)(2,1)S(1)}, u32[]{:S(2)}, u32[]{:S(2)}) collective-permute-start(bf16[128,4096]{1,0:T(8,128)(2,1)} %get-tuple-element.161), channel_id=1, source_target_pairs={{0,16},{8,24},{16,0},{24,8},{32,48},{40,56},{48,32},{56,40},{64,80... | collective-permute-start | bytes 3145736 | tf_op jit(solution)/shard_map/ppermute | solution.py:386
  136.6 27.9 %all-to-all-start.5 = ((f32[8,16,512]{2,1,0:T(8,128)}), f32[8,16,512]{2,1,0:T(8,128)S(1)}, u32[]{:S(2)}, u32[]{:S(2)}) async-start(f32[8,16,512]{2,1,0:T(8,128)} %bitcast.18), calls=%async_computation.5 | async-start | bytes 524288 | tf_op jit(solution)/shard_map/all_to_all | solution.py:30
  140.0 24.5 %collective-permute-start.6 = (bf16[128,4096]{1,0:T(8,128)(2,1)S(1)}, bf16[128,4096]{1,0:T(8,128)(2,1)}, u32[]{:S(2)}, u32[]{:S(2)}) collective-permute-start(bf16[128,4096]{1,0:T(8,128)(2,1)S(1)} %collective-permute-done.4.refs_2_), channel_id=1, source_target_pairs={{0,8},{8,0},{16,24},{24,16},{32,40},{40,32},{48,56},{56,48},{64,72... | collective-permute-start | bytes 3145736 | tf_op jit(solution)/shard_map/ppermute | solution.py:421
  164.5 36.5 %copy-start.11 = (bf16[128,4096]{1,0:T(8,128)(2,1)}, bf16[128,4096]{1,0:T(8,128)(2,1)S(1)}, u32[]{:S(2)}) copy-start(bf16[128,4096]{1,0:T(8,128)(2,1)S(1)} %collective-permute-done.5.refs_3_) | copy-start | bytes 3145732
  164.5 2.8 collective-permute-start.7
  201.1 9.5 %collective-permute-start.8 = (bf16[320,512]{1,0:T(8,128)(2,1)S(1)}, bf16[320,512]{1,0:T(8,128)(2,1)S(1)}, u32[]{:S(2)}, u32[]{:S(2)}) collective-permute-start(bf16[320,512]{1,0:T(8,128)(2,1)S(1)} %get-tuple-element.146), channel_id=1, source_target_pairs={{0,16},{8,24},{16,0},{24,8},{32,48},{40,56},{48,32},{56,40},{64,80... | collective-permute-start | bytes 983048 | tf_op jit(solution)/shard_map/ppermute | solution.py:451
Sparse Core Ops, SparseCore 0:
  134.1 57.1 all-gather.1

commit v5 on v4

--- a/solution.py
+++ b/solution.py
@@ -224,40 +224,50 @@
     return copies
 
 
-def gathered_half(x_ref, held_ref, sem, parity):
-    pairs, _, capacity, _ = x_ref.shape
-    copies = [pltpu.make_async_copy(x_ref.at[i, parity], held_ref.at[i], sem.at[i]) for i in range(pairs)]
-    for copy in copies:
+def sliced(source, target, sem, parts, axis):
+    size = target.shape[axis] // parts
+    at = lambda k: (slice(None),) * axis + (pl.ds(k * size, size),)
+    return [pltpu.make_async_copy(source.at[at(k)], target.at[at(k)], sem.at[k]) for k in range(parts)]
+
+
+def hidden_of(x_held, x_copies, weights, weight_copies, out_ref):
+    parts = len(x_copies)
+    size = x_held.shape[2] // parts
+    totals = None
+    for k in range(parts):
+        x_copies[k].wait()
+        for copies in weight_copies:
+            copies[k].wait()
+        x = x_held[:, :, k * size : (k + 1) * size].reshape(out_ref.shape[0], size)
+        terms = [dot(x, w[k * size : (k + 1) * size, :]) for w in weights]
+        totals = terms if totals is None else [a + b for a, b in zip(totals, terms)]
+    width = weights[0].shape[1]
+    for k in range(2):
+        out_ref[:, k * width : (k + 1) * width] = (silu(totals[2 * k]) * totals[2 * k + 1]).astype(BF16)
+
+
+def first_kernel(parity_ref, x_ref, g0_ref, u0_ref, g1_ref, u1_ref, out_ref, g0, u0, g1, u1, x_held, x_sem, sems):
+    parts = x_sem.shape[0]
+    x_copies = sliced(x_ref.at[:, 1 - parity_ref[0]], x_held, x_sem, parts, 2)
+    held = (g0, u0, g1, u1)
+    sources = (g0_ref, u0_ref, g1_ref, u1_ref)
+    weight_copies = [sliced(a, b, sems.at[i], parts, 0) for i, (a, b) in enumerate(zip(sources, held))]
+    for k in range(parts):
+        x_copies[k].start()
+        for copies in weight_copies:
+            copies[k].start()
+    hidden_of(x_held, x_copies, held, weight_copies, out_ref)
+
+
+def second_kernel(parity_ref, x_ref, g0, u0, g1, u1, *refs):
+    sources, out_ref, held, x_held, x_sem, sem = refs[:6], refs[6], refs[7:11], refs[11], refs[12], refs[13]
+    x_copies = sliced(x_ref.at[:, parity_ref[0]], x_held, x_sem, x_sem.shape[0], 2)
+    for copy in x_copies:
         copy.start()
-    return copies
-
-
-def first_kernel(parity_ref, x_ref, g0_ref, u0_ref, g1_ref, u1_ref, out_ref, g0, u0, g1, u1, x_held, sems, sem):
-    theirs = gathered_half(x_ref, x_held, sems, 1 - parity_ref[0])
-    copies = fetched((g0_ref, u0_ref, g1_ref, u1_ref), (g0, u0, g1, u1), sem)
-    for copy in theirs:
-        copy.wait()
-    x = x_held[...].reshape(out_ref.shape[0], -1)
-    width = g0.shape[1]
-    for k, (g, u) in enumerate(((g0, u0), (g1, u1))):
-        copies[2 * k].wait()
-        gate = dot(x, g[...])
-        copies[2 * k + 1].wait()
-        out_ref[:, k * width : (k + 1) * width] = (silu(gate) * dot(x, u[...])).astype(BF16)
-
-
-def second_kernel(parity_ref, x_ref, g0, u0, g1, u1, *refs):
-    sources, out_ref, held, x_held, sems, sem = refs[:6], refs[6], refs[7:11], refs[11], refs[12], refs[13]
-    ours = gathered_half(x_ref, x_held, sems, parity_ref[0])
     part = sources[2].shape[0]
     targets = held[:2] + tuple(d.at[pl.ds(k * part, part)] for d in held[2:] for k in range(2))
     copies = fetched(sources, targets, sem)
-    for copy in ours:
-        copy.wait()
-    x = x_held[...].reshape(out_ref.shape[0], -1)
-    width = g0.shape[1]
-    for k, (g, u) in enumerate(((g0, u0), (g1, u1))):
-        out_ref[:, k * width : (k + 1) * width] = (silu(dot(x, g[...])) * dot(x, u[...])).astype(BF16)
+    hidden_of(x_held, x_copies, (g0, u0, g1, u1), (), out_ref)
     for copy in copies:
         copy.wait()
 
@@ -291,7 +301,8 @@
 def final_kernel(own_ref, got_ref, out_ref):
     width = got_ref.shape[2]
     for j in range(got_ref.shape[0]):
-        out_ref[:, j * width : (j + 1) * width] = own_ref[j] + got_ref[j].astype(F32)
+        total = own_ref[j] + got_ref[j].astype(F32)
+        out_ref[:, :, j * width : (j + 1) * width] = total.reshape(out_ref.shape[0], out_ref.shape[1], width)
 
 
 def shape(dims, dtype=F32):
@@ -438,13 +449,14 @@
     dma = pltpu.SemaphoreType.DMA
     parity = ((place // 2) % 2)[None]
     pieces = pltpu.with_memory_space_constraint(pieces, pltpu.HBM)
-    held_rows = [pltpu.VMEM((pairs, capacity, d_model), BF16), dma((pairs,))]
+    parts = 4
+    held_rows = [pltpu.VMEM((pairs, capacity, d_model), BF16), dma((parts,))]
     theirs, *ups = pl.pallas_call(
         first_kernel,
         out_shape=(shape((half, inner), BF16),) + tuple(pltpu.VMEM(w.shape, BF16) for w in ups),
         in_specs=[SCALAR] + [hbm] * 5,
         out_specs=(VM,) * 5,
-        scratch_shapes=held_rows + [dma((4,))],
+        scratch_shapes=held_rows + [dma((4, parts))],
         compiler_params=pltpu.CompilerParams(vmem_limit_bytes=16 * 1024 * 1024),
         name="first",
     )(parity, pieces, *(pltpu.with_memory_space_constraint(v, pltpu.HBM) for v in ups))
@@ -486,8 +498,7 @@
     back = exchanged(weighted, "expert")
     total = call(combine_kernel, shape((rows, width), BF16), [VM] * 2, name="combine")(back, slots)
     out = exchanged(total, "expert").reshape(groups, own_rows, width)
-    out = call(final_kernel, shape((own_rows, d_model)), [VM] * 2, name="final")(own_residual, out)
-    return out.reshape(own_rows // prompts, prompts, d_model)
+    return call(final_kernel, shape((own_rows // prompts, prompts, d_model)), [VM] * 2, name="final")(own_residual, out)
 
 
 def solution(mesh):

time: 290 us -> 286 us (0.986)
  Pallas kernels: 32.4 us -> 26.6 us
    pallas_call x1, Pallas kernels: 9.75 us -> 5.74 us  [shards(): pl.pallas_call(first_kernel, out_shape=(shape((half, inner), BF16),) + tu...]
where the time goes in v5:
time: 286 us; the launch traced here: 285 us
  blocking collectives  141 us (49%)
  waiting for transfers between devices  81.5 us (28%)
  Pallas kernels  26.6 us (9%)
  starting transfers between devices  13.8 us (5%)
  between operations  13.7 us (5%)
  local copies, waits for them, and re-layouts  8.21 us (3%)
    all_to_all x7, blocking collectives, exchanged(): lax.all_to_all(blocks, axis, 0, 0, tiled=True, axis_index_groups=groups)  141 us
    ppermute x2, waiting for transfers between devices, shards(): lax.ppermute(down_w[k * part:(k + 1) * part], 'seq', across)  24.4 us
    all_to_all x2, waiting for transfers between devices, exchanged(): lax.all_to_all(blocks, axis, 0, 0, tiled=True, axis_index_groups=groups)  24.1 us
    all_gather x1, waiting for transfers between devices, shards(): lax.all_gather(normed, 'seq', axis=0, tiled=True, axis_index_groups=same_...  24 us
    all_to_all x2, starting transfers between devices, exchanged(): lax.all_to_all(blocks, axis, 0, 0, tiled=True, axis_index_groups=groups)  7.12 us
    pallas_call x1, Pallas kernels, shards(): pl.pallas_call(first_kernel, out_shape=(shape((half, inner), BF16),) + tu...  5.74 us
  transfers between devices with their start and end apart: 12, of which 6 were waited for; matrix products, arithmetic and copies ran while one was open for 3% of the time, Pallas kernels for 4%

profile of v5, /device:TPU:2, one launch (start us, length us, event | category | flops | bytes accessed | tf_op | source)
XLA Modules:
  0.0 285.3 jit_solution(2087391950079771212)
XLA Ops:
  7.8 2.4 collective-permute-start
  10.3 1.0 reshape.50.x_ref
  12.6 1.0 reshape.53.own_ref
  13.6 1.0 reshape.52.gate_ref
  14.6 1.7 collective-permute-done.got_ref
  16.3 1.3 conv.1
  17.6 19.3 %all_to_all.61.got_ref = f32[8,16,288]{2,1,0:T(8,128)S(1)} all-to-all(f32[8,16,288]{2,1,0:T(8,128)S(1)} %bitcast.33), channel_id=1, replica_groups=mesh['seq'=32,'expert'=8] {'expert'}, dimensions={0} | all-to-all | bytes 294912 | tf_op jit(solution)/shard_map/all_to_all | solution.py:30
  37.0 11.1 %all_to_all.62 = bf16[8,16,384]{2,1,0:T(8,128)(2,1)S(1)} all-to-all(bf16[8,16,384]{2,1,0:T(8,128)(2,1)S(1)} %sum.1), channel_id=1, replica_groups=mesh['seq'=32,'expert'=8] {'expert'}, dimensions={0} | all-to-all | bytes 196608 | tf_op jit(solution)/shard_map/all_to_all | solution.py:30
  48.8 1.2 local.1
  50.2 26.3 %all_to_all.63.all_ref = bf16[32,40,512]{2,1,0:T(8,128)(2,1)S(1)} all-to-all(bf16[32,40,512]{2,1,0:T(8,128)(2,1)S(1)} %broadcast_in_dim.34), channel_id=1, replica_groups=mesh['seq'=32,'expert'=8] {'seq'}, dimensions={0} | all-to-all | bytes 2621440 | tf_op jit(solution)/shard_map/all_to_all | solution.py:30
  76.6 4.4 %scan.1 = bf16[8,128,512]{2,1,0:T(8,128)(2,1)} custom-call(s32[2]{0:T(128)S(1)} %pad_add_fusion.ids_ref, bf16[32,40,512]{2,1,0:T(8,128)(2,1)S(1)} %all_to_all.63.all_ref, f32[2,16,512]{2,1,0:T(8,128)S(1)} %bitcast.37, f32[128,512]{1,0:T(8,128)S(1)} %get-tuple-element.113.step_ref, f32[128,512]{1,0:T(8,128)S(1)} %get-tuple-element.114.act_ref, ...), custom_call_target="tpu_custom_call" | custom-call | tf_op jit(solution)/shard_map/scan/pallas_call | solution.py:398
  80.9 3.7 %all-to-all-start.3 = ((bf16[8,128,512]{2,1,0:T(8,128)(2,1)}), bf16[8,128,512]{2,1,0:T(8,128)(2,1)S(1)}, u32[]{:S(2)}, u32[]{:S(2)}) async-start(bf16[8,128,512]{2,1,0:T(8,128)(2,1)} %scan.1), calls=%async_computation.3 | async-start | bytes 2097152 | tf_op jit(solution)/shard_map/all_to_all | solution.py:30
  84.8 1.5 fusion
  86.2 1.4 collective-permute-start.4
  88.6 1.5 clean.1
  90.2 24.1 %all-to-all-done.3.mixed_ref = bf16[8,128,512]{2,1,0:T(8,128)(2,1)S(1)} async-done(((bf16[8,128,512]{2,1,0:T(8,128)(2,1)}), bf16[8,128,512]{2,1,0:T(8,128)(2,1)S(1)}, u32[]{:S(2)}, u32[]{:S(2)}) %all-to-all-start.3) | async-done | bytes 1048608 | tf_op jit(solution)/shard_map/all_to_all | solution.py:30
  114.3 0.9 dispatch.1
  115.1 17.9 %all_to_all.64.got_ref = bf16[8,40,640]{2,1,0:T(8,128)(2,1)S(1)} all-to-all(bf16[8,40,640]{2,1,0:T(8,128)(2,1)S(1)} %get-tuple-element.124), channel_id=1, replica_groups=mesh['seq'=32,'expert'=8] {'expert'}, dimensions={0} | all-to-all | bytes 819200 | tf_op jit(solution)/shard_map/all_to_all | solution.py:30
  133.1 0.9 normed.1.x_ref
  133.9 1.4 collective-permute-start.5
  135.3 1.3 share.1.share_ref
  136.6 3.4 %all-to-all-start.5 = ((f32[8,16,512]{2,1,0:T(8,128)}), f32[8,16,512]{2,1,0:T(8,128)S(1)}, u32[]{:S(2)}, u32[]{:S(2)}) async-start(f32[8,16,512]{2,1,0:T(8,128)} %bitcast.18), calls=%async_computation.5 | async-start | bytes 524288 | tf_op jit(solution)/shard_map/all_to_all | solution.py:30
  140.1 24.4 %collective-permute-done.5.refs_3_ = bf16[128,4096]{1,0:T(8,128)(2,1)S(1)} collective-permute-done((bf16[128,4096]{1,0:T(8,128)(2,1)}, bf16[128,4096]{1,0:T(8,128)(2,1)S(1)}, u32[]{:S(2)}, u32[]{:S(2)}) %collective-permute-start.5) | collective-permute-done | bytes 1048608 | tf_op jit(solution)/shard_map/ppermute | solution.py:397
  164.6 2.8 collective-permute-done.7.refs_5_
  167.3 24.0 %all-gather.2.cloned.1.call-done = bf16[640,4096]{1,0:T(8,128)(2,1)} async-done(((bf16[40,4096]{1,0:T(8,128)(2,1)}), bf16[640,4096]{1,0:T(8,128)(2,1)}) %all-gather.2.cloned.1.call-update) | async-done | bytes 5242896 | tf_op jit(solution)/shard_map/all_gather | solution.py:433
  191.3 5.7 %first.1 = (bf16[320,512]{1,0:T(8,128)(2,1)S(1)}, bf16[4096,256]{1,0:T(8,128)(2,1)S(1)}, bf16[4096,256]{1,0:T(8,128)(2,1)S(1)}, bf16[4096,256]{1,0:T(8,128)(2,1)S(1)}, bf16[4096,256]{1,0:T(8,128)(2,1)S(1)}) custom-call(s32[1]{0:T(128)} %bitcast.parity_ref, bf16[8,2,40,4096]{3,2,1,0:T(8,128)(2,1)} %bitcast.43, bf16[4096,256]{1,0:T(8,128)(2,1)} %bitcast.49, ...), custom_call_target="tpu_custom_call" | custom-call | tf_op jit(solution)/shard_map/first/pallas_call | solution.py:454
  197.9 4.4 %second.1 = (bf16[320,512]{1,0:T(8,128)(2,1)S(1)}, bf16[256,4096]{1,0:T(8,128)(2,1)S(1)}, bf16[256,4096]{1,0:T(8,128)(2,1)S(1)}, bf16[256,4096]{1,0:T(8,128)(2,1)S(1)}, bf16[256,4096]{1,0:T(8,128)(2,1)S(1)}) custom-call(s32[1]{0:T(128)} %bitcast.parity_ref, bf16[8,2,40,4096]{3,2,1,0:T(8,128)(2,1)} %bitcast.44, bf16[4096,256]{1,0:T(8,128)(2,1)S(1)} %get-tuple-element.138.g0, ...), custom_call_target="tpu_custom_call" | custom-call | flops 2684354560 | bytes 16777216 | tf_op jit(solution)/shard_map/second/pallas_call | solution.py:464
  202.3 4.5 %collective-permute-done.8.far_ref = bf16[320,512]{1,0:T(8,128)(2,1)S(1)} collective-permute-done((bf16[320,512]{1,0:T(8,128)(2,1)S(1)}, bf16[320,512]{1,0:T(8,128)(2,1)S(1)}, u32[]{:S(2)}, u32[]{:S(2)}) %collective-permute-start.8) | collective-permute-done | bytes 327712 | tf_op jit(solution)/shard_map/ppermute | solution.py:463
  206.8 2.9 %down.1 = bf16[320,4096]{1,0:T(8,128)(2,1)S(1)} custom-call(bf16[320,512]{1,0:T(8,128)(2,1)S(1)} %get-tuple-element.145.own_ref, bf16[320,512]{1,0:T(8,128)(2,1)S(1)} %collective-permute-done.8.far_ref, bf16[256,4096]{1,0:T(8,128)(2,1)S(1)} %get-tuple-element.147.d0, bf16[256,4096]{1,0:T(8,128)(2,1)S(1)} %get-tuple-element.148.d1, ...), custom_call_target="tpu_custom_call" | custom-call | tf_op jit(solution)/shard_map/down/pallas_call | solution.py:474
  209.7 37.2 %all_to_all.65.got_ref = bf16[8,40,4096]{2,1,0:T(8,128)(2,1)S(1)} all-to-all(bf16[8,40,4096]{2,1,0:T(8,128)(2,1)S(1)} %bitcast.27), channel_id=1, replica_groups={{0,32,64,96,128,160,192,224},{8,40,72,104,136,168,200,232},{16,48,80,11..., dimensions={0} | all-to-all | bytes 5242880 | tf_op jit(solution)/shard_map/all_to_all | solution.py:30
  247.8 18.0 %all_to_all.66.got_ref = bf16[8,40,512]{2,1,0:T(8,128)(2,1)S(1)} all-to-all(bf16[8,40,512]{2,1,0:T(8,128)(2,1)S(1)} %weigh.1), channel_id=1, replica_groups=mesh['seq'=32,'expert'=8] {'expert'}, dimensions={0} | all-to-all | bytes 655360 | tf_op jit(solution)/shard_map/all_to_all | solution.py:30
  266.2 11.5 %all_to_all.67.got_ref = bf16[8,16,512]{2,1,0:T(8,128)(2,1)S(1)} all-to-all(bf16[8,16,512]{2,1,0:T(8,128)(2,1)S(1)} %bitcast.32), channel_id=1, replica_groups=mesh['seq'=32,'expert'=8] {'expert'}, dimensions={0} | all-to-all | bytes 262144 | tf_op jit(solution)/shard_map/all_to_all | solution.py:30
  (60 shorter events, 7.6 us)
Async XLA Ops:
  6.5 41.5 %collective-permute-start.1 = (bf16[4096,256]{1,0:T(8,128)(2,1)}, bf16[4096,256]{1,0:T(8,128)(2,1)}, u32[]{:S(2)}, u32[]{:S(2)}) collective-permute-start(bf16[4096,256]{1,0:T(8,128)(2,1)} %bitcast.48), channel_id=1, source_target_pairs={{0,8},{8,0},{16,24},{24,16},{32,40},{40,32},{48,56},{56,48},{64,72... | collective-permute-start | bytes 6291464 | tf_op jit(solution)/shard_map/ppermute | solution.py:344
  6.5 41.5 %collective-permute-start.2 = (bf16[4096,256]{1,0:T(8,128)(2,1)}, bf16[4096,256]{1,0:T(8,128)(2,1)}, u32[]{:S(2)}, u32[]{:S(2)}) collective-permute-start(bf16[4096,256]{1,0:T(8,128)(2,1)} %bitcast.50), channel_id=1, source_target_pairs={{0,8},{8,0},{16,24},{24,16},{32,40},{40,32},{48,56},{56,48},{64,72... | collective-permute-start | bytes 6291464 | tf_op jit(solution)/shard_map/ppermute | solution.py:344
  7.0 41.0 %collective-permute-start.3 = (bf16[256,4096]{1,0:T(8,128)(2,1)}, bf16[256,4096]{1,0:T(8,128)(2,1)S(1)}, u32[]{:S(2)}, u32[]{:S(2)}) collective-permute-start(bf16[256,4096]{1,0:T(8,128)(2,1)} %bitcast.45), channel_id=1, source_target_pairs={{0,8},{8,0},{16,24},{24,16},{32,40},{40,32},{48,56},{56,48},{64,72... | collective-permute-start | bytes 6291464 | tf_op jit(solution)/shard_map/ppermute | solution.py:344
  7.8 8.6 %collective-permute-start = (bf16[6,512]{1,0:T(8,128)(2,1)S(1)}, bf16[6,512]{1,0:T(8,128)(2,1)S(1)}, u32[]{:S(2)}, u32[]{:S(2)}) collective-permute-start(bf16[6,512]{1,0:T(8,128)(2,1)S(1)} %slice.22), channel_id=1, source_target_pairs={{0,8},{8,16},{16,24},{24,32},{32,40},{40,48},{48,56},{56,64},{64,7... | collective-permute-start | bytes 18440 | tf_op jit(solution)/shard_map/ppermute | solution.py:348
  12.6 36.2 %copy-start.1 = (bf16[256,512]{1,0:T(8,128)(2,1)S(1)}, bf16[256,512]{1,0:T(8,128)(2,1)}, u32[]{:S(2)}) copy-start(bf16[256,512]{1,0:T(8,128)(2,1)} %dtp_ref.1) | copy-start | bytes 786436
  12.6 36.2 %copy-start.2 = (f32[512,16]{0,1:T(8,128)S(1)}, f32[512,16]{0,1:T(8,128)}, u32[]{:S(2)}) copy-start(f32[512,16]{0,1:T(8,128)} %param.29) | copy-start | bytes 98308
  12.6 36.2 %copy-start.6 = (f32[512]{0:T(512)S(1)}, f32[512]{0:T(512)}, u32[]{:S(2)}) copy-start(f32[512]{0:T(512)} %param.28) | copy-start | bytes 6148
  48.1 2.0 copy-start.9
  48.8 27.7 %copy-start = (bf16[512,4096]{1,0:T(8,128)(2,1)S(1)}, bf16[512,4096]{1,0:T(8,128)(2,1)}, u32[]{:S(2)}) copy-start(bf16[512,4096]{1,0:T(8,128)(2,1)} %outp_ref.1) | copy-start | bytes 12582916
  50.1 26.5 %copy-start.3 = (f32[2,512,16]{1,2,0:T(8,128)S(1)}, f32[2,512,16]{1,2,0:T(8,128)}, u32[]{:S(2)}) copy-start(f32[2,512,16]{1,2,0:T(8,128)} %param.31) | copy-start | bytes 196612
  50.1 26.5 %copy-start.7 = (f32[512]{0:T(512)S(1)}, f32[512]{0:T(512)}, u32[]{:S(2)}) copy-start(f32[512]{0:T(512)} %param.30) | copy-start | bytes 6148
  80.9 3.8 %copy-start.8 = (bf16[1,256,4096]{2,1,0:T(8,128)(2,1)S(1)}, bf16[1,256,4096]{2,1,0:T(8,128)(2,1)}, u32[]{:S(2)}) copy-start(bf16[1,256,4096]{2,1,0:T(8,128)(2,1)} %param.40) | copy-start | bytes 6291460
  80.9 33.3 %all-to-all-start.3 = ((bf16[8,128,512]{2,1,0:T(8,128)(2,1)}), bf16[8,128,512]{2,1,0:T(8,128)(2,1)S(1)}, u32[]{:S(2)}, u32[]{:S(2)}) async-start(bf16[8,128,512]{2,1,0:T(8,128)(2,1)} %scan.1), calls=%async_computation.3 | async-start | bytes 2097152 | tf_op jit(solution)/shard_map/all_to_all | solution.py:30
  84.7 3.7 %copy-start.12 = (bf16[4,4096]{1,0:T(4,128)(2,1)S(1)}, bf16[4,4096]{1,0:T(4,128)(2,1)}, u32[]{:S(2)}) copy-start(bf16[4,4096]{1,0:T(4,128)(2,1)} %param.35) | copy-start | bytes 98308
  84.7 3.7 %copy-start.13 = (s32[64,2,2]{0,2,1:T(2,128)S(1)}, s32[64,2,2]{0,2,1:T(2,128)}, u32[]{:S(2)}) copy-start(s32[64,2,2]{0,2,1:T(2,128)} %param.41) | copy-start | bytes 3076
  84.7 3.9 %copy-start.5 = (bf16[4096]{0:T(1024)(128)(2,1)S(1)}, bf16[4096]{0:T(1024)(128)(2,1)}, u32[]{:S(2)}) copy-start(bf16[4096]{0:T(1024)(128)(2,1)} %param.34) | copy-start | bytes 24580
  84.7 106.6 %all-gather.2.cloned.1.call-start = ((), (), s32[]{:S(2)}) async-start(), calls=%async_computation.9 | async-start | bytes 5570560 | tf_op jit(solution)/shard_map/all_gather | solution.py:433
  86.2 49.1 %copy-start.4 = (bf16[4096,8]{0,1:T(8,128)(2,1)S(1)}, bf16[4096,8]{0,1:T(8,128)(2,1)}, u32[]{:S(2)}) copy-start(bf16[4096,8]{0,1:T(8,128)(2,1)} %param.37) | copy-start | bytes 196612
  86.2 47.7 %collective-permute-start.4 = (bf16[128,4096]{1,0:T(8,128)(2,1)}, bf16[128,4096]{1,0:T(8,128)(2,1)S(1)}, u32[]{:S(2)}, u32[]{:S(2)}) collective-permute-start(bf16[128,4096]{1,0:T(8,128)(2,1)} %get-tuple-element.162), channel_id=1, source_target_pairs={{0,16},{8,24},{16,0},{24,8},{32,48},{40,56},{48,32},{56,40},{64,80... | collective-permute-start | bytes 3145736 | tf_op jit(solution)/shard_map/ppermute | solution.py:397
  133.9 63.1 %copy-start.10 = (bf16[128,4096]{1,0:T(8,128)(2,1)}, bf16[128,4096]{1,0:T(8,128)(2,1)S(1)}, u32[]{:S(2)}) copy-start(bf16[128,4096]{1,0:T(8,128)(2,1)S(1)} %collective-permute-done.4.refs_2_) | copy-start | bytes 3145732
  133.9 30.6 %collective-permute-start.5 = (bf16[128,4096]{1,0:T(8,128)(2,1)}, bf16[128,4096]{1,0:T(8,128)(2,1)S(1)}, u32[]{:S(2)}, u32[]{:S(2)}) collective-permute-start(bf16[128,4096]{1,0:T(8,128)(2,1)} %get-tuple-element.161), channel_id=1, source_target_pairs={{0,16},{8,24},{16,0},{24,8},{32,48},{40,56},{48,32},{56,40},{64,80... | collective-permute-start | bytes 3145736 | tf_op jit(solution)/shard_map/ppermute | solution.py:397
  136.6 27.9 %all-to-all-start.5 = ((f32[8,16,512]{2,1,0:T(8,128)}), f32[8,16,512]{2,1,0:T(8,128)S(1)}, u32[]{:S(2)}, u32[]{:S(2)}) async-start(f32[8,16,512]{2,1,0:T(8,128)} %bitcast.18), calls=%async_computation.5 | async-start | bytes 524288 | tf_op jit(solution)/shard_map/all_to_all | solution.py:30
  140.0 24.5 %collective-permute-start.6 = (bf16[128,4096]{1,0:T(8,128)(2,1)S(1)}, bf16[128,4096]{1,0:T(8,128)(2,1)}, u32[]{:S(2)}, u32[]{:S(2)}) collective-permute-start(bf16[128,4096]{1,0:T(8,128)(2,1)S(1)} %collective-permute-done.4.refs_2_), channel_id=1, source_target_pairs={{0,8},{8,0},{16,24},{24,16},{32,40},{40,32},{48,56},{56,48},{64,72... | collective-permute-start | bytes 3145736 | tf_op jit(solution)/shard_map/ppermute | solution.py:432
  164.5 32.5 %copy-start.11 = (bf16[128,4096]{1,0:T(8,128)(2,1)}, bf16[128,4096]{1,0:T(8,128)(2,1)S(1)}, u32[]{:S(2)}) copy-start(bf16[128,4096]{1,0:T(8,128)(2,1)S(1)} %collective-permute-done.5.refs_3_) | copy-start | bytes 3145732
  164.5 2.8 collective-permute-start.7
  197.1 9.7 %collective-permute-start.8 = (bf16[320,512]{1,0:T(8,128)(2,1)S(1)}, bf16[320,512]{1,0:T(8,128)(2,1)S(1)}, u32[]{:S(2)}, u32[]{:S(2)}) collective-permute-start(bf16[320,512]{1,0:T(8,128)(2,1)S(1)} %get-tuple-element.146), channel_id=1, source_target_pairs={{0,16},{8,24},{16,0},{24,8},{32,48},{40,56},{48,32},{56,40},{64,80... | collective-permute-start | bytes 983048 | tf_op jit(solution)/shard_map/ppermute | solution.py:463
Sparse Core Ops, SparseCore 0:
  134.1 57.1 all-gather.1

commit v6 on v5

--- a/solution.py
+++ b/solution.py
@@ -168,21 +168,14 @@
     out_ref[...] = vector
 
 
-def dispatch_kernel(mixed_ref, clean_ref, gain_ref, lanes_ref, res_ref, send_ref, slots_ref):
+def dispatch_kernel(mixed_ref, clean_ref, lanes_ref, res_ref, send_ref, slots_ref):
     experts, capacity, rows = slots_ref.shape
     width = res_ref.shape[1]
     residual = clean_ref[...]
     for j in range(mixed_ref.shape[0]):
         residual = residual + mixed_ref[j].astype(F32)
     res_ref[...] = residual
-    scaled = (residual * gain_ref[...].astype(F32)).astype(BF16)
-    square = jnp.sum(residual * residual, axis=1, keepdims=True)
-    high = square.astype(BF16).astype(F32)
-    middle = (square - high).astype(BF16).astype(F32)
-    low = square - high - middle
-    lane = lax.broadcasted_iota(jnp.int32, (rows, 128), 1)
-    extra = jnp.where(lane == 0, high, jnp.where(lane == 1, middle, jnp.where(lane == 2, low, 0.0)))
-    payload = jnp.concatenate([scaled, extra.astype(BF16)], axis=1)
+    payload = residual.astype(BF16)
     label = lax.broadcasted_iota(jnp.int32, (experts, rows), 0)
     member = (lanes_ref[0:1, :] == label) | (lanes_ref[1:2, :] == label)
     upper = lax.broadcasted_iota(jnp.int32, (rows, rows), 0) <= lax.broadcasted_iota(jnp.int32, (rows, rows), 1)
@@ -195,14 +188,16 @@
         send_ref[e] = dot(chosen, payload).astype(BF16)
 
 
-def normed_kernel(features, got_ref, out_ref):
-    width = out_ref.shape[1] // got_ref.shape[0]
-    total = jnp.zeros((out_ref.shape[0], 128), F32)
-    for j in range(got_ref.shape[0]):
-        total = total + got_ref[j, :, width:].astype(F32)
-    scale = lax.rsqrt(jnp.sum(total, axis=1, keepdims=True) / features + EPS)
-    for j in range(got_ref.shape[0]):
-        out_ref[:, j * width : (j + 1) * width] = (got_ref[j, :, :width].astype(F32) * scale).astype(BF16)
+def normed_kernel(got_ref, gain_ref, out_ref):
+    blocks, rows, width = got_ref.shape
+    total = jnp.zeros((rows, width), F32)
+    for j in range(blocks):
+        block = got_ref[j].astype(F32)
+        total = total + block * block
+    scale = lax.rsqrt(jnp.sum(total, axis=1, keepdims=True) / (blocks * width) + EPS)
+    for j in range(blocks):
+        at = slice(j * width, (j + 1) * width)
+        out_ref[:, at] = (got_ref[j].astype(F32) * scale * gain_ref[:, at].astype(F32)).astype(BF16)
 
 
 def share_kernel(owner_ref, x_ref, router_ref, slots_ref, rows_ref, out_ref):
@@ -260,26 +255,31 @@
 
 
 def second_kernel(parity_ref, x_ref, g0, u0, g1, u1, *refs):
-    sources, out_ref, held, x_held, x_sem, sem = refs[:6], refs[6], refs[7:11], refs[11], refs[12], refs[13]
+    sources, out_ref, held, hidden, x_held, x_sem, sem = refs[:6], refs[6], refs[7:9], refs[9:12], refs[12], refs[13], refs[14]
+    near, hidden = hidden[:2], hidden[2]
     x_copies = sliced(x_ref.at[:, parity_ref[0]], x_held, x_sem, x_sem.shape[0], 2)
     for copy in x_copies:
         copy.start()
     part = sources[2].shape[0]
-    targets = held[:2] + tuple(d.at[pl.ds(k * part, part)] for d in held[2:] for k in range(2))
+    targets = near + tuple(d.at[pl.ds(k * part, part)] for d in held for k in range(2))
     copies = fetched(sources, targets, sem)
-    hidden_of(x_held, x_copies, (g0, u0, g1, u1), (), out_ref)
-    for copy in copies:
+    hidden_of(x_held, x_copies, (g0, u0, g1, u1), (), hidden)
+    copies[0].wait()
+    copies[1].wait()
+    width = near[0].shape[0]
+    for j in range(0, out_ref.shape[1], 512):
+        at = slice(j, j + 512)
+        out_ref[:, at] = dot(hidden[:, :width], near[0][:, at]) + dot(hidden[:, width:], near[1][:, at])
+    for copy in copies[2:]:
         copy.wait()
 
 
-def down_kernel(own_ref, far_ref, d0, d1, d2, d3, out_ref):
-    width = d0.shape[0]
-    hidden = [ref[:, k * width : (k + 1) * width] for ref in (own_ref, far_ref) for k in range(2)]
+def down_kernel(sofar_ref, far_ref, d2, d3, out_ref):
+    width = d2.shape[0]
     for j in range(0, out_ref.shape[1], 512):
-        total = dot(hidden[0], d0[:, j : j + 512])
-        for h, d in zip(hidden[1:], (d1, d2, d3)):
-            total = total + dot(h, d[:, j : j + 512])
-        out_ref[:, j : j + 512] = total.astype(BF16)
+        at = slice(j, j + 512)
+        total = sofar_ref[:, at] + dot(far_ref[:, :width], d2[:, at]) + dot(far_ref[:, width:], d3[:, at])
+        out_ref[:, at] = total.astype(BF16)
 
 
 def weigh_kernel(got_ref, share_ref, out_ref):
@@ -409,23 +409,20 @@
     )
     start = owner * width
     clean = lax.dynamic_slice_in_dim(clean.reshape(1, d_model), start, width, 1)
-    gain = lax.dynamic_slice_in_dim(norm_gain[None], start, width, 1)
     ids = expert_ids.reshape(rows, top_count)
 
     residual, send, slots = call(
         dispatch_kernel,
         (
             shape((rows, width)),
-            shape((experts, capacity, width + 128), BF16),
+            shape((experts, capacity, width), BF16),
             shape((experts, capacity, rows), BF16),
         ),
-        [VM] * 4,
+        [VM] * 3,
         name="dispatch",
-    )(mixed, clean, gain, ids.T)
+    )(mixed, clean, ids.T)
     got = exchanged(send, "expert")
-    normed = call(
-        functools.partial(normed_kernel, float(d_model)), shape((capacity, d_model), BF16), [VM], name="normed"
-    )(got)
+    normed = call(normed_kernel, shape((capacity, d_model), BF16), [VM] * 2, name="normed")(got, norm_gain[None])
 
     same_core = [[i for i in range(n_seq) if i % 2 == c] for c in range(2)]
     normed, far_a = fence(normed, far_a)
@@ -461,12 +458,12 @@
         name="first",
     )(parity, pieces, *(pltpu.with_memory_space_constraint(v, pltpu.HBM) for v in ups))
     given = lax.ppermute(theirs, "seq", across)
-    kept, *downs = pl.pallas_call(
+    sofar, *downs = pl.pallas_call(
         second_kernel,
-        out_shape=(shape((half, inner), BF16),) + (pltpu.VMEM(down_w.shape, BF16),) * 4,
+        out_shape=(pltpu.VMEM((half, d_model), F32),) + (pltpu.VMEM(down_w.shape, BF16),) * 2,
         in_specs=[SCALAR, hbm] + [VM] * 4 + [hbm] * 6,
-        out_specs=(VM,) * 5,
-        scratch_shapes=held_rows + [dma((6,))],
+        out_specs=(VM,) * 3,
+        scratch_shapes=[pltpu.VMEM(down_w.shape, BF16)] * 2 + [pltpu.VMEM((half, inner), BF16)] + held_rows + [dma((6,))],
         compiler_params=pltpu.CompilerParams(vmem_limit_bytes=16 * 1024 * 1024),
         cost_estimate=pl.CostEstimate(flops=4 * half * inner * d_model, bytes_accessed=1 << 24, transcendentals=0),
         name="second",
@@ -474,11 +471,11 @@
     partial = pl.pallas_call(
         down_kernel,
         out_shape=pltpu.VMEM((half, d_model), BF16),
-        in_specs=[VM] * 6,
+        in_specs=[VM] * 4,
         out_specs=VM,
         compiler_params=pltpu.CompilerParams(vmem_limit_bytes=16 * 1024 * 1024),
         name="down",
-    )(kept, given, *downs)
+    )(sofar, given, *downs)
     kinds = [[i for i in range(n_seq) if i % 4 == k] for k in range(4)]
     partial, share, slots, own_residual = fence(partial, share, slots, own_residual)
     partial = exchanged(partial, "seq", kinds).reshape(pairs, capacity, d_model)

time: 286 us -> 284 us (level)
  blocking collectives: 141 us -> 123 us
  waiting for transfers between devices: 81.5 us -> 94.1 us
  starting transfers between devices: 13.8 us -> 17.2 us
    all_to_all x7 -> x6, blocking collectives: 141 us -> 123 us  [exchanged(): lax.all_to_all(blocks, axis, 0, 0, tiled=True, axis_index_groups=groups)]
    all_to_all x2 -> x3, waiting for transfers between devices: 24.1 us -> 38.5 us  [exchanged(): lax.all_to_all(blocks, axis, 0, 0, tiled=True, axis_index_groups=groups)]
    all_to_all x2 -> x3, starting transfers between devices: 7.12 us -> 10.6 us  [exchanged(): lax.all_to_all(blocks, axis, 0, 0, tiled=True, axis_index_groups=groups)]
  transfers between devices with their start and end apart: 12 -> 13, of which waited for: 6 -> 7; matrix products, arithmetic and copies ran while one was open for 3% -> 2% of each run, Pallas kernels for 4% -> 4%
where the time goes in v6:
time: 284 us; the launch traced here: 283 us
  blocking collectives  123 us (43%)
  waiting for transfers between devices  94.1 us (33%)
  Pallas kernels  27.1 us (10%)
  starting transfers between devices  17.2 us (6%)
  between operations  13.8 us (5%)
  local copies, waits for them, and re-layouts  7.48 us (3%)
    all_to_all x6, blocking collectives, exchanged(): lax.all_to_all(blocks, axis, 0, 0, tiled=True, axis_index_groups=groups)  123 us
    all_to_all x3, waiting for transfers between devices, exchanged(): lax.all_to_all(blocks, axis, 0, 0, tiled=True, axis_index_groups=groups)  38.5 us
    ppermute x2, waiting for transfers between devices, shards(): lax.ppermute(down_w[k * part:(k + 1) * part], 'seq', across)  24.4 us
    all_gather x1, waiting for transfers between devices, shards(): lax.all_gather(normed, 'seq', axis=0, tiled=True, axis_index_groups=same_...  23.7 us
    all_to_all x3, starting transfers between devices, exchanged(): lax.all_to_all(blocks, axis, 0, 0, tiled=True, axis_index_groups=groups)  10.6 us
    pallas_call x1, Pallas kernels, shards(): pl.pallas_call(second_kernel, out_shape=(pltpu.VMEM((half, d_model), F32)...  5.93 us
    pallas_call x1, Pallas kernels, shards(): pl.pallas_call(first_kernel, out_shape=(shape((half, inner), BF16),) + tu...  5.74 us
  transfers between devices with their start and end apart: 13, of which 7 were waited for; matrix products, arithmetic and copies ran while one was open for 2% of the time, Pallas kernels for 4%

profile of v6, /device:TPU:2, one launch (start us, length us, event | category | flops | bytes accessed | tf_op | source)
XLA Modules:
  0.0 283.2 jit_solution(16755004263162509865)
XLA Ops:
  7.8 2.4 collective-permute-start
  10.3 1.0 reshape.49.x_ref
  12.6 1.0 reshape.52.own_ref
  13.6 1.0 reshape.51.gate_ref
  14.6 1.7 collective-permute-done.got_ref
  16.3 1.3 conv.1
  17.6 19.3 %all_to_all.61.got_ref = f32[8,16,288]{2,1,0:T(8,128)S(1)} all-to-all(f32[8,16,288]{2,1,0:T(8,128)S(1)} %bitcast.33), channel_id=1, replica_groups=mesh['seq'=32,'expert'=8] {'expert'}, dimensions={0} | all-to-all | bytes 294912 | tf_op jit(solution)/shard_map/all_to_all | solution.py:30
  37.0 11.1 %all_to_all.62 = bf16[8,16,384]{2,1,0:T(8,128)(2,1)S(1)} all-to-all(bf16[8,16,384]{2,1,0:T(8,128)(2,1)S(1)} %sum.1), channel_id=1, replica_groups=mesh['seq'=32,'expert'=8] {'expert'}, dimensions={0} | all-to-all | bytes 196608 | tf_op jit(solution)/shard_map/all_to_all | solution.py:30
  48.8 1.2 local.1
  50.2 26.3 %all_to_all.63.all_ref = bf16[32,40,512]{2,1,0:T(8,128)(2,1)S(1)} all-to-all(bf16[32,40,512]{2,1,0:T(8,128)(2,1)S(1)} %broadcast_in_dim.36), channel_id=1, replica_groups=mesh['seq'=32,'expert'=8] {'seq'}, dimensions={0} | all-to-all | bytes 2621440 | tf_op jit(solution)/shard_map/all_to_all | solution.py:30
  76.6 4.3 %scan.1 = bf16[8,128,512]{2,1,0:T(8,128)(2,1)} custom-call(s32[2]{0:T(128)S(1)} %pad_add_fusion.ids_ref, bf16[32,40,512]{2,1,0:T(8,128)(2,1)S(1)} %all_to_all.63.all_ref, f32[2,16,512]{2,1,0:T(8,128)S(1)} %bitcast.37, f32[128,512]{1,0:T(8,128)S(1)} %get-tuple-element.111.step_ref, f32[128,512]{1,0:T(8,128)S(1)} %get-tuple-element.112.act_ref, ...), custom_call_target="tpu_custom_call" | custom-call | tf_op jit(solution)/shard_map/scan/pallas_call | solution.py:398
  80.9 3.7 %all-to-all-start.3 = ((bf16[8,128,512]{2,1,0:T(8,128)(2,1)}), bf16[8,128,512]{2,1,0:T(8,128)(2,1)S(1)}, u32[]{:S(2)}, u32[]{:S(2)}) async-start(bf16[8,128,512]{2,1,0:T(8,128)(2,1)} %scan.1), calls=%async_computation.3 | async-start | bytes 2097152 | tf_op jit(solution)/shard_map/all_to_all | solution.py:30
  84.7 1.5 fusion
  86.2 1.4 collective-permute-start.4
  87.8 1.5 clean.1
  89.3 24.9 %all-to-all-done.3.mixed_ref = bf16[8,128,512]{2,1,0:T(8,128)(2,1)S(1)} async-done(((bf16[8,128,512]{2,1,0:T(8,128)(2,1)}), bf16[8,128,512]{2,1,0:T(8,128)(2,1)S(1)}, u32[]{:S(2)}, u32[]{:S(2)}) %all-to-all-start.3) | async-done | bytes 1048608 | tf_op jit(solution)/shard_map/all_to_all | solution.py:30
  114.2 1.2 dispatch.1
  115.4 3.4 %all-to-all-start.4 = ((bf16[8,40,512]{2,1,0:T(8,128)(2,1)}), bf16[8,40,512]{2,1,0:T(8,128)(2,1)S(1)}, u32[]{:S(2)}, u32[]{:S(2)}) async-start(bf16[8,40,512]{2,1,0:T(8,128)(2,1)} %get-tuple-element.121), calls=%async_computation.4 | async-start | bytes 655360 | tf_op jit(solution)/shard_map/all_to_all | solution.py:30
  118.9 13.6 %all-to-all-done.4.got_ref = bf16[8,40,512]{2,1,0:T(8,128)(2,1)S(1)} async-done(((bf16[8,40,512]{2,1,0:T(8,128)(2,1)}), bf16[8,40,512]{2,1,0:T(8,128)(2,1)S(1)}, u32[]{:S(2)}, u32[]{:S(2)}) %all-to-all-start.4) | async-done | bytes 327712 | tf_op jit(solution)/shard_map/all_to_all | solution.py:30
  133.5 1.4 collective-permute-start.5
  134.8 1.3 share.1.share_ref
  136.2 3.4 %all-to-all-start.5 = ((f32[8,16,512]{2,1,0:T(8,128)}), f32[8,16,512]{2,1,0:T(8,128)S(1)}, u32[]{:S(2)}, u32[]{:S(2)}) async-start(f32[8,16,512]{2,1,0:T(8,128)} %bitcast.18), calls=%async_computation.5 | async-start | bytes 524288 | tf_op jit(solution)/shard_map/all_to_all | solution.py:30
  139.7 24.4 %collective-permute-done.5.refs_3_ = bf16[128,4096]{1,0:T(8,128)(2,1)S(1)} collective-permute-done((bf16[128,4096]{1,0:T(8,128)(2,1)}, bf16[128,4096]{1,0:T(8,128)(2,1)S(1)}, u32[]{:S(2)}, u32[]{:S(2)}) %collective-permute-start.5) | collective-permute-done | bytes 1048608 | tf_op jit(solution)/shard_map/ppermute | solution.py:397
  164.2 2.8 collective-permute-done.7.refs_5_
  166.9 23.7 %all-gather.2.cloned.1.call-done = bf16[640,4096]{1,0:T(8,128)(2,1)} async-done(((bf16[40,4096]{1,0:T(8,128)(2,1)}), bf16[640,4096]{1,0:T(8,128)(2,1)}) %all-gather.2.cloned.1.call-update) | async-done | bytes 5242896 | tf_op jit(solution)/shard_map/all_gather | solution.py:430
  190.6 5.7 %first.1 = (bf16[320,512]{1,0:T(8,128)(2,1)S(1)}, bf16[4096,256]{1,0:T(8,128)(2,1)S(1)}, bf16[4096,256]{1,0:T(8,128)(2,1)S(1)}, bf16[4096,256]{1,0:T(8,128)(2,1)S(1)}, bf16[4096,256]{1,0:T(8,128)(2,1)S(1)}) custom-call(s32[1]{0:T(128)} %bitcast.parity_ref, bf16[8,2,40,4096]{3,2,1,0:T(8,128)(2,1)} %bitcast.43, bf16[4096,256]{1,0:T(8,128)(2,1)} %bitcast.49, ...), custom_call_target="tpu_custom_call" | custom-call | tf_op jit(solution)/shard_map/first/pallas_call | solution.py:451
  197.2 5.9 %second.1 = (f32[320,4096]{1,0:T(8,128)S(1)}, bf16[256,4096]{1,0:T(8,128)(2,1)S(1)}, bf16[256,4096]{1,0:T(8,128)(2,1)S(1)}) custom-call(s32[1]{0:T(128)} %bitcast.parity_ref, bf16[8,2,40,4096]{3,2,1,0:T(8,128)(2,1)} %bitcast.44, bf16[4096,256]{1,0:T(8,128)(2,1)S(1)} %get-tuple-element.136.g0, bf16[4096,256]{1,0:T(8,128)(2,1)S(1)} %get-tuple-element.137.u0, ...), custom_call_target="tpu_custom_call" | custom-call | flops 2684354560 | bytes 16777216 | tf_op jit(solution)/shard_map/second/pallas_call | solution.py:461
  203.1 3.0 %collective-permute-done.8.far_ref = bf16[320,512]{1,0:T(8,128)(2,1)S(1)} collective-permute-done((bf16[320,512]{1,0:T(8,128)(2,1)S(1)}, bf16[320,512]{1,0:T(8,128)(2,1)S(1)}, u32[]{:S(2)}, u32[]{:S(2)}) %collective-permute-start.8) | collective-permute-done | bytes 327712 | tf_op jit(solution)/shard_map/ppermute | solution.py:460
  206.1 1.5 down.1
  207.6 37.2 %all_to_all.64.got_ref = bf16[8,40,4096]{2,1,0:T(8,128)(2,1)S(1)} all-to-all(bf16[8,40,4096]{2,1,0:T(8,128)(2,1)S(1)} %bitcast.27), channel_id=1, replica_groups={{0,32,64,96,128,160,192,224},{8,40,72,104,136,168,200,232},{16,48,80,11..., dimensions={0} | all-to-all | bytes 5242880 | tf_op jit(solution)/shard_map/all_to_all | solution.py:30
  245.7 18.0 %all_to_all.65.got_ref = bf16[8,40,512]{2,1,0:T(8,128)(2,1)S(1)} all-to-all(bf16[8,40,512]{2,1,0:T(8,128)(2,1)S(1)} %weigh.1), channel_id=1, replica_groups=mesh['seq'=32,'expert'=8] {'expert'}, dimensions={0} | all-to-all | bytes 655360 | tf_op jit(solution)/shard_map/all_to_all | solution.py:30
  264.1 11.5 %all_to_all.66.got_ref = bf16[8,16,512]{2,1,0:T(8,128)(2,1)S(1)} all-to-all(bf16[8,16,512]{2,1,0:T(8,128)(2,1)S(1)} %bitcast.32), channel_id=1, replica_groups=mesh['seq'=32,'expert'=8] {'expert'}, dimensions={0} | all-to-all | bytes 262144 | tf_op jit(solution)/shard_map/all_to_all | solution.py:30
  (62 shorter events, 7.7 us)
Async XLA Ops:
  6.5 41.5 %collective-permute-start.1 = (bf16[4096,256]{1,0:T(8,128)(2,1)}, bf16[4096,256]{1,0:T(8,128)(2,1)}, u32[]{:S(2)}, u32[]{:S(2)}) collective-permute-start(bf16[4096,256]{1,0:T(8,128)(2,1)} %bitcast.48), channel_id=1, source_target_pairs={{0,8},{8,0},{16,24},{24,16},{32,40},{40,32},{48,56},{56,48},{64,72... | collective-permute-start | bytes 6291464 | tf_op jit(solution)/shard_map/ppermute | solution.py:344
  6.5 41.5 %collective-permute-start.2 = (bf16[4096,256]{1,0:T(8,128)(2,1)}, bf16[4096,256]{1,0:T(8,128)(2,1)}, u32[]{:S(2)}, u32[]{:S(2)}) collective-permute-start(bf16[4096,256]{1,0:T(8,128)(2,1)} %bitcast.50), channel_id=1, source_target_pairs={{0,8},{8,0},{16,24},{24,16},{32,40},{40,32},{48,56},{56,48},{64,72... | collective-permute-start | bytes 6291464 | tf_op jit(solution)/shard_map/ppermute | solution.py:344
  7.0 41.0 %collective-permute-start.3 = (bf16[256,4096]{1,0:T(8,128)(2,1)}, bf16[256,4096]{1,0:T(8,128)(2,1)S(1)}, u32[]{:S(2)}, u32[]{:S(2)}) collective-permute-start(bf16[256,4096]{1,0:T(8,128)(2,1)} %bitcast.45), channel_id=1, source_target_pairs={{0,8},{8,0},{16,24},{24,16},{32,40},{40,32},{48,56},{56,48},{64,72... | collective-permute-start | bytes 6291464 | tf_op jit(solution)/shard_map/ppermute | solution.py:344
  7.8 8.6 %collective-permute-start = (bf16[6,512]{1,0:T(8,128)(2,1)S(1)}, bf16[6,512]{1,0:T(8,128)(2,1)S(1)}, u32[]{:S(2)}, u32[]{:S(2)}) collective-permute-start(bf16[6,512]{1,0:T(8,128)(2,1)S(1)} %slice.22), channel_id=1, source_target_pairs={{0,8},{8,16},{16,24},{24,32},{32,40},{40,48},{48,56},{56,64},{64,7... | collective-permute-start | bytes 18440 | tf_op jit(solution)/shard_map/ppermute | solution.py:348
  12.6 36.2 %copy-start.1 = (bf16[256,512]{1,0:T(8,128)(2,1)S(1)}, bf16[256,512]{1,0:T(8,128)(2,1)}, u32[]{:S(2)}) copy-start(bf16[256,512]{1,0:T(8,128)(2,1)} %dtp_ref.1) | copy-start | bytes 786436
  12.6 36.2 %copy-start.2 = (f32[512,16]{0,1:T(8,128)S(1)}, f32[512,16]{0,1:T(8,128)}, u32[]{:S(2)}) copy-start(f32[512,16]{0,1:T(8,128)} %param.29) | copy-start | bytes 98308
  12.6 36.2 %copy-start.6 = (f32[512]{0:T(512)S(1)}, f32[512]{0:T(512)}, u32[]{:S(2)}) copy-start(f32[512]{0:T(512)} %param.28) | copy-start | bytes 6148
  48.1 2.0 copy-start.9
  48.8 27.7 %copy-start = (bf16[512,4096]{1,0:T(8,128)(2,1)S(1)}, bf16[512,4096]{1,0:T(8,128)(2,1)}, u32[]{:S(2)}) copy-start(bf16[512,4096]{1,0:T(8,128)(2,1)} %outp_ref.1) | copy-start | bytes 12582916
  50.1 26.5 %copy-start.3 = (f32[2,512,16]{1,2,0:T(8,128)S(1)}, f32[2,512,16]{1,2,0:T(8,128)}, u32[]{:S(2)}) copy-start(f32[2,512,16]{1,2,0:T(8,128)} %param.31) | copy-start | bytes 196612
  50.1 26.5 %copy-start.7 = (f32[512]{0:T(512)S(1)}, f32[512]{0:T(512)}, u32[]{:S(2)}) copy-start(f32[512]{0:T(512)} %param.30) | copy-start | bytes 6148
  80.9 3.7 %copy-start.8 = (bf16[1,256,4096]{2,1,0:T(8,128)(2,1)S(1)}, bf16[1,256,4096]{2,1,0:T(8,128)(2,1)}, u32[]{:S(2)}) copy-start(bf16[1,256,4096]{2,1,0:T(8,128)(2,1)} %param.40) | copy-start | bytes 6291460
  80.9 33.3 %all-to-all-start.3 = ((bf16[8,128,512]{2,1,0:T(8,128)(2,1)}), bf16[8,128,512]{2,1,0:T(8,128)(2,1)S(1)}, u32[]{:S(2)}, u32[]{:S(2)}) async-start(bf16[8,128,512]{2,1,0:T(8,128)(2,1)} %scan.1), calls=%async_computation.3 | async-start | bytes 2097152 | tf_op jit(solution)/shard_map/all_to_all | solution.py:30
  84.6 3.0 %copy-start.12 = (bf16[4,4096]{1,0:T(4,128)(2,1)S(1)}, bf16[4,4096]{1,0:T(4,128)(2,1)}, u32[]{:S(2)}) copy-start(bf16[4,4096]{1,0:T(4,128)(2,1)} %param.35) | copy-start | bytes 98308
  84.7 3.0 %copy-start.14 = (s32[64,2,2]{0,2,1:T(2,128)S(1)}, s32[64,2,2]{0,2,1:T(2,128)}, u32[]{:S(2)}) copy-start(s32[64,2,2]{0,2,1:T(2,128)} %param.41) | copy-start | bytes 3076
  84.7 3.1 %copy-start.5 = (bf16[4096]{0:T(1024)(128)(2,1)S(1)}, bf16[4096]{0:T(1024)(128)(2,1)}, u32[]{:S(2)}) copy-start(bf16[4096]{0:T(1024)(128)(2,1)} %param.34) | copy-start | bytes 24580
  84.7 34.2 %copy-start.13 = (bf16[4096]{0:T(1024)(128)(2,1)S(1)}, bf16[4096]{0:T(1024)(128)(2,1)}, u32[]{:S(2)}) copy-start(bf16[4096]{0:T(1024)(128)(2,1)} %param.36) | copy-start | bytes 24580
  86.2 48.7 %copy-start.4 = (bf16[4096,8]{0,1:T(8,128)(2,1)S(1)}, bf16[4096,8]{0,1:T(8,128)(2,1)}, u32[]{:S(2)}) copy-start(bf16[4096,8]{0,1:T(8,128)(2,1)} %param.37) | copy-start | bytes 196612
  86.2 47.3 %collective-permute-start.4 = (bf16[128,4096]{1,0:T(8,128)(2,1)}, bf16[128,4096]{1,0:T(8,128)(2,1)S(1)}, u32[]{:S(2)}, u32[]{:S(2)}) collective-permute-start(bf16[128,4096]{1,0:T(8,128)(2,1)} %get-tuple-element.158), channel_id=1, source_target_pairs={{0,16},{8,24},{16,0},{24,8},{32,48},{40,56},{48,32},{56,40},{64,80... | collective-permute-start | bytes 3145736 | tf_op jit(solution)/shard_map/ppermute | solution.py:397
  115.4 17.1 %all-to-all-start.4 = ((bf16[8,40,512]{2,1,0:T(8,128)(2,1)}), bf16[8,40,512]{2,1,0:T(8,128)(2,1)S(1)}, u32[]{:S(2)}, u32[]{:S(2)}) async-start(bf16[8,40,512]{2,1,0:T(8,128)(2,1)} %get-tuple-element.121), calls=%async_computation.4 | async-start | bytes 655360 | tf_op jit(solution)/shard_map/all_to_all | solution.py:30
  118.8 71.8 %all-gather.2.cloned.1.call-start = ((), (), s32[]{:S(2)}) async-start(), calls=%async_computation.9 | async-start | bytes 5570560 | tf_op jit(solution)/shard_map/all_gather | solution.py:430
  133.5 62.9 %copy-start.10 = (bf16[128,4096]{1,0:T(8,128)(2,1)}, bf16[128,4096]{1,0:T(8,128)(2,1)S(1)}, u32[]{:S(2)}) copy-start(bf16[128,4096]{1,0:T(8,128)(2,1)S(1)} %collective-permute-done.4.refs_2_) | copy-start | bytes 3145732
  133.5 30.7 %collective-permute-start.5 = (bf16[128,4096]{1,0:T(8,128)(2,1)}, bf16[128,4096]{1,0:T(8,128)(2,1)S(1)}, u32[]{:S(2)}, u32[]{:S(2)}) collective-permute-start(bf16[128,4096]{1,0:T(8,128)(2,1)} %get-tuple-element.157), channel_id=1, source_target_pairs={{0,16},{8,24},{16,0},{24,8},{32,48},{40,56},{48,32},{56,40},{64,80... | collective-permute-start | bytes 3145736 | tf_op jit(solution)/shard_map/ppermute | solution.py:397
  136.2 28.0 %all-to-all-start.5 = ((f32[8,16,512]{2,1,0:T(8,128)}), f32[8,16,512]{2,1,0:T(8,128)S(1)}, u32[]{:S(2)}, u32[]{:S(2)}) async-start(f32[8,16,512]{2,1,0:T(8,128)} %bitcast.18), calls=%async_computation.5 | async-start | bytes 524288 | tf_op jit(solution)/shard_map/all_to_all | solution.py:30
  139.6 24.6 %collective-permute-start.6 = (bf16[128,4096]{1,0:T(8,128)(2,1)S(1)}, bf16[128,4096]{1,0:T(8,128)(2,1)}, u32[]{:S(2)}, u32[]{:S(2)}) collective-permute-start(bf16[128,4096]{1,0:T(8,128)(2,1)S(1)} %collective-permute-done.4.refs_2_), channel_id=1, source_target_pairs={{0,8},{8,0},{16,24},{24,16},{32,40},{40,32},{48,56},{56,48},{64,72... | collective-permute-start | bytes 3145736 | tf_op jit(solution)/shard_map/ppermute | solution.py:429
  164.1 32.2 %copy-start.11 = (bf16[128,4096]{1,0:T(8,128)(2,1)}, bf16[128,4096]{1,0:T(8,128)(2,1)S(1)}, u32[]{:S(2)}) copy-start(bf16[128,4096]{1,0:T(8,128)(2,1)S(1)} %collective-permute-done.5.refs_3_) | copy-start | bytes 3145732
  164.1 2.8 collective-permute-start.7
  196.4 9.7 %collective-permute-start.8 = (bf16[320,512]{1,0:T(8,128)(2,1)S(1)}, bf16[320,512]{1,0:T(8,128)(2,1)S(1)}, u32[]{:S(2)}, u32[]{:S(2)}) collective-permute-start(bf16[320,512]{1,0:T(8,128)(2,1)S(1)} %get-tuple-element.144), channel_id=1, source_target_pairs={{0,16},{8,24},{16,0},{24,8},{32,48},{40,56},{48,32},{56,40},{64,80... | collective-permute-start | bytes 983048 | tf_op jit(solution)/shard_map/ppermute | solution.py:460
Sparse Core Ops, SparseCore 0:
  133.6 56.9 all-gather.1

commit v7 on v6

--- a/solution.py
+++ b/solution.py
@@ -410,6 +410,7 @@
     start = owner * width
     clean = lax.dynamic_slice_in_dim(clean.reshape(1, d_model), start, width, 1)
     ids = expert_ids.reshape(rows, top_count)
+    gain = norm_gain[None]
 
     residual, send, slots = call(
         dispatch_kernel,
@@ -421,8 +422,9 @@
         [VM] * 3,
         name="dispatch",
     )(mixed, clean, ids.T)
+    send, gain = fence(send, gain)
     got = exchanged(send, "expert")
-    normed = call(normed_kernel, shape((capacity, d_model), BF16), [VM] * 2, name="normed")(got, norm_gain[None])
+    normed = call(normed_kernel, shape((capacity, d_model), BF16), [VM] * 2, name="normed")(got, gain)
 
     same_core = [[i for i in range(n_seq) if i % 2 == c] for c in range(2)]
     normed, far_a = fence(normed, far_a)

time: 284 us -> 283 us (level)
  blocking collectives: 123 us -> 140 us
  waiting for transfers between devices: 94.1 us -> 80.6 us
  starting transfers between devices: 17.2 us -> 13.8 us
    all_to_all x6 -> x7, blocking collectives: 123 us -> 140 us  [exchanged(): lax.all_to_all(blocks, axis, 0, 0, tiled=True, axis_index_groups=groups)]
    all_to_all x3 -> x2, waiting for transfers between devices: 38.5 us -> 24.8 us  [exchanged(): lax.all_to_all(blocks, axis, 0, 0, tiled=True, axis_index_groups=groups)]
    all_to_all x3 -> x2, starting transfers between devices: 10.6 us -> 7.12 us  [exchanged(): lax.all_to_all(blocks, axis, 0, 0, tiled=True, axis_index_groups=groups)]
  transfers between devices with their start and end apart: 13 -> 12, of which waited for: 7 -> 6; matrix products, arithmetic and copies ran while one was open for 2% -> 2% of each run, Pallas kernels for 4% -> 4%
where the time goes in v7:
time: 283 us; the launch traced here: 282 us
  blocking collectives  140 us (49%)
  waiting for transfers between devices  80.6 us (28%)
  Pallas kernels  26.7 us (9%)
  starting transfers between devices  13.8 us (5%)
  between operations  13.8 us (5%)
  local copies, waits for them, and re-layouts  7.46 us (3%)
    all_to_all x7, blocking collectives, exchanged(): lax.all_to_all(blocks, axis, 0, 0, tiled=True, axis_index_groups=groups)  140 us
    all_to_all x2, waiting for transfers between devices, exchanged(): lax.all_to_all(blocks, axis, 0, 0, tiled=True, axis_index_groups=groups)  24.8 us
    all_gather x1, waiting for transfers between devices, shards(): lax.all_gather(normed, 'seq', axis=0, tiled=True, axis_index_groups=same_...  24.5 us
    ppermute x2, waiting for transfers between devices, shards(): lax.ppermute(down_w[k * part:(k + 1) * part], 'seq', across)  23.8 us
    all_to_all x2, starting transfers between devices, exchanged(): lax.all_to_all(blocks, axis, 0, 0, tiled=True, axis_index_groups=groups)  7.12 us
    pallas_call x1, Pallas kernels, shards(): pl.pallas_call(second_kernel, out_shape=(pltpu.VMEM((half, d_model), F32)...  5.93 us
    pallas_call x1, Pallas kernels, shards(): pl.pallas_call(first_kernel, out_shape=(shape((half, inner), BF16),) + tu...  5.74 us
  transfers between devices with their start and end apart: 12, of which 6 were waited for; matrix products, arithmetic and copies ran while one was open for 2% of the time, Pallas kernels for 4%

profile of v7, /device:TPU:2, one launch (start us, length us, event | category | flops | bytes accessed | tf_op | source)
XLA Modules:
  0.0 282.1 jit_solution(5009130213241851222)
XLA Ops:
  7.8 2.4 collective-permute-start
  10.3 1.0 reshape.49.x_ref
  12.6 1.0 reshape.52.own_ref
  13.6 1.0 reshape.51.gate_ref
  14.6 1.7 collective-permute-done.got_ref
  16.3 1.3 conv.1
  17.6 19.3 %all_to_all.61.got_ref = f32[8,16,288]{2,1,0:T(8,128)S(1)} all-to-all(f32[8,16,288]{2,1,0:T(8,128)S(1)} %bitcast.33), channel_id=1, replica_groups=mesh['seq'=32,'expert'=8] {'expert'}, dimensions={0} | all-to-all | bytes 294912 | tf_op jit(solution)/shard_map/all_to_all | solution.py:30
  37.0 11.1 %all_to_all.62 = bf16[8,16,384]{2,1,0:T(8,128)(2,1)S(1)} all-to-all(bf16[8,16,384]{2,1,0:T(8,128)(2,1)S(1)} %sum.1), channel_id=1, replica_groups=mesh['seq'=32,'expert'=8] {'expert'}, dimensions={0} | all-to-all | bytes 196608 | tf_op jit(solution)/shard_map/all_to_all | solution.py:30
  48.8 1.2 local.1
  50.2 26.3 %all_to_all.63.all_ref = bf16[32,40,512]{2,1,0:T(8,128)(2,1)S(1)} all-to-all(bf16[32,40,512]{2,1,0:T(8,128)(2,1)S(1)} %broadcast_in_dim.36), channel_id=1, replica_groups=mesh['seq'=32,'expert'=8] {'seq'}, dimensions={0} | all-to-all | bytes 2621440 | tf_op jit(solution)/shard_map/all_to_all | solution.py:30
  76.6 4.4 %scan.1 = bf16[8,128,512]{2,1,0:T(8,128)(2,1)} custom-call(s32[2]{0:T(128)S(1)} %pad_add_fusion.ids_ref, bf16[32,40,512]{2,1,0:T(8,128)(2,1)S(1)} %all_to_all.63.all_ref, f32[2,16,512]{2,1,0:T(8,128)S(1)} %bitcast.37, f32[128,512]{1,0:T(8,128)S(1)} %get-tuple-element.113.step_ref, f32[128,512]{1,0:T(8,128)S(1)} %get-tuple-element.114.act_ref, ...), custom_call_target="tpu_custom_call" | custom-call | tf_op jit(solution)/shard_map/scan/pallas_call | solution.py:398
  80.9 3.7 %all-to-all-start.3 = ((bf16[8,128,512]{2,1,0:T(8,128)(2,1)}), bf16[8,128,512]{2,1,0:T(8,128)(2,1)S(1)}, u32[]{:S(2)}, u32[]{:S(2)}) async-start(bf16[8,128,512]{2,1,0:T(8,128)(2,1)} %scan.1), calls=%async_computation.3 | async-start | bytes 2097152 | tf_op jit(solution)/shard_map/all_to_all | solution.py:30
  84.8 1.5 fusion
  86.2 1.4 collective-permute-start.4
  87.9 1.5 clean.1
  89.4 24.8 %all-to-all-done.3.mixed_ref = bf16[8,128,512]{2,1,0:T(8,128)(2,1)S(1)} async-done(((bf16[8,128,512]{2,1,0:T(8,128)(2,1)}), bf16[8,128,512]{2,1,0:T(8,128)(2,1)S(1)}, u32[]{:S(2)}, u32[]{:S(2)}) %all-to-all-start.3) | async-done | bytes 1048608 | tf_op jit(solution)/shard_map/all_to_all | solution.py:30
  114.3 0.9 dispatch.1
  115.1 16.2 %all_to_all.64.got_ref = bf16[8,40,512]{2,1,0:T(8,128)(2,1)S(1)} all-to-all(bf16[8,40,512]{2,1,0:T(8,128)(2,1)S(1)} %get-tuple-element.125), channel_id=1, replica_groups=mesh['seq'=32,'expert'=8] {'expert'}, dimensions={0} | all-to-all | bytes 655360 | tf_op jit(solution)/shard_map/all_to_all | solution.py:30
  131.3 0.9 normed.1.x_ref
  132.2 1.4 collective-permute-start.5
  133.5 1.3 share.1.share_ref
  134.9 3.4 %all-to-all-start.5 = ((f32[8,16,512]{2,1,0:T(8,128)}), f32[8,16,512]{2,1,0:T(8,128)S(1)}, u32[]{:S(2)}, u32[]{:S(2)}) async-start(f32[8,16,512]{2,1,0:T(8,128)} %bitcast.18), calls=%async_computation.5 | async-start | bytes 524288 | tf_op jit(solution)/shard_map/all_to_all | solution.py:30
  138.4 23.8 %collective-permute-done.5.refs_3_ = bf16[128,4096]{1,0:T(8,128)(2,1)S(1)} collective-permute-done((bf16[128,4096]{1,0:T(8,128)(2,1)}, bf16[128,4096]{1,0:T(8,128)(2,1)S(1)}, u32[]{:S(2)}, u32[]{:S(2)}) %collective-permute-start.5) | collective-permute-done | bytes 1048608 | tf_op jit(solution)/shard_map/ppermute | solution.py:397
  162.3 2.8 collective-permute-done.7.refs_5_
  165.0 24.5 %all-gather.2.cloned.1.call-done = bf16[640,4096]{1,0:T(8,128)(2,1)} async-done(((bf16[40,4096]{1,0:T(8,128)(2,1)}), bf16[640,4096]{1,0:T(8,128)(2,1)}) %all-gather.2.cloned.1.call-update) | async-done | bytes 5242896 | tf_op jit(solution)/shard_map/all_gather | solution.py:432
  189.5 5.7 %first.1 = (bf16[320,512]{1,0:T(8,128)(2,1)S(1)}, bf16[4096,256]{1,0:T(8,128)(2,1)S(1)}, bf16[4096,256]{1,0:T(8,128)(2,1)S(1)}, bf16[4096,256]{1,0:T(8,128)(2,1)S(1)}, bf16[4096,256]{1,0:T(8,128)(2,1)S(1)}) custom-call(s32[1]{0:T(128)} %bitcast.parity_ref, bf16[8,2,40,4096]{3,2,1,0:T(8,128)(2,1)} %bitcast.43, bf16[4096,256]{1,0:T(8,128)(2,1)} %bitcast.49, ...), custom_call_target="tpu_custom_call" | custom-call | tf_op jit(solution)/shard_map/first/pallas_call | solution.py:453
  196.1 5.9 %second.1 = (f32[320,4096]{1,0:T(8,128)S(1)}, bf16[256,4096]{1,0:T(8,128)(2,1)S(1)}, bf16[256,4096]{1,0:T(8,128)(2,1)S(1)}) custom-call(s32[1]{0:T(128)} %bitcast.parity_ref, bf16[8,2,40,4096]{3,2,1,0:T(8,128)(2,1)} %bitcast.44, bf16[4096,256]{1,0:T(8,128)(2,1)S(1)} %get-tuple-element.140.g0, bf16[4096,256]{1,0:T(8,128)(2,1)S(1)} %get-tuple-element.141.u0, ...), custom_call_target="tpu_custom_call" | custom-call | flops 2684354560 | bytes 16777216 | tf_op jit(solution)/shard_map/second/pallas_call | solution.py:463
  202.1 2.9 %collective-permute-done.8.far_ref = bf16[320,512]{1,0:T(8,128)(2,1)S(1)} collective-permute-done((bf16[320,512]{1,0:T(8,128)(2,1)S(1)}, bf16[320,512]{1,0:T(8,128)(2,1)S(1)}, u32[]{:S(2)}, u32[]{:S(2)}) %collective-permute-start.8) | collective-permute-done | bytes 327712 | tf_op jit(solution)/shard_map/ppermute | solution.py:462
  205.0 1.5 down.1
  206.6 37.2 %all_to_all.65.got_ref = bf16[8,40,4096]{2,1,0:T(8,128)(2,1)S(1)} all-to-all(bf16[8,40,4096]{2,1,0:T(8,128)(2,1)S(1)} %bitcast.27), channel_id=1, replica_groups={{0,32,64,96,128,160,192,224},{8,40,72,104,136,168,200,232},{16,48,80,11..., dimensions={0} | all-to-all | bytes 5242880 | tf_op jit(solution)/shard_map/all_to_all | solution.py:30
  244.6 18.0 %all_to_all.66.got_ref = bf16[8,40,512]{2,1,0:T(8,128)(2,1)S(1)} all-to-all(bf16[8,40,512]{2,1,0:T(8,128)(2,1)S(1)} %weigh.1), channel_id=1, replica_groups=mesh['seq'=32,'expert'=8] {'expert'}, dimensions={0} | all-to-all | bytes 655360 | tf_op jit(solution)/shard_map/all_to_all | solution.py:30
  263.1 11.5 %all_to_all.67.got_ref = bf16[8,16,512]{2,1,0:T(8,128)(2,1)S(1)} all-to-all(bf16[8,16,512]{2,1,0:T(8,128)(2,1)S(1)} %bitcast.32), channel_id=1, replica_groups=mesh['seq'=32,'expert'=8] {'expert'}, dimensions={0} | all-to-all | bytes 262144 | tf_op jit(solution)/shard_map/all_to_all | solution.py:30
  (61 shorter events, 6.8 us)
Async XLA Ops:
  6.5 41.5 %collective-permute-start.1 = (bf16[4096,256]{1,0:T(8,128)(2,1)}, bf16[4096,256]{1,0:T(8,128)(2,1)}, u32[]{:S(2)}, u32[]{:S(2)}) collective-permute-start(bf16[4096,256]{1,0:T(8,128)(2,1)} %bitcast.48), channel_id=1, source_target_pairs={{0,8},{8,0},{16,24},{24,16},{32,40},{40,32},{48,56},{56,48},{64,72... | collective-permute-start | bytes 6291464 | tf_op jit(solution)/shard_map/ppermute | solution.py:344
  6.5 41.5 %collective-permute-start.2 = (bf16[4096,256]{1,0:T(8,128)(2,1)}, bf16[4096,256]{1,0:T(8,128)(2,1)}, u32[]{:S(2)}, u32[]{:S(2)}) collective-permute-start(bf16[4096,256]{1,0:T(8,128)(2,1)} %bitcast.50), channel_id=1, source_target_pairs={{0,8},{8,0},{16,24},{24,16},{32,40},{40,32},{48,56},{56,48},{64,72... | collective-permute-start | bytes 6291464 | tf_op jit(solution)/shard_map/ppermute | solution.py:344
  7.0 41.0 %collective-permute-start.3 = (bf16[256,4096]{1,0:T(8,128)(2,1)}, bf16[256,4096]{1,0:T(8,128)(2,1)S(1)}, u32[]{:S(2)}, u32[]{:S(2)}) collective-permute-start(bf16[256,4096]{1,0:T(8,128)(2,1)} %bitcast.45), channel_id=1, source_target_pairs={{0,8},{8,0},{16,24},{24,16},{32,40},{40,32},{48,56},{56,48},{64,72... | collective-permute-start | bytes 6291464 | tf_op jit(solution)/shard_map/ppermute | solution.py:344
  7.8 8.6 %collective-permute-start = (bf16[6,512]{1,0:T(8,128)(2,1)S(1)}, bf16[6,512]{1,0:T(8,128)(2,1)S(1)}, u32[]{:S(2)}, u32[]{:S(2)}) collective-permute-start(bf16[6,512]{1,0:T(8,128)(2,1)S(1)} %slice.22), channel_id=1, source_target_pairs={{0,8},{8,16},{16,24},{24,32},{32,40},{40,48},{48,56},{56,64},{64,7... | collective-permute-start | bytes 18440 | tf_op jit(solution)/shard_map/ppermute | solution.py:348
  12.6 36.2 %copy-start.1 = (bf16[256,512]{1,0:T(8,128)(2,1)S(1)}, bf16[256,512]{1,0:T(8,128)(2,1)}, u32[]{:S(2)}) copy-start(bf16[256,512]{1,0:T(8,128)(2,1)} %dtp_ref.1) | copy-start | bytes 786436
  12.6 36.2 %copy-start.2 = (f32[512,16]{0,1:T(8,128)S(1)}, f32[512,16]{0,1:T(8,128)}, u32[]{:S(2)}) copy-start(f32[512,16]{0,1:T(8,128)} %param.29) | copy-start | bytes 98308
  12.6 36.2 %copy-start.6 = (f32[512]{0:T(512)S(1)}, f32[512]{0:T(512)}, u32[]{:S(2)}) copy-start(f32[512]{0:T(512)} %param.28) | copy-start | bytes 6148
  48.1 2.0 copy-start.9
  48.8 27.7 %copy-start = (bf16[512,4096]{1,0:T(8,128)(2,1)S(1)}, bf16[512,4096]{1,0:T(8,128)(2,1)}, u32[]{:S(2)}) copy-start(bf16[512,4096]{1,0:T(8,128)(2,1)} %outp_ref.1) | copy-start | bytes 12582916
  50.1 26.5 %copy-start.3 = (f32[2,512,16]{1,2,0:T(8,128)S(1)}, f32[2,512,16]{1,2,0:T(8,128)}, u32[]{:S(2)}) copy-start(f32[2,512,16]{1,2,0:T(8,128)} %param.31) | copy-start | bytes 196612
  50.1 26.5 %copy-start.7 = (f32[512]{0:T(512)S(1)}, f32[512]{0:T(512)}, u32[]{:S(2)}) copy-start(f32[512]{0:T(512)} %param.30) | copy-start | bytes 6148
  80.9 3.8 %copy-start.8 = (bf16[1,256,4096]{2,1,0:T(8,128)(2,1)S(1)}, bf16[1,256,4096]{2,1,0:T(8,128)(2,1)}, u32[]{:S(2)}) copy-start(bf16[1,256,4096]{2,1,0:T(8,128)(2,1)} %param.40) | copy-start | bytes 6291460
  80.9 33.3 %all-to-all-start.3 = ((bf16[8,128,512]{2,1,0:T(8,128)(2,1)}), bf16[8,128,512]{2,1,0:T(8,128)(2,1)S(1)}, u32[]{:S(2)}, u32[]{:S(2)}) async-start(bf16[8,128,512]{2,1,0:T(8,128)(2,1)} %scan.1), calls=%async_computation.3 | async-start | bytes 2097152 | tf_op jit(solution)/shard_map/all_to_all | solution.py:30
  84.7 3.0 %copy-start.13 = (bf16[4096]{0:T(1024)(128)(2,1)S(1)}, bf16[4096]{0:T(1024)(128)(2,1)}, u32[]{:S(2)}) copy-start(bf16[4096]{0:T(1024)(128)(2,1)} %param.36) | copy-start | bytes 24580
  84.7 3.0 %copy-start.12 = (bf16[4,4096]{1,0:T(4,128)(2,1)S(1)}, bf16[4,4096]{1,0:T(4,128)(2,1)}, u32[]{:S(2)}) copy-start(bf16[4,4096]{1,0:T(4,128)(2,1)} %param.35) | copy-start | bytes 98308
  84.7 3.0 %copy-start.14 = (s32[64,2,2]{0,2,1:T(2,128)S(1)}, s32[64,2,2]{0,2,1:T(2,128)}, u32[]{:S(2)}) copy-start(s32[64,2,2]{0,2,1:T(2,128)} %param.41) | copy-start | bytes 3076
  84.7 3.2 %copy-start.5 = (bf16[4096]{0:T(1024)(128)(2,1)S(1)}, bf16[4096]{0:T(1024)(128)(2,1)}, u32[]{:S(2)}) copy-start(bf16[4096]{0:T(1024)(128)(2,1)} %param.34) | copy-start | bytes 24580
  84.7 104.8 %all-gather.2.cloned.1.call-start = ((), (), s32[]{:S(2)}) async-start(), calls=%async_computation.9 | async-start | bytes 5570560 | tf_op jit(solution)/shard_map/all_gather | solution.py:432
  86.2 47.3 %copy-start.4 = (bf16[4096,8]{0,1:T(8,128)(2,1)S(1)}, bf16[4096,8]{0,1:T(8,128)(2,1)}, u32[]{:S(2)}) copy-start(bf16[4096,8]{0,1:T(8,128)(2,1)} %param.37) | copy-start | bytes 196612
  86.2 45.9 %collective-permute-start.4 = (bf16[128,4096]{1,0:T(8,128)(2,1)}, bf16[128,4096]{1,0:T(8,128)(2,1)S(1)}, u32[]{:S(2)}, u32[]{:S(2)}) collective-permute-start(bf16[128,4096]{1,0:T(8,128)(2,1)} %get-tuple-element.162), channel_id=1, source_target_pairs={{0,16},{8,24},{16,0},{24,8},{32,48},{40,56},{48,32},{56,40},{64,80... | collective-permute-start | bytes 3145736 | tf_op jit(solution)/shard_map/ppermute | solution.py:397
  132.2 63.1 %copy-start.10 = (bf16[128,4096]{1,0:T(8,128)(2,1)}, bf16[128,4096]{1,0:T(8,128)(2,1)S(1)}, u32[]{:S(2)}) copy-start(bf16[128,4096]{1,0:T(8,128)(2,1)S(1)} %collective-permute-done.4.refs_2_) | copy-start | bytes 3145732
  132.2 30.0 %collective-permute-start.5 = (bf16[128,4096]{1,0:T(8,128)(2,1)}, bf16[128,4096]{1,0:T(8,128)(2,1)S(1)}, u32[]{:S(2)}, u32[]{:S(2)}) collective-permute-start(bf16[128,4096]{1,0:T(8,128)(2,1)} %get-tuple-element.161), channel_id=1, source_target_pairs={{0,16},{8,24},{16,0},{24,8},{32,48},{40,56},{48,32},{56,40},{64,80... | collective-permute-start | bytes 3145736 | tf_op jit(solution)/shard_map/ppermute | solution.py:397
  134.9 27.4 %all-to-all-start.5 = ((f32[8,16,512]{2,1,0:T(8,128)}), f32[8,16,512]{2,1,0:T(8,128)S(1)}, u32[]{:S(2)}, u32[]{:S(2)}) async-start(f32[8,16,512]{2,1,0:T(8,128)} %bitcast.18), calls=%async_computation.5 | async-start | bytes 524288 | tf_op jit(solution)/shard_map/all_to_all | solution.py:30
  138.3 24.0 %collective-permute-start.6 = (bf16[128,4096]{1,0:T(8,128)(2,1)S(1)}, bf16[128,4096]{1,0:T(8,128)(2,1)}, u32[]{:S(2)}, u32[]{:S(2)}) collective-permute-start(bf16[128,4096]{1,0:T(8,128)(2,1)S(1)} %collective-permute-done.4.refs_2_), channel_id=1, source_target_pairs={{0,8},{8,0},{16,24},{24,16},{32,40},{40,32},{48,56},{56,48},{64,72... | collective-permute-start | bytes 3145736 | tf_op jit(solution)/shard_map/ppermute | solution.py:431
  162.2 33.1 %copy-start.11 = (bf16[128,4096]{1,0:T(8,128)(2,1)}, bf16[128,4096]{1,0:T(8,128)(2,1)S(1)}, u32[]{:S(2)}) copy-start(bf16[128,4096]{1,0:T(8,128)(2,1)S(1)} %collective-permute-done.5.refs_3_) | copy-start | bytes 3145732
  162.2 2.8 collective-permute-start.7
  195.3 9.7 %collective-permute-start.8 = (bf16[320,512]{1,0:T(8,128)(2,1)S(1)}, bf16[320,512]{1,0:T(8,128)(2,1)S(1)}, u32[]{:S(2)}, u32[]{:S(2)}) collective-permute-start(bf16[320,512]{1,0:T(8,128)(2,1)S(1)} %get-tuple-element.148), channel_id=1, source_target_pairs={{0,16},{8,24},{16,0},{24,8},{32,48},{40,56},{48,32},{56,40},{64,80... | collective-permute-start | bytes 983048 | tf_op jit(solution)/shard_map/ppermute | solution.py:462
Sparse Core Ops, SparseCore 0:
  132.3 57.1 all-gather.1

commit v8 on v7

--- a/solution.py
+++ b/solution.py
@@ -448,7 +448,7 @@
     dma = pltpu.SemaphoreType.DMA
     parity = ((place // 2) % 2)[None]
     pieces = pltpu.with_memory_space_constraint(pieces, pltpu.HBM)
-    parts = 4
+    parts = 8
     held_rows = [pltpu.VMEM((pairs, capacity, d_model), BF16), dma((parts,))]
     theirs, *ups = pl.pallas_call(
         first_kernel,

time: 283 us -> 282 us (level)
  no operation moved by 1% of the time
where the time goes in v8:
time: 282 us
  blocking collectives  140 us (50%)
  waiting for transfers between devices  80.6 us (29%)
  Pallas kernels  26.4 us (9%)
  starting transfers between devices  13.8 us (5%)
  between operations  13.8 us (5%)
  local copies, waits for them, and re-layouts  7.46 us (3%)
    all_to_all x7, blocking collectives, exchanged(): lax.all_to_all(blocks, axis, 0, 0, tiled=True, axis_index_groups=groups)  140 us
    all_to_all x2, waiting for transfers between devices, exchanged(): lax.all_to_all(blocks, axis, 0, 0, tiled=True, axis_index_groups=groups)  24.8 us
    all_gather x1, waiting for transfers between devices, shards(): lax.all_gather(normed, 'seq', axis=0, tiled=True, axis_index_groups=same_...  24.5 us
    ppermute x2, waiting for transfers between devices, shards(): lax.ppermute(down_w[k * part:(k + 1) * part], 'seq', across)  23.8 us
    all_to_all x2, starting transfers between devices, exchanged(): lax.all_to_all(blocks, axis, 0, 0, tiled=True, axis_index_groups=groups)  7.12 us
    pallas_call x1, Pallas kernels, shards(): pl.pallas_call(second_kernel, out_shape=(pltpu.VMEM((half, d_model), F32)...  5.98 us
  transfers between devices with their start and end apart: 12, of which 6 were waited for; matrix products, arithmetic and copies ran while one was open for 2% of the time, Pallas kernels for 4%

profile of v8, /device:TPU:2, one launch (start us, length us, event | category | flops | bytes accessed | tf_op | source)
XLA Modules:
  0.0 281.7 jit_solution(11724109133978665221)
XLA Ops:
  7.8 2.4 collective-permute-start
  10.3 1.0 reshape.49.x_ref
  12.6 1.0 reshape.52.own_ref
  13.6 1.0 reshape.51.gate_ref
  14.6 1.7 collective-permute-done.got_ref
  16.3 1.3 conv.1
  17.6 19.3 %all_to_all.61.got_ref = f32[8,16,288]{2,1,0:T(8,128)S(1)} all-to-all(f32[8,16,288]{2,1,0:T(8,128)S(1)} %bitcast.33), channel_id=1, replica_groups=mesh['seq'=32,'expert'=8] {'expert'}, dimensions={0} | all-to-all | bytes 294912 | tf_op jit(solution)/shard_map/all_to_all | solution.py:30
  37.0 11.1 %all_to_all.62 = bf16[8,16,384]{2,1,0:T(8,128)(2,1)S(1)} all-to-all(bf16[8,16,384]{2,1,0:T(8,128)(2,1)S(1)} %sum.1), channel_id=1, replica_groups=mesh['seq'=32,'expert'=8] {'expert'}, dimensions={0} | all-to-all | bytes 196608 | tf_op jit(solution)/shard_map/all_to_all | solution.py:30
  48.8 1.2 local.1
  50.2 26.3 %all_to_all.63.all_ref = bf16[32,40,512]{2,1,0:T(8,128)(2,1)S(1)} all-to-all(bf16[32,40,512]{2,1,0:T(8,128)(2,1)S(1)} %broadcast_in_dim.36), channel_id=1, replica_groups=mesh['seq'=32,'expert'=8] {'seq'}, dimensions={0} | all-to-all | bytes 2621440 | tf_op jit(solution)/shard_map/all_to_all | solution.py:30
  76.6 4.4 %scan.1 = bf16[8,128,512]{2,1,0:T(8,128)(2,1)} custom-call(s32[2]{0:T(128)S(1)} %pad_add_fusion.ids_ref, bf16[32,40,512]{2,1,0:T(8,128)(2,1)S(1)} %all_to_all.63.all_ref, f32[2,16,512]{2,1,0:T(8,128)S(1)} %bitcast.37, f32[128,512]{1,0:T(8,128)S(1)} %get-tuple-element.113.step_ref, f32[128,512]{1,0:T(8,128)S(1)} %get-tuple-element.114.act_ref, ...), custom_call_target="tpu_custom_call" | custom-call | tf_op jit(solution)/shard_map/scan/pallas_call | solution.py:398
  80.9 3.7 %all-to-all-start.3 = ((bf16[8,128,512]{2,1,0:T(8,128)(2,1)}), bf16[8,128,512]{2,1,0:T(8,128)(2,1)S(1)}, u32[]{:S(2)}, u32[]{:S(2)}) async-start(bf16[8,128,512]{2,1,0:T(8,128)(2,1)} %scan.1), calls=%async_computation.3 | async-start | bytes 2097152 | tf_op jit(solution)/shard_map/all_to_all | solution.py:30
  84.8 1.5 fusion
  86.2 1.4 collective-permute-start.4
  87.9 1.5 clean.1
  89.4 24.8 %all-to-all-done.3.mixed_ref = bf16[8,128,512]{2,1,0:T(8,128)(2,1)S(1)} async-done(((bf16[8,128,512]{2,1,0:T(8,128)(2,1)}), bf16[8,128,512]{2,1,0:T(8,128)(2,1)S(1)}, u32[]{:S(2)}, u32[]{:S(2)}) %all-to-all-start.3) | async-done | bytes 1048608 | tf_op jit(solution)/shard_map/all_to_all | solution.py:30
  114.3 0.9 dispatch.1
  115.1 16.2 %all_to_all.64.got_ref = bf16[8,40,512]{2,1,0:T(8,128)(2,1)S(1)} all-to-all(bf16[8,40,512]{2,1,0:T(8,128)(2,1)S(1)} %get-tuple-element.125), channel_id=1, replica_groups=mesh['seq'=32,'expert'=8] {'expert'}, dimensions={0} | all-to-all | bytes 655360 | tf_op jit(solution)/shard_map/all_to_all | solution.py:30
  131.3 0.9 normed.1.x_ref
  132.2 1.4 collective-permute-start.5
  133.5 1.3 share.1.share_ref
  134.9 3.4 %all-to-all-start.5 = ((f32[8,16,512]{2,1,0:T(8,128)}), f32[8,16,512]{2,1,0:T(8,128)S(1)}, u32[]{:S(2)}, u32[]{:S(2)}) async-start(f32[8,16,512]{2,1,0:T(8,128)} %bitcast.18), calls=%async_computation.5 | async-start | bytes 524288 | tf_op jit(solution)/shard_map/all_to_all | solution.py:30
  138.4 23.8 %collective-permute-done.5.refs_3_ = bf16[128,4096]{1,0:T(8,128)(2,1)S(1)} collective-permute-done((bf16[128,4096]{1,0:T(8,128)(2,1)}, bf16[128,4096]{1,0:T(8,128)(2,1)S(1)}, u32[]{:S(2)}, u32[]{:S(2)}) %collective-permute-start.5) | collective-permute-done | bytes 1048608 | tf_op jit(solution)/shard_map/ppermute | solution.py:397
  162.3 2.8 collective-permute-done.7.refs_5_
  165.0 24.5 %all-gather.2.cloned.1.call-done = bf16[640,4096]{1,0:T(8,128)(2,1)} async-done(((bf16[40,4096]{1,0:T(8,128)(2,1)}), bf16[640,4096]{1,0:T(8,128)(2,1)}) %all-gather.2.cloned.1.call-update) | async-done | bytes 5242896 | tf_op jit(solution)/shard_map/all_gather | solution.py:432
  189.5 5.3 %first.1 = (bf16[320,512]{1,0:T(8,128)(2,1)S(1)}, bf16[4096,256]{1,0:T(8,128)(2,1)S(1)}, bf16[4096,256]{1,0:T(8,128)(2,1)S(1)}, bf16[4096,256]{1,0:T(8,128)(2,1)S(1)}, bf16[4096,256]{1,0:T(8,128)(2,1)S(1)}) custom-call(s32[1]{0:T(128)} %bitcast.parity_ref, bf16[8,2,40,4096]{3,2,1,0:T(8,128)(2,1)} %bitcast.43, bf16[4096,256]{1,0:T(8,128)(2,1)} %bitcast.49, ...), custom_call_target="tpu_custom_call" | custom-call | tf_op jit(solution)/shard_map/first/pallas_call | solution.py:453
  195.7 6.0 %second.1 = (f32[320,4096]{1,0:T(8,128)S(1)}, bf16[256,4096]{1,0:T(8,128)(2,1)S(1)}, bf16[256,4096]{1,0:T(8,128)(2,1)S(1)}) custom-call(s32[1]{0:T(128)} %bitcast.parity_ref, bf16[8,2,40,4096]{3,2,1,0:T(8,128)(2,1)} %bitcast.44, bf16[4096,256]{1,0:T(8,128)(2,1)S(1)} %get-tuple-element.140.g0, bf16[4096,256]{1,0:T(8,128)(2,1)S(1)} %get-tuple-element.141.u0, ...), custom_call_target="tpu_custom_call" | custom-call | flops 2684354560 | bytes 16777216 | tf_op jit(solution)/shard_map/second/pallas_call | solution.py:463
  201.7 2.9 %collective-permute-done.8.far_ref = bf16[320,512]{1,0:T(8,128)(2,1)S(1)} collective-permute-done((bf16[320,512]{1,0:T(8,128)(2,1)S(1)}, bf16[320,512]{1,0:T(8,128)(2,1)S(1)}, u32[]{:S(2)}, u32[]{:S(2)}) %collective-permute-start.8) | collective-permute-done | bytes 327712 | tf_op jit(solution)/shard_map/ppermute | solution.py:462
  204.6 1.5 down.1
  206.2 37.2 %all_to_all.65.got_ref = bf16[8,40,4096]{2,1,0:T(8,128)(2,1)S(1)} all-to-all(bf16[8,40,4096]{2,1,0:T(8,128)(2,1)S(1)} %bitcast.27), channel_id=1, replica_groups={{0,32,64,96,128,160,192,224},{8,40,72,104,136,168,200,232},{16,48,80,11..., dimensions={0} | all-to-all | bytes 5242880 | tf_op jit(solution)/shard_map/all_to_all | solution.py:30
  244.2 18.0 %all_to_all.66.got_ref = bf16[8,40,512]{2,1,0:T(8,128)(2,1)S(1)} all-to-all(bf16[8,40,512]{2,1,0:T(8,128)(2,1)S(1)} %weigh.1), channel_id=1, replica_groups=mesh['seq'=32,'expert'=8] {'expert'}, dimensions={0} | all-to-all | bytes 655360 | tf_op jit(solution)/shard_map/all_to_all | solution.py:30
  262.7 11.5 %all_to_all.67.got_ref = bf16[8,16,512]{2,1,0:T(8,128)(2,1)S(1)} all-to-all(bf16[8,16,512]{2,1,0:T(8,128)(2,1)S(1)} %bitcast.32), channel_id=1, replica_groups=mesh['seq'=32,'expert'=8] {'expert'}, dimensions={0} | all-to-all | bytes 262144 | tf_op jit(solution)/shard_map/all_to_all | solution.py:30
  (61 shorter events, 6.8 us)
Async XLA Ops:
  6.5 41.5 %collective-permute-start.1 = (bf16[4096,256]{1,0:T(8,128)(2,1)}, bf16[4096,256]{1,0:T(8,128)(2,1)}, u32[]{:S(2)}, u32[]{:S(2)}) collective-permute-start(bf16[4096,256]{1,0:T(8,128)(2,1)} %bitcast.48), channel_id=1, source_target_pairs={{0,8},{8,0},{16,24},{24,16},{32,40},{40,32},{48,56},{56,48},{64,72... | collective-permute-start | bytes 6291464 | tf_op jit(solution)/shard_map/ppermute | solution.py:344
  6.5 41.5 %collective-permute-start.2 = (bf16[4096,256]{1,0:T(8,128)(2,1)}, bf16[4096,256]{1,0:T(8,128)(2,1)}, u32[]{:S(2)}, u32[]{:S(2)}) collective-permute-start(bf16[4096,256]{1,0:T(8,128)(2,1)} %bitcast.50), channel_id=1, source_target_pairs={{0,8},{8,0},{16,24},{24,16},{32,40},{40,32},{48,56},{56,48},{64,72... | collective-permute-start | bytes 6291464 | tf_op jit(solution)/shard_map/ppermute | solution.py:344
  7.0 41.0 %collective-permute-start.3 = (bf16[256,4096]{1,0:T(8,128)(2,1)}, bf16[256,4096]{1,0:T(8,128)(2,1)S(1)}, u32[]{:S(2)}, u32[]{:S(2)}) collective-permute-start(bf16[256,4096]{1,0:T(8,128)(2,1)} %bitcast.45), channel_id=1, source_target_pairs={{0,8},{8,0},{16,24},{24,16},{32,40},{40,32},{48,56},{56,48},{64,72... | collective-permute-start | bytes 6291464 | tf_op jit(solution)/shard_map/ppermute | solution.py:344
  7.8 8.6 %collective-permute-start = (bf16[6,512]{1,0:T(8,128)(2,1)S(1)}, bf16[6,512]{1,0:T(8,128)(2,1)S(1)}, u32[]{:S(2)}, u32[]{:S(2)}) collective-permute-start(bf16[6,512]{1,0:T(8,128)(2,1)S(1)} %slice.22), channel_id=1, source_target_pairs={{0,8},{8,16},{16,24},{24,32},{32,40},{40,48},{48,56},{56,64},{64,7... | collective-permute-start | bytes 18440 | tf_op jit(solution)/shard_map/ppermute | solution.py:348
  12.6 36.2 %copy-start.1 = (bf16[256,512]{1,0:T(8,128)(2,1)S(1)}, bf16[256,512]{1,0:T(8,128)(2,1)}, u32[]{:S(2)}) copy-start(bf16[256,512]{1,0:T(8,128)(2,1)} %dtp_ref.1) | copy-start | bytes 786436
  12.6 36.2 %copy-start.2 = (f32[512,16]{0,1:T(8,128)S(1)}, f32[512,16]{0,1:T(8,128)}, u32[]{:S(2)}) copy-start(f32[512,16]{0,1:T(8,128)} %param.29) | copy-start | bytes 98308
  12.6 36.2 %copy-start.6 = (f32[512]{0:T(512)S(1)}, f32[512]{0:T(512)}, u32[]{:S(2)}) copy-start(f32[512]{0:T(512)} %param.28) | copy-start | bytes 6148
  48.1 2.0 copy-start.9
  48.8 27.7 %copy-start = (bf16[512,4096]{1,0:T(8,128)(2,1)S(1)}, bf16[512,4096]{1,0:T(8,128)(2,1)}, u32[]{:S(2)}) copy-start(bf16[512,4096]{1,0:T(8,128)(2,1)} %outp_ref.1) | copy-start | bytes 12582916
  50.1 26.5 %copy-start.3 = (f32[2,512,16]{1,2,0:T(8,128)S(1)}, f32[2,512,16]{1,2,0:T(8,128)}, u32[]{:S(2)}) copy-start(f32[2,512,16]{1,2,0:T(8,128)} %param.31) | copy-start | bytes 196612
  50.1 26.5 %copy-start.7 = (f32[512]{0:T(512)S(1)}, f32[512]{0:T(512)}, u32[]{:S(2)}) copy-start(f32[512]{0:T(512)} %param.30) | copy-start | bytes 6148
  80.9 3.8 %copy-start.8 = (bf16[1,256,4096]{2,1,0:T(8,128)(2,1)S(1)}, bf16[1,256,4096]{2,1,0:T(8,128)(2,1)}, u32[]{:S(2)}) copy-start(bf16[1,256,4096]{2,1,0:T(8,128)(2,1)} %param.40) | copy-start | bytes 6291460
  80.9 33.3 %all-to-all-start.3 = ((bf16[8,128,512]{2,1,0:T(8,128)(2,1)}), bf16[8,128,512]{2,1,0:T(8,128)(2,1)S(1)}, u32[]{:S(2)}, u32[]{:S(2)}) async-start(bf16[8,128,512]{2,1,0:T(8,128)(2,1)} %scan.1), calls=%async_computation.3 | async-start | bytes 2097152 | tf_op jit(solution)/shard_map/all_to_all | solution.py:30
  84.7 3.0 %copy-start.13 = (bf16[4096]{0:T(1024)(128)(2,1)S(1)}, bf16[4096]{0:T(1024)(128)(2,1)}, u32[]{:S(2)}) copy-start(bf16[4096]{0:T(1024)(128)(2,1)} %param.36) | copy-start | bytes 24580
  84.7 3.0 %copy-start.12 = (bf16[4,4096]{1,0:T(4,128)(2,1)S(1)}, bf16[4,4096]{1,0:T(4,128)(2,1)}, u32[]{:S(2)}) copy-start(bf16[4,4096]{1,0:T(4,128)(2,1)} %param.35) | copy-start | bytes 98308
  84.7 3.0 %copy-start.14 = (s32[64,2,2]{0,2,1:T(2,128)S(1)}, s32[64,2,2]{0,2,1:T(2,128)}, u32[]{:S(2)}) copy-start(s32[64,2,2]{0,2,1:T(2,128)} %param.41) | copy-start | bytes 3076
  84.7 3.2 %copy-start.5 = (bf16[4096]{0:T(1024)(128)(2,1)S(1)}, bf16[4096]{0:T(1024)(128)(2,1)}, u32[]{:S(2)}) copy-start(bf16[4096]{0:T(1024)(128)(2,1)} %param.34) | copy-start | bytes 24580
  84.7 104.8 %all-gather.2.cloned.1.call-start = ((), (), s32[]{:S(2)}) async-start(), calls=%async_computation.9 | async-start | bytes 5570560 | tf_op jit(solution)/shard_map/all_gather | solution.py:432
  86.2 47.3 %copy-start.4 = (bf16[4096,8]{0,1:T(8,128)(2,1)S(1)}, bf16[4096,8]{0,1:T(8,128)(2,1)}, u32[]{:S(2)}) copy-start(bf16[4096,8]{0,1:T(8,128)(2,1)} %param.37) | copy-start | bytes 196612
  86.2 45.9 %collective-permute-start.4 = (bf16[128,4096]{1,0:T(8,128)(2,1)}, bf16[128,4096]{1,0:T(8,128)(2,1)S(1)}, u32[]{:S(2)}, u32[]{:S(2)}) collective-permute-start(bf16[128,4096]{1,0:T(8,128)(2,1)} %get-tuple-element.162), channel_id=1, source_target_pairs={{0,16},{8,24},{16,0},{24,8},{32,48},{40,56},{48,32},{56,40},{64,80... | collective-permute-start | bytes 3145736 | tf_op jit(solution)/shard_map/ppermute | solution.py:397
  132.2 62.7 %copy-start.10 = (bf16[128,4096]{1,0:T(8,128)(2,1)}, bf16[128,4096]{1,0:T(8,128)(2,1)S(1)}, u32[]{:S(2)}) copy-start(bf16[128,4096]{1,0:T(8,128)(2,1)S(1)} %collective-permute-done.4.refs_2_) | copy-start | bytes 3145732
  132.2 30.0 %collective-permute-start.5 = (bf16[128,4096]{1,0:T(8,128)(2,1)}, bf16[128,4096]{1,0:T(8,128)(2,1)S(1)}, u32[]{:S(2)}, u32[]{:S(2)}) collective-permute-start(bf16[128,4096]{1,0:T(8,128)(2,1)} %get-tuple-element.161), channel_id=1, source_target_pairs={{0,16},{8,24},{16,0},{24,8},{32,48},{40,56},{48,32},{56,40},{64,80... | collective-permute-start | bytes 3145736 | tf_op jit(solution)/shard_map/ppermute | solution.py:397
  134.9 27.4 %all-to-all-start.5 = ((f32[8,16,512]{2,1,0:T(8,128)}), f32[8,16,512]{2,1,0:T(8,128)S(1)}, u32[]{:S(2)}, u32[]{:S(2)}) async-start(f32[8,16,512]{2,1,0:T(8,128)} %bitcast.18), calls=%async_computation.5 | async-start | bytes 524288 | tf_op jit(solution)/shard_map/all_to_all | solution.py:30
  138.3 24.0 %collective-permute-start.6 = (bf16[128,4096]{1,0:T(8,128)(2,1)S(1)}, bf16[128,4096]{1,0:T(8,128)(2,1)}, u32[]{:S(2)}, u32[]{:S(2)}) collective-permute-start(bf16[128,4096]{1,0:T(8,128)(2,1)S(1)} %collective-permute-done.4.refs_2_), channel_id=1, source_target_pairs={{0,8},{8,0},{16,24},{24,16},{32,40},{40,32},{48,56},{56,48},{64,72... | collective-permute-start | bytes 3145736 | tf_op jit(solution)/shard_map/ppermute | solution.py:431
  162.2 32.7 %copy-start.11 = (bf16[128,4096]{1,0:T(8,128)(2,1)}, bf16[128,4096]{1,0:T(8,128)(2,1)S(1)}, u32[]{:S(2)}) copy-start(bf16[128,4096]{1,0:T(8,128)(2,1)S(1)} %collective-permute-done.5.refs_3_) | copy-start | bytes 3145732
  162.2 2.8 collective-permute-start.7
  194.9 9.7 %collective-permute-start.8 = (bf16[320,512]{1,0:T(8,128)(2,1)S(1)}, bf16[320,512]{1,0:T(8,128)(2,1)S(1)}, u32[]{:S(2)}, u32[]{:S(2)}) collective-permute-start(bf16[320,512]{1,0:T(8,128)(2,1)S(1)} %get-tuple-element.148), channel_id=1, source_target_pairs={{0,16},{8,24},{16,0},{24,8},{32,48},{40,56},{48,32},{56,40},{64,80... | collective-permute-start | bytes 983048 | tf_op jit(solution)/shard_map/ppermute | solution.py:462
Sparse Core Ops, SparseCore 0:
  132.3 57.1 all-gather.1
